TPU v7x, 32 devices: a whole 2x2x4 slice. The times are simulated.
32 devices in a mesh: dp: 16 (over z, y, x), head: 2 (over core).
Axes of the slice: x: 2, y: 2, z: 4, core: 2. Of those that a mesh axis runs over, the one named last changes fastest.
Arguments:
- inputs: bfloat16 [24576, 768], P(('dp', 'head')), may hold values from -6 to 6
- qkv_weight: bfloat16 [768, 3, 768], P('dp', None, 'head'), may hold values from -0.21875 to 0.21875
- qv_bias: float32 [2, 768], P(None, 'head'), may hold values from -3 to 3
- out_weight: bfloat16 [768, 768], P('dp', 'head'), may hold values from -2.5 to 2.5
- out_bias: float32 [768], replicated, may hold values from -1.75 to 1.75
- first_gain: float32 [768], replicated, may hold values from 0.5 to 1.5
- first_shift: float32 [768], replicated, may hold values from -1.75 to 1.75
- up_weight: bfloat16 [768, 3072], P('dp', 'head'), may hold values from -0.21875 to 0.21875
- up_bias: float32 [3072], P('head'), may hold values from -3 to 3
- down_weight: bfloat16 [768, 3072], P('dp', 'head'), may hold values from -0.15625 to 0.15625
- down_bias: float32 [768], replicated, may hold values from -1.75 to 1.75
- second_gain: float32 [768], replicated, may hold values from 0.5 to 1.5
- second_shift: float32 [768], replicated, may hold values from -1.75 to 1.75
- item_lengths: int32 [16, 2], P('dp'), may hold values from 0 to 1536, as said below
- random_blocks: int32 [16, 12, 24, 3], P('dp', 'head'), may hold values from 0 to 22, as said below
- out_grad: bfloat16 [24576, 768], P(('dp', 'head')), may hold values from -16 to 16
Outputs:
- layer_out: bfloat16 [24576, 768], P(('dp', 'head'))
- input_grad: bfloat16 [24576, 768], P(('dp', 'head'))
- grad_qkv: float32 [768, 3, 768], P('dp', None, 'head')
- grad_qv_bias: float32 [2, 768], P(None, 'head')
- grad_out: float32 [768, 768], P('dp', 'head')
- grad_out_bias: float32 [768], replicated
- grad_first_gain: float32 [768], replicated
- grad_first_shift: float32 [768], replicated
- grad_up: float32 [768, 3072], P('dp', 'head')
- grad_up_bias: float32 [3072], P('head')
- grad_down: float32 [768, 3072], P('dp', 'head')
- grad_down_bias: float32 [768], replicated
- grad_second_gain: float32 [768], replicated
- grad_second_shift: float32 [768], replicated
Inputs may be any that keep to these rules, and one draw needn't show every extreme that they name: `item_lengths`: each row lists a data group's items in order, then zeros. A group holds either one item of 1536 tokens (filling all 1536 rows; 1 group are such) or one to 2 items of 768 tokens; some group holds 2 items. `random_blocks`: for head h and block b of a group, where b is block r of an item of n blocks with 0 < r < n - 1: three different block numbers of that item, none of them 0, n - 1, r - 1, r or r + 1. Elsewhere 0.
All inputs are finite; a program needn't handle non-finite values.
Results may differ from a plain program's by a relative error of at most 0.019.
Values may be sent and summed in bfloat16 or wider, within the bound.
No kernel may reach another device: no remote copies, remote signals or barrier semaphores. Data moves between devices by JAX's collectives and lax.ppermute only.
A program may use at most 256 MiB of HBM per device.

v0:
```python
import functools

import jax
import jax.numpy as jnp
import numpy as np
from jax import lax
from jax.experimental import pallas as pl
from jax.experimental.pallas import tpu as pltpu
from jax.sharding import Mesh
from jax.sharding import PartitionSpec as P

BLK = 64


norm_eps = 1e-06
negative = -1e30


def norm_forward(values, gain, shift):
    centered = values - jnp.mean(values, axis=-1, keepdims=True)
    inverse = lax.rsqrt(jnp.mean(centered * centered, axis=-1, keepdims=True) + norm_eps)
    normed = centered * inverse
    return (normed * gain + shift, normed, inverse)


def dot_nt(a, b):
    return lax.dot_general(a, b, (((1,), (1,)), ((), ())), preferred_element_type=jnp.float32)


def dot_nn(a, b):
    return lax.dot_general(a, b, (((1,), (0,)), ((), ())), preferred_element_type=jnp.float32)


def dot_tn(a, b):
    return lax.dot_general(a, b, (((0,), (0,)), ((), ())), preferred_element_type=jnp.float32)


PAIR = 2 * BLK


def even_lanes(rows):
    return lax.broadcasted_iota(jnp.int32, (rows, PAIR), 1) < BLK


def stacked(values):
    zero = jnp.zeros_like(values)
    even = even_lanes(BLK)
    return jnp.concatenate([jnp.where(even, values, zero), jnp.where(even, zero, values)], axis=0)


def unstacked(values):
    return jnp.where(even_lanes(BLK), values[:BLK], values[BLK:])


class Layout:
    def __init__(self, len_ref, rb_ref, blocks, position):
        self.len_ref, self.rb_ref, self.blocks = len_ref, rb_ref, blocks
        self.half = blocks // 2
        self.rand = rb_ref.shape[-1]
        self.shift = position * self.half

    def moved(self, index):
        at = index + self.shift
        return jnp.where(at >= self.blocks, at - self.blocks, at)

    def spot(self, index):
        return pl.ds(pl.multiple_of(self.moved(index) * BLK, BLK), BLK)

    def part(self, index):
        return pl.ds(pl.multiple_of(self.moved(index) * BLK, BLK), self.half * BLK)

    def counts(self):
        self.count0 = lax.div(self.len_ref[0, 0], BLK)
        self.count1 = lax.div(self.len_ref[0, 1], BLK)
        self.second = jnp.where(self.count1 > 0, 1, 0)
        self.inner = self.blocks - 2 - 2 * self.second

    def locate(self, i):
        in0 = i < self.count0 - 2
        self.b = b = jnp.where(in0, i + 1, i + 2 + self.second)
        self.live = live = b < self.count0 + self.count1
        self.first = first = jnp.where(in0, 0, jnp.where(live, self.count0, b))
        items = jnp.where(in0, self.count0, jnp.where(live, self.count1, 1))
        rel = b - first
        last = items - 1
        zero, neg = jnp.float32(0.0), jnp.float32(negative)
        self.fixed = [
            first,
            first + last,
            jnp.where(live, b - 1, b),
            jnp.where(live, b + 1, b),
            b,
        ]
        self.low_bias = jnp.where(live & (rel == 1), neg, zero)
        self.high_bias = jnp.where(live & (rel + 1 == last), neg, zero)
        return self

    def ends(self, item):
        first = jnp.where(item == 0, 0, self.count0)
        count = jnp.where(item == 0, self.count0, self.count1)
        return first, first + count - 1, lax.div(count, self.half)

    def chosen(self, head):
        return [
            jnp.where(self.live, self.first + self.rb_ref[0, head, self.b, k], self.b)
            for k in range(self.rand)
        ]


def gathered(ref, layout, column, picked):
    even = even_lanes(BLK)

    def rows(index):
        return ref[layout.spot(index), column : column + PAIR]

    return jnp.concatenate(
        [rows(i) for i in layout.fixed]
        + [jnp.where(even, rows(i), rows(j)) for i, j in zip(*picked)],
        axis=0,
    )


ROWS = 32


def soft_rows(held):
    probs, inverse = [], []
    for row in range(0, held.shape[0], ROWS):
        scores = held[row : row + ROWS, :]
        expo = jnp.exp(scores - jnp.max(scores, axis=1, keepdims=True))
        inverse.append(1.0 / jnp.sum(expo, axis=1, keepdims=True))
        probs.append(expo.astype(jnp.bfloat16))
    return jnp.concatenate(probs, axis=0), jnp.concatenate(inverse, axis=0)


def attn_fwd_kernel(pairs, position, len_ref, rb_ref, tri_ref, out_ref, wide, *held):
    blocks = tri_ref.shape[0] // BLK
    scale = jnp.bfloat16(BLK**-0.5)
    layout = Layout(len_ref, rb_ref, blocks, position())
    layout.counts()

    def query_of(p, b):
        at = layout.spot(b)
        return stacked(tri_ref[at, p * 3 * PAIR : p * 3 * PAIR + PAIR]) * scale

    def put(p, b, mixed):
        at = layout.spot(b)
        out_ref[at, p * PAIR : (p + 1) * PAIR] = unstacked(mixed).astype(jnp.bfloat16)

    def sparse_scores(i, held):
        at = layout.locate(i)
        lane = lax.broadcasted_iota(jnp.int32, (1, PAIR), 1) < BLK
        bias_row = jnp.where(lane, at.low_bias, at.high_bias)
        for n, p in enumerate(pairs):
            picked = [at.chosen(2 * p), at.chosen(2 * p + 1)]
            keys = gathered(tri_ref, at, (3 * p + 1) * PAIR, picked)
            scores = dot_nt(query_of(p, at.b), keys)
            held[n][...] = jnp.concatenate(
                [scores[:, :PAIR], scores[:, PAIR : 2 * PAIR] + bias_row, scores[:, 2 * PAIR :]],
                axis=1,
            )

    def sparse_mix(i, held):
        at = layout.locate(i)
        for n, p in enumerate(pairs):
            picked = [at.chosen(2 * p), at.chosen(2 * p + 1)]
            probs, inverse = soft_rows(held[n])
            values = gathered(tri_ref, at, (3 * p + 2) * PAIR, picked)
            put(p, at.b, dot_nn(probs, values) * inverse)

    held_a, held_b = held[: len(pairs)], held[len(pairs) :]
    sparse_scores(0, held_a)

    def two(j, carry):
        sparse_scores(2 * j + 1, held_b)
        sparse_mix(2 * j, held_a)
        sparse_scores(jnp.minimum(2 * j + 2, layout.inner - 1), held_a)
        sparse_mix(2 * j + 1, held_b)
        return carry

    lax.fori_loop(0, lax.div(layout.inner, 2), two, 0)

    def dense(item, carry):
        first, last, chunks = layout.ends(item)
        queries = [
            jnp.concatenate([query_of(p, first), query_of(p, last)], axis=0) for p in pairs
        ]

        def dense_of(spans):
            for query, p in zip(queries, pairs):
                span = layout.half * BLK
                for c, at in enumerate(spans):
                    keys = tri_ref[at, (3 * p + 1) * PAIR : (3 * p + 2) * PAIR]
                    wide[:, c * span : (c + 1) * span] = dot_nt(query, keys)
                probs, inverse = soft_rows(wide.at[:, : len(spans) * span])
                mixed = sum(
                    dot_nn(
                        probs[:, c * span : (c + 1) * span],
                        tri_ref[at, (3 * p + 2) * PAIR : (3 * p + 3) * PAIR],
                    )
                    for c, at in enumerate(spans)
                ) * inverse
                put(p, first, mixed[:PAIR])
                put(p, last, mixed[PAIR:])

        @pl.when(chunks == 1)
        def short():
            dense_of([layout.part(first)])

        @pl.when(chunks == 2)
        def long():
            dense_of([layout.part(first), layout.part(first + layout.half)])

        return carry

    lax.fori_loop(0, 1 + layout.second, dense, 0)


def grad_rows(held_scores, held_grads, probs_ref, grads_ref):
    for row in range(0, held_scores.shape[0], ROWS):
        at = slice(row, row + ROWS)
        scores = held_scores[at, :]
        grad_probs = held_grads[at, :]
        expo = jnp.exp(scores - jnp.max(scores, axis=1, keepdims=True))
        probs = expo * (1.0 / jnp.sum(expo, axis=1, keepdims=True))
        delta = jnp.sum(probs * grad_probs, axis=1, keepdims=True)
        probs_ref[at, :] = probs.astype(jnp.bfloat16)
        grads_ref[at, :] = (probs * (grad_probs - delta)).astype(jnp.bfloat16)


def attn_bwd_kernel(
    pairs, position, len_ref, rb_ref, tri_ref, grad_ref, out_ref, sum_ref, *scratch
):
    blocks = tri_ref.shape[0] // BLK
    scale = jnp.bfloat16(BLK**-0.5)
    back = BLK**-0.5
    layout = Layout(len_ref, rb_ref, blocks, position())
    layout.counts()
    count = len(pairs)
    key_acc, value_acc = scratch[:count], scratch[count : 2 * count]
    held_a, held_b, done = (scratch[n * count : (n + 2) * count] for n in (2, 4, 6))
    wide = scratch[8 * count :]

    def clear(r, carry):
        at = pl.ds(pl.multiple_of(r * BLK, BLK), BLK)
        for acc in scratch[: 2 * count]:
            acc[at, :] = jnp.zeros((BLK, PAIR), jnp.float32)
        return carry

    lax.fori_loop(0, blocks, clear, 0)

    def query_of(p, b):
        at = layout.spot(b)
        return stacked(tri_ref[at, p * 3 * PAIR : p * 3 * PAIR + PAIR]) * scale

    def grad_of(p, b):
        at = layout.spot(b)
        return stacked(grad_ref[at, p * PAIR : (p + 1) * PAIR])

    def put(i, b, grad_query):
        out_ref[layout.spot(b), i * 3 * PAIR : i * 3 * PAIR + PAIR] = unstacked(
            grad_query * back
        ).astype(jnp.bfloat16)

    def sparse_scores(n, held):
        at = layout.locate(n)
        lane = lax.broadcasted_iota(jnp.int32, (1, PAIR), 1) < BLK
        bias_row = jnp.where(lane, at.low_bias, at.high_bias)
        for i, p in enumerate(pairs):
            picked = [at.chosen(2 * p), at.chosen(2 * p + 1)]
            keys = gathered(tri_ref, at, (3 * p + 1) * PAIR, picked)
            values = gathered(tri_ref, at, (3 * p + 2) * PAIR, picked)
            scores = dot_nt(query_of(p, at.b), keys)
            held[2 * i][...] = jnp.concatenate(
                [scores[:, :PAIR], scores[:, PAIR : 2 * PAIR] + bias_row, scores[:, 2 * PAIR :]],
                axis=1,
            )
            held[2 * i + 1][...] = dot_nt(grad_of(p, at.b), values)

    def sparse_grads(n, held):
        at = layout.locate(n)
        even = even_lanes(BLK)
        for i, p in enumerate(pairs):
            grad_rows(held[2 * i], held[2 * i + 1], done[2 * i], done[2 * i + 1])
            picked = [at.chosen(2 * p), at.chosen(2 * p + 1)]
            spots = [at.spot(index) for index in at.fixed]
            spots += [(at.spot(one), at.spot(two)) for one, two in zip(*picked)]
            keys = gathered(tri_ref, at, (3 * p + 1) * PAIR, picked)
            put(i, at.b, dot_nn(done[2 * i + 1][...], keys))
            for acc, update in (
                (key_acc[i], dot_tn(done[2 * i + 1][...], query_of(p, at.b))),
                (value_acc[i], dot_tn(done[2 * i][...], grad_of(p, at.b))),
            ):
                for j, spot in enumerate(spots):
                    piece = update[j * BLK : (j + 1) * BLK]
                    if j < len(at.fixed):
                        acc[spot, :] += piece
                    else:
                        zero = jnp.zeros_like(piece)
                        acc[spot[0], :] += jnp.where(even, piece, zero)
                        acc[spot[1], :] += jnp.where(even, zero, piece)

    sparse_scores(0, held_a)

    def two(j, carry):
        sparse_scores(2 * j + 1, held_b)
        sparse_grads(2 * j, held_a)
        sparse_scores(jnp.minimum(2 * j + 2, layout.inner - 1), held_a)
        sparse_grads(2 * j + 1, held_b)
        return carry

    lax.fori_loop(0, lax.div(layout.inner, 2), two, 0)

    wide_scores, wide_grads, wide_probs, wide_out = wide

    def dense(item, carry):
        first, last, chunks = layout.ends(item)

        def dense_of(spans):
            span = layout.half * BLK
            cover = len(spans) * span
            def end(n, carry):
                b = jnp.where(n == 0, first, last)
                for i, p in enumerate(pairs):
                    query, grad = query_of(p, b), grad_of(p, b)
                    for c, at in enumerate(spans):
                        cut = slice(c * span, (c + 1) * span)
                        keys = tri_ref[at, (3 * p + 1) * PAIR : (3 * p + 2) * PAIR]
                        values = tri_ref[at, (3 * p + 2) * PAIR : (3 * p + 3) * PAIR]
                        wide_scores[:, cut] = dot_nt(query, keys)
                        wide_grads[:, cut] = dot_nt(grad, values)
                    grad_rows(*(ref.at[:, :cover] for ref in wide))
                    total = jnp.zeros((PAIR, PAIR), jnp.float32)
                    for c, at in enumerate(spans):
                        cut = slice(c * span, (c + 1) * span)
                        keys = tri_ref[at, (3 * p + 1) * PAIR : (3 * p + 2) * PAIR]
                        total += dot_nn(wide_out[:, cut], keys)
                        key_acc[i][at, :] += dot_tn(wide_out[:, cut], query)
                        value_acc[i][at, :] += dot_tn(wide_probs[:, cut], grad)
                    put(i, b, total)
                return carry

            lax.fori_loop(0, 2, end, 0)

        @pl.when(chunks == 1)
        def short():
            dense_of([layout.part(first)])

        @pl.when(chunks == 2)
        def long():
            dense_of([layout.part(first), layout.part(first + layout.half)])

        return carry

    lax.fori_loop(0, 1 + layout.second, dense, 0)

    sum_ref[...] = jnp.zeros_like(sum_ref)

    def finish(r, carry):
        at = pl.ds(pl.multiple_of(r * BLK, BLK), BLK)
        new = []
        for i in range(count):
            column = i * 3 * PAIR
            query_sum, value_sum = carry[i]
            out_ref[at, column + PAIR : column + 2 * PAIR] = key_acc[i][at, :].astype(jnp.bfloat16)
            value = value_acc[i][at, :].astype(jnp.bfloat16)
            out_ref[at, column + 2 * PAIR : column + 3 * PAIR] = value
            query = out_ref[at, column : column + PAIR].astype(jnp.float32)
            new.append(
                tuple(
                    total + jnp.sum(part.reshape(-1, 8, PAIR), axis=0)
                    for total, part in (
                        (query_sum, query),
                        (value_sum, value.astype(jnp.float32)),
                    )
                )
            )
        return tuple(new)

    zero = jnp.zeros((8, PAIR), jnp.float32)
    sums = lax.fori_loop(0, blocks, finish, tuple((zero, zero) for _ in pairs))
    for i, totals in enumerate(sums):
        for kind, total in enumerate(totals):
            sum_ref[kind : kind + 1, i * PAIR : (i + 1) * PAIR] = jnp.sum(
                total, axis=0, keepdims=True
            )


vmem = pl.BlockSpec(memory_space=pltpu.VMEM)
smem = pl.BlockSpec(memory_space=pltpu.SMEM)
def attention_forward(lengths, randoms, triple, position):
    pairs = randoms.shape[1] // 2
    rows = triple.shape[0]
    area = rows * rows // 3 * 2 * pairs
    return pl.pallas_call(
        functools.partial(attn_fwd_kernel, range(pairs), position),
        out_shape=jax.ShapeDtypeStruct((rows, pairs * PAIR), jnp.bfloat16),
        in_specs=[smem, smem, vmem],
        out_specs=vmem,
        name="attend_forward",
        scratch_shapes=[pltpu.VMEM((2 * PAIR, rows), jnp.float32)]
        + [pltpu.VMEM((PAIR, 8 * BLK), jnp.float32)] * (2 * pairs),
        cost_estimate=pl.CostEstimate(
            flops=16 * area * PAIR, transcendentals=area, bytes_accessed=rows * pairs * PAIR * 8
        ),
        compiler_params=pltpu.CompilerParams(vmem_limit_bytes=8 << 20),
    )(lengths, randoms, triple)


def attention_backward(lengths, randoms, triple, grad, pairs, position):
    rows = triple.shape[0]
    count = len(pairs)
    area = rows * rows // 3 * 2 * count
    return pl.pallas_call(
        functools.partial(attn_bwd_kernel, pairs, position),
        out_shape=(
            jax.ShapeDtypeStruct((rows, count * 3 * PAIR), jnp.bfloat16),
            jax.ShapeDtypeStruct((8, count * PAIR), jnp.float32),
        ),
        in_specs=[smem, smem, vmem, vmem],
        out_specs=(vmem, vmem),
        name="attend_backward",
        scratch_shapes=[pltpu.VMEM((rows, PAIR), jnp.float32)] * (2 * count)
        + [pltpu.VMEM((PAIR, 8 * BLK), jnp.float32)] * (4 * count)
        + [pltpu.VMEM((PAIR, 8 * BLK), jnp.bfloat16)] * (2 * count)
        + [pltpu.VMEM((PAIR, rows), kind) for kind in (jnp.float32,) * 2 + (jnp.bfloat16,) * 2],
        cost_estimate=pl.CostEstimate(
            flops=40 * area * PAIR, transcendentals=area, bytes_accessed=rows * count * PAIR * 20
        ),
        compiler_params=pltpu.CompilerParams(vmem_limit_bytes=20 << 20),
    )(lengths, randoms, triple, grad)


TILE = 256
EPS = 1e-06


def tile_at(n):
    return pl.ds(pl.multiple_of(n * TILE, TILE), TILE)


def up_kernel(rows_ref, weight_ref, bias_ref, active_ref, slope_ref, held_a, held_b):
    tiles = weight_ref.shape[1] // TILE
    root = (2.0 / np.pi) ** 0.5
    cube = 0.044715 * root

    def product(n, held):
        held[...] = dot_nn(rows_ref[...], weight_ref[:, tile_at(n)])

    def gelu(n, held):
        bias = bias_ref[:, tile_at(n)]
        for row in range(0, held.shape[0], ROWS):
            at = slice(row, row + ROWS)
            upper = (held[at, :] + bias).astype(jnp.bfloat16).astype(jnp.float32)
            square = upper * upper
            half = 0.5 + 0.5 * jnp.tanh(upper * (square * cube + root))
            active = upper * half
            active_ref[at, tile_at(n)] = active.astype(jnp.bfloat16)
            bend = (1.0 - half) * (square * (6.0 * cube) + 2.0 * root)
            slope_ref[at, tile_at(n)] = (half + active * bend).astype(jnp.bfloat16)

    product(0, held_a)

    def two(j, carry):
        product(2 * j + 1, held_b)
        gelu(2 * j, held_a)
        product(jnp.minimum(2 * j + 2, tiles - 1), held_a)
        gelu(2 * j + 1, held_b)
        return carry

    lax.fori_loop(0, tiles // 2, two, 0)


def up_gelu(rows, weight, bias):
    count, width = rows.shape[0], weight.shape[1]
    shape = jax.ShapeDtypeStruct((count, width), jnp.bfloat16)
    return pl.pallas_call(
        up_kernel,
        out_shape=(shape, shape),
        in_specs=[vmem] * 3,
        out_specs=(vmem, vmem),
        name="up_gelu",
        scratch_shapes=[pltpu.VMEM((count, TILE), jnp.float32)] * 2,
        cost_estimate=pl.CostEstimate(
            flops=2 * count * width * rows.shape[1],
            transcendentals=count * width,
            bytes_accessed=2 * (rows.size + weight.size + 2 * count * width),
        ),
        compiler_params=pltpu.CompilerParams(vmem_limit_bytes=12 << 20),
    )(rows, weight, bias.reshape(1, -1))


def back_kernel(grad_ref, weight_ref, slope_ref, out_ref, sum_ref):
    def step(n, carry):
        grad_active = dot_nn(grad_ref[...], weight_ref[:, tile_at(n)])
        total = jnp.zeros((8, TILE), jnp.float32)
        for row in range(0, grad_active.shape[0], ROWS):
            at = slice(row, row + ROWS)
            grad = grad_active[at] * slope_ref[at, tile_at(n)].astype(jnp.float32)
            grad = grad.astype(jnp.bfloat16)
            out_ref[at, tile_at(n)] = grad
            total += jnp.sum(grad.astype(jnp.float32).reshape(-1, 8, TILE), axis=0)
        sum_ref[:, tile_at(n)] = total
        return carry

    lax.fori_loop(0, weight_ref.shape[1] // TILE, step, 0)


def back_slope(grad, weight, slope):
    count, width = slope.shape
    return pl.pallas_call(
        back_kernel,
        out_shape=(
            jax.ShapeDtypeStruct((count, width), jnp.bfloat16),
            jax.ShapeDtypeStruct((8, width), jnp.float32),
        ),
        in_specs=[vmem] * 3,
        out_specs=(vmem, vmem),
        name="back_slope",
        cost_estimate=pl.CostEstimate(
            flops=2 * count * width * grad.shape[1],
            transcendentals=0,
            bytes_accessed=2 * (grad.size + weight.size + 2 * count * width),
        ),
        compiler_params=pltpu.CompilerParams(vmem_limit_bytes=12 << 20),
    )(grad, weight, slope)


def outer_kernel(count, *refs):
    lefts, rights, out_ref = refs[:count], refs[count:-1], refs[-1]
    if len(rights) < count:
        rows = lefts[0].shape[0]
        rights = [rights[0].at[n * rows : (n + 1) * rows] for n in range(count)]

    def step(at):
        total = sum(dot_tn(a[...], b[:, at]) for a, b in zip(lefts, rights))
        out_ref[:, at] = total.astype(jnp.bfloat16)

    width = out_ref.shape[1]
    if width % TILE:
        step(slice(0, width))
    else:

        def body(n, carry):
            step(tile_at(n))
            return carry

        lax.fori_loop(0, width // TILE, body, 0)


def outer(lefts, rights):
    shape = (lefts[0].shape[1], rights[0].shape[1])
    inner = sum(a.shape[0] for a in lefts)
    return pl.pallas_call(
        functools.partial(outer_kernel, len(lefts)),
        out_shape=jax.ShapeDtypeStruct(shape, jnp.bfloat16),
        in_specs=[vmem] * (len(lefts) + len(rights)),
        out_specs=vmem,
        name="outer",
        cost_estimate=pl.CostEstimate(
            flops=2 * inner * shape[0] * shape[1],
            transcendentals=0,
            bytes_accessed=2 * inner * sum(shape),
        ),
        compiler_params=pltpu.CompilerParams(vmem_limit_bytes=12 << 20),
    )(*lefts, *rights)


def project_kernel(own_ref, other_ref, weight_ref, out_ref):
    rows = own_ref.shape[0]
    for n, ref in enumerate((own_ref, other_ref)):
        product = dot_nn(ref[...], weight_ref[...])
        out_ref[n * rows : (n + 1) * rows, :] = product.astype(jnp.bfloat16)


def project_both(own, other, weight):
    return pl.pallas_call(
        project_kernel,
        out_shape=jax.ShapeDtypeStruct((2 * own.shape[0], weight.shape[1]), jnp.bfloat16),
        in_specs=[vmem] * 3,
        out_specs=vmem,
        name="project_both",
        compiler_params=pltpu.CompilerParams(vmem_limit_bytes=12 << 20),
    )(own, other, weight)


GROUP = 16
SPLIT = 4


def groups_at(r):
    return [
        (r * SPLIT + n, pl.ds(pl.multiple_of((r * SPLIT + n) * GROUP, GROUP), GROUP))
        for n in range(SPLIT)
    ]


def row_mean(values):
    return jnp.sum(values, axis=1, keepdims=True) * (1.0 / values.shape[1])


def folded(values):
    return jnp.sum(values.reshape(-1, 8, values.shape[1]), axis=0)


def norm_two_kernel(position, len_ref, down_ref, other_ref, resid_ref, cot_ref, vec_ref, out_ref, grad_ref, low_ref, sum_ref):
    count, width = down_ref.shape
    live_rows = len_ref[0, 0] + len_ref[0, 1] - position() * count
    bias, gain, shift = (vec_ref[n : n + 1, :] for n in range(3))

    def group(r, at, sums):
        row = r * GROUP + lax.broadcasted_iota(jnp.int32, (GROUP, 1), 0)
        live = jnp.where(row < live_rows, 1.0, 0.0)
        values = down_ref[at, :] + other_ref[at, :].astype(jnp.float32) + bias + resid_ref[at, :]
        centered = values - row_mean(values)
        inverse = lax.rsqrt(row_mean(centered * centered) + EPS)
        normed = centered * inverse
        out_ref[at, :] = ((normed * gain + shift) * live).astype(jnp.bfloat16)
        cot = cot_ref[at, :].astype(jnp.float32) * live
        scaled = cot * gain
        grad = inverse * (scaled - row_mean(scaled) - normed * row_mean(scaled * normed))
        grad_ref[at, :] = grad
        low_ref[at, :] = grad.astype(jnp.bfloat16)
        return tuple(s + folded(v) for s, v in zip(sums, (grad, cot * normed, cot)))

    def step(r, sums):
        for n, at in groups_at(r):
            sums = group(n, at, sums)
        return sums

    zero = jnp.zeros((8, width), jnp.float32)
    sums = lax.fori_loop(0, count // (GROUP * SPLIT), step, (zero,) * 3)
    for n, total in enumerate(sums):
        sum_ref[n : n + 1, :] = jnp.sum(total, axis=0, keepdims=True)
    sum_ref[3:8, :] = jnp.zeros((5, width), jnp.float32)


def norm_two(lengths, down, other, resid, cot, bias, gain, shift, position):
    shape = down.shape
    row = jax.ShapeDtypeStruct((8, shape[1]), jnp.float32)
    return pl.pallas_call(
        functools.partial(norm_two_kernel, position),
        out_shape=(
            jax.ShapeDtypeStruct(shape, jnp.bfloat16),
            jax.ShapeDtypeStruct(shape, jnp.float32),
            jax.ShapeDtypeStruct(shape, jnp.bfloat16),
            row,
        ),
        in_specs=[smem] + [vmem] * 5,
        out_specs=(vmem,) * 4,
        name="norm_two",
        cost_estimate=pl.CostEstimate(
            flops=40 * down.size, transcendentals=0, bytes_accessed=20 * down.size
        ),
        compiler_params=pltpu.CompilerParams(vmem_limit_bytes=12 << 20),
    )(lengths, down, other, resid, cot, jnp.stack([bias, gain, shift]))


def norm_one_kernel(own_ref, other_ref, grad_ref, normed_ref, inverse_ref, gain_ref, out_ref, low_ref, sum_ref):
    count, width = own_ref.shape
    gain = gain_ref[...]

    def group(r, at, sums):
        grad = own_ref[at, :] + other_ref[at, :].astype(jnp.float32) + grad_ref[at, :]
        normed = normed_ref[at, :]
        scaled = grad * gain
        result = inverse_ref[at, :] * (
            scaled - row_mean(scaled) - normed * row_mean(scaled * normed)
        )
        out_ref[at, :] = result
        low_ref[at, :] = result.astype(jnp.bfloat16)
        return tuple(s + folded(v) for s, v in zip(sums, (result, grad * normed, grad)))

    def step(r, sums):
        for n, at in groups_at(r):
            sums = group(n, at, sums)
        return sums

    zero = jnp.zeros((8, width), jnp.float32)
    sums = lax.fori_loop(0, count // (GROUP * SPLIT), step, (zero,) * 3)
    for n, total in enumerate(sums):
        sum_ref[n : n + 1, :] = jnp.sum(total, axis=0, keepdims=True)
    sum_ref[3:8, :] = jnp.zeros((5, width), jnp.float32)


def norm_one_back(own, other, grad, normed, inverse, gain):
    shape = own.shape
    return pl.pallas_call(
        norm_one_kernel,
        out_shape=(
            jax.ShapeDtypeStruct(shape, jnp.float32),
            jax.ShapeDtypeStruct(shape, jnp.bfloat16),
            jax.ShapeDtypeStruct((8, shape[1]), jnp.float32),
        ),
        in_specs=[vmem] * 6,
        out_specs=(vmem,) * 3,
        name="norm_one_back",
        cost_estimate=pl.CostEstimate(
            flops=20 * own.size, transcendentals=0, bytes_accessed=20 * own.size
        ),
        compiler_params=pltpu.CompilerParams(vmem_limit_bytes=12 << 20),
    )(own, other, grad, normed, inverse, gain.reshape(1, -1))


def pack_rows(ref, at, small):
    rows = small.shape[0]
    high = small.astype(jnp.bfloat16)
    ref[at : at + rows, :] = high
    ref[at + rows : at + 2 * rows, :] = (small - high.astype(jnp.float32)).astype(jnp.bfloat16)


def unpack_rows(ref, at, rows):
    high = ref[at : at + rows, :].astype(jnp.float32)
    return high + ref[at + rows : at + 2 * rows, :].astype(jnp.float32)


def slab_at(at_ref, place, z, rows):
    return pl.ds(pl.multiple_of((z * QUAD + at_ref[place]) * rows, rows), rows)


def columns_of(totals):
    cuts, low = [], 0
    for total in totals:
        cuts.append(slice(low, low + total.shape[1]))
        low += total.shape[1]
    return cuts


def sum_first_kernel(count, deep, at_ref, *refs):
    totals, rest = refs[:count], refs[count:]
    out_ref = rest[-1]
    rows = totals[0].shape[0] // (deep * QUAD)
    for part, place in enumerate((1, 3)):
        for z in range(deep):
            row = (part * deep + z) * rows
            for total, cut in zip(totals, columns_of(totals)):
                out_ref[row : row + rows, cut] = total[slab_at(at_ref, place, z, rows), :]
    if len(rest) > 1:
        pack_rows(out_ref, 2 * deep * rows, rest[0][...])


def sum_second_kernel(count, deep, at_ref, *refs):
    totals, got_ref = refs[:count], refs[count]
    rows = totals[0].shape[0] // (deep * QUAD)
    if len(refs) > count + 2:
        small_ref, out_ref, new_ref = refs[count + 1 :]
        small = small_ref[...] + unpack_rows(got_ref, 2 * deep * rows, small_ref.shape[0])
        new_ref[...] = small
        pack_rows(out_ref, deep * rows, small)
    else:
        out_ref = refs[-1]
    for z in range(deep):
        for total, cut in zip(totals, columns_of(totals)):
            far = total[slab_at(at_ref, 2, z, rows), :].astype(jnp.float32)
            row = (deep + z) * rows
            far = far + got_ref[row : row + rows, cut].astype(jnp.float32)
            out_ref[z * rows : (z + 1) * rows, cut] = far.astype(jnp.bfloat16)


def sum_deep_kernel(groups, deep, small_rows, at_ref, *refs):
    count = sum(groups)
    totals, refs = refs[:count], refs[count:]
    gots, twos, refs = refs[: len(groups)], refs[len(groups) : 2 * len(groups)], refs[2 * len(groups) :]
    rows = totals[0].shape[0] // (deep * QUAD)
    small = None
    if small_rows:
        small_ref, new_ref, refs = refs[0], refs[1], refs[2:]
        small = small_ref[...] + unpack_rows(twos[-1], deep * rows, small_rows)
        part = new_ref.shape[0]
        cuts = [small[n * part : (n + 1) * part] for n in range(small_rows // part)]
        small = jnp.concatenate(cuts, axis=1)
        new_ref[...] = small
    out_cuts = columns_of(totals)
    for k in range(deep):
        z = at_ref[QUAD] ^ k
        near = pl.ds(pl.multiple_of(z * rows, rows), rows)
        n = 0
        for group, got_ref, two_ref in zip(groups, gots, twos):
            members = totals[n : n + group]
            for total, cut, out_cut in zip(members, columns_of(members), out_cuts[n : n + group]):
                value = (
                    total[slab_at(at_ref, 0, z, rows), :].astype(jnp.float32)
                    + got_ref[near, cut].astype(jnp.float32)
                    + two_ref[near, cut].astype(jnp.float32)
                )
                refs[k][:rows, out_cut] = value.astype(refs[k].dtype)
            n += group
        if k and small is not None:
            pack_rows(refs[k], rows, small)


def sum_last_kernel(count, small_rows, *refs):
    own_ref, answers = refs[0], refs[1 : 1 + count]
    rows = own_ref.shape[0]
    own = own_ref[...]
    for answer in answers:
        own = own + answer[:rows, :].astype(jnp.float32)
    outs = refs[1 + count :]
    if small_rows:
        small_ref, new_ref, outs = outs[0], outs[-1], outs[1:-1]
        small = small_ref[...]
        for answer in answers:
            small = small + unpack_rows(answer, rows, small_rows)
        new_ref[...] = small
    for out_ref, cut in zip(outs, columns_of(outs)):
        out_ref[...] = own[:, cut]


def vmem_call(kernel, outs, operands, name, scalars=1, limit=12):
    outs = [jax.ShapeDtypeStruct(shape, dtype) for shape, dtype in outs]
    return pl.pallas_call(
        kernel,
        out_shape=outs,
        in_specs=[smem] * scalars + [vmem] * (len(operands) - scalars),
        out_specs=[vmem] * len(outs),
        name=name,
        compiler_params=pltpu.CompilerParams(vmem_limit_bytes=limit << 20),
    )(*operands)


def sum_first(totals, spot, small=None):
    span = totals[0].shape[0] // QUAD
    extra = 0 if small is None else 2 * small.shape[0]
    shape = (2 * span + extra, sum(t.shape[1] for t in totals))
    operands = [spot.at, *totals] + ([] if small is None else [small])
    kernel = functools.partial(sum_first_kernel, len(totals), spot.deep)
    return vmem_call(kernel, [(shape, jnp.bfloat16)], operands, "sum_first")[0]


def sum_second(totals, spot, got, small=None):
    span = totals[0].shape[0] // QUAD
    kernel = functools.partial(sum_second_kernel, len(totals), spot.deep)
    operands = [spot.at, *totals, got]
    if small is None:
        outs = [((span, got.shape[1]), jnp.bfloat16)]
        return vmem_call(kernel, outs, operands, "sum_second")[0]
    outs = [((span + 2 * small.shape[0], got.shape[1]), jnp.bfloat16), (small.shape, jnp.float32)]
    return vmem_call(kernel, outs, operands + [small], "sum_second")


def sum_deep(groups, spot, gots, twos, small=None):
    totals = [total for group in groups for total in group]
    rows = totals[0].shape[0] // (QUAD * spot.deep)
    columns = sum(t.shape[1] for t in totals)
    small_rows = 0 if small is None else small.shape[0]
    kernel = functools.partial(
        sum_deep_kernel, [len(group) for group in groups], spot.deep, small_rows
    )
    operands = [spot.at, *totals, *gots, *twos] + ([] if small is None else [small])
    outs, extra = [], 0
    if small is not None:
        part = small_rows // 3
        outs, extra = [((part, columns), jnp.float32)], 2 * part
    outs += [((rows, columns), jnp.float32)]
    outs += [((rows + extra, columns), jnp.bfloat16)] * (spot.deep - 1)
    return vmem_call(kernel, outs, operands, "sum_deep")


def sum_last(own, answers, widths, small=None):
    kernel = functools.partial(
        sum_last_kernel, len(answers), 0 if small is None else small.shape[0]
    )
    operands = [own, *answers] + ([] if small is None else [small])
    outs = [((own.shape[0], w), jnp.float32) for w in widths]
    outs += [] if small is None else [(small.shape, jnp.float32)]
    return vmem_call(kernel, outs, operands, "sum_last", scalars=0)


def small_kernel(own_ref, swapped_ref, up_one_ref, up_two_ref, *refs):
    out_ref = refs[-1]
    columns = out_ref.shape[1]
    both = own_ref[...] + swapped_ref[...]
    rows = [both[0:3], both[8:11]]
    row = 0
    for low in range(0, both.shape[1], columns):
        for part in rows:
            out_ref[row : row + 3, :] = part[:, low : low + columns]
            row += 3
    up = jnp.sum(up_one_ref[...] + up_two_ref[...], axis=0, keepdims=True)
    for low in range(0, up.shape[1], columns):
        out_ref[row : row + 1, :] = up[:, low : low + columns]
        row += 1
    low = 0
    for ref in refs[:-1]:
        out_ref[row : row + 2, low : low + ref.shape[1]] = ref[0:2, :]
        low += ref.shape[1]


def small_sums(own, swapped, up_one, up_two, sums):
    columns = sum(s.shape[1] for s in sums)
    rows = 6 * own.shape[1] // columns + up_one.shape[1] // columns + 2
    return vmem_call(
        small_kernel,
        [((rows, columns), jnp.float32)],
        [own, swapped, up_one, up_two, *sums],
        "small_sums",
        scalars=0,
    )[0]


def rows_kernel(window, cuts, *refs):
    lefts, weight_ref, out_ref = refs[:-2], refs[-2], refs[-1]
    rows = slice(*window)

    def step(n, carry):
        total = sum(
            dot_nt(left[rows, :], weight_ref[tile_at(n), cut]) for left, cut in zip(lefts, cuts)
        )
        out_ref[:, tile_at(n)] = total.astype(out_ref.dtype)
        return carry

    lax.fori_loop(0, out_ref.shape[1] // TILE, step, 0)


def rows_product(lefts, weight, window, dtype):
    shape = (window[1] - window[0], weight.shape[0])
    return pl.pallas_call(
        functools.partial(rows_kernel, window, columns_of(lefts)),
        out_shape=jax.ShapeDtypeStruct(shape, dtype),
        in_specs=[vmem] * (len(lefts) + 1),
        out_specs=vmem,
        name="rows_product",
        cost_estimate=pl.CostEstimate(
            flops=2 * shape[0] * weight.size,
            transcendentals=0,
            bytes_accessed=2 * (shape[0] * sum(weight.shape) + weight.size),
        ),
        compiler_params=pltpu.CompilerParams(vmem_limit_bytes=12 << 20),
    )(*lefts, weight)


def triple_kernel(own_ref, other_ref, weight_ref, bias_ref, out_ref):
    rows = own_ref.shape[0]
    span = 3 * PAIR

    def step(n, carry):
        at = pl.ds(pl.multiple_of(n * span, span), span)
        for k, ref in enumerate((own_ref, other_ref)):
            product = dot_nn(ref[...], weight_ref[:, at]) + bias_ref[:, at]
            out_ref[k * rows : (k + 1) * rows, at] = product.astype(jnp.bfloat16)
        return carry

    lax.fori_loop(0, out_ref.shape[1] // span, step, 0)


def triple_of(own, other, weight, bias):
    shape = (2 * own.shape[0], weight.shape[1])
    return pl.pallas_call(
        triple_kernel,
        out_shape=jax.ShapeDtypeStruct(shape, jnp.bfloat16),
        in_specs=[vmem] * 4,
        out_specs=vmem,
        name="triple",
        cost_estimate=pl.CostEstimate(
            flops=2 * shape[0] * weight.size,
            transcendentals=0,
            bytes_accessed=2 * (shape[0] * sum(weight.shape) + weight.size),
        ),
        compiler_params=pltpu.CompilerParams(vmem_limit_bytes=12 << 20),
    )(own, other, weight, bias.reshape(1, -1))


QUAD = 4


def group_permute(value, deep, target):
    pairs = []
    for z in range(deep):
        for q in range(QUAD):
            for h in range(2):
                to_z, to_q = target(z, q, h)
                pairs.append(((z * QUAD + q) * 2 + h, (to_z * QUAD + to_q) * 2 + h))
    return lax.ppermute(value, ("deep", "quad", "head"), pairs)


def deep_step(value, deep, bit):
    return group_permute(value, deep, lambda z, q, h: (z ^ bit, q))


def quad_step(value, deep, second):
    return group_permute(value, deep, lambda z, q, h: (z, q ^ ((2 >> h) if second else (1 << h))))


def swap(value):
    return lax.ppermute(value, "head", [(0, 1), (1, 0)])


def after(value, *others):
    return lax.optimization_barrier((value,) + others)[0]


class Spot:
    def __init__(self):
        self.z, self.q, self.h = (lax.axis_index(a) for a in ("deep", "quad", "head"))
        self.deep = lax.axis_size("deep")
        one, two = 1 << self.h, 2 >> self.h
        self.places = [self.q, self.q ^ one, self.q ^ two, self.q ^ 3]
        self.at = jnp.stack(self.places + [self.z]).astype(jnp.int32)


def deep_pieces(value, spot):
    return [deep_step(value, spot.deep, k) for k in range(1, spot.deep)]


def place_kernel(deep, windows, at_ref, *refs):
    pieces, outs = refs[:QUAD], refs[QUAD:]
    rows = pieces[0].shape[1]
    for k in range(deep):
        for j, piece in enumerate(pieces):
            row = pl.multiple_of(((at_ref[QUAD] ^ k) * QUAD + at_ref[j]) * rows, rows)
            for out, (low, high) in zip(outs, windows):
                out[pl.ds(row, rows), :] = piece[k, :, low:high]


def place(spot, pieces, widths):
    windows, low = [], 0
    for width in widths:
        windows.append((low, low + width))
        low += width
    deep, rows = pieces[0].shape[:2]
    outs = [((deep * QUAD * rows, width), pieces[0].dtype) for width in widths]
    kernel = functools.partial(place_kernel, deep, windows)
    return vmem_call(kernel, outs, [spot.at, *pieces], "place_pieces", limit=8)


def low(value):
    return value.astype(jnp.bfloat16)


def by_pair(value):
    lead, kinds, columns = value.shape[:-2], value.shape[-2], value.shape[-1]
    split = value.reshape(lead + (kinds, columns // PAIR, PAIR))
    return jnp.swapaxes(split, -3, -2).reshape(lead + (kinds * columns,))


def by_kind(value, kinds):
    lead, columns = value.shape[:-1], value.shape[-1]
    split = value.reshape(lead + (columns // (kinds * PAIR), kinds, PAIR))
    return jnp.swapaxes(split, -3, -2).reshape(lead + (kinds, columns // kinds))


def on_device(
    inputs,
    qkv_weight,
    qv_bias,
    out_weight,
    out_bias,
    first_gain,
    first_shift,
    up_weight,
    up_bias,
    down_weight,
    down_bias,
    second_gain,
    second_shift,
    item_lengths,
    random_blocks,
    out_grad,
):
    half, width = inputs.shape
    spot = Spot()
    deep = spot.deep
    shard = qkv_weight.shape[0]
    head_width = qkv_weight.shape[2]
    up_width = up_weight.shape[1]
    pair_count = head_width // PAIR

    def position():
        return lax.axis_index("head")

    staged = deep == 4 and shard % 16 == 0
    every = ("deep", "quad")

    def gathered_whole(block):
        return lax.all_gather(block, every, axis=0, tiled=True)

    def scattered(total):
        return lax.psum_scatter(total, every, scatter_dimension=0, tiled=True).astype(jnp.float32)

    def first_quad(block):
        return quad_step(block, deep, False)

    def second_quad(block):
        return quad_step(block, deep, True)

    tokens_other = swap(inputs)
    qkv_block = by_pair(qkv_weight)
    mid = jnp.concatenate([out_weight, up_weight], axis=1)
    if staged:
        qkv_pieces = deep_pieces(qkv_block, spot)
        mid_pieces = deep_pieces(after(mid, *qkv_pieces), spot)
        qkv_deep = jnp.stack([qkv_block] + qkv_pieces)
        qkv_other, qkv_far = first_quad(qkv_deep), second_quad(qkv_deep)
        qkv_other, qkv_far, *mid_pieces = lax.optimization_barrier(
            (qkv_other, qkv_far, *mid_pieces)
        )
        qkv_across = second_quad(qkv_other)
        (full_qkv,) = place(spot, (qkv_deep, qkv_other, qkv_far, qkv_across), [3 * head_width])
        full_qkv, *mid_pieces = lax.optimization_barrier((full_qkv, *mid_pieces))
        mid_deep = jnp.stack([mid] + mid_pieces)
        mid_other, mid_far = first_quad(mid_deep), second_quad(mid_deep)
        full_qkv, mid_deep = lax.optimization_barrier((full_qkv, mid_deep))
        down_pieces = deep_pieces(after(down_weight, *mid_pieces), spot)
    else:
        full_qkv = gathered_whole(qkv_block)
        full_mid = gathered_whole(mid)
        full_out, full_up = full_mid[:, :head_width], full_mid[:, head_width:]
        full_down = gathered_whole(down_weight)

    bias = by_pair(jnp.stack([qv_bias[0], jnp.zeros_like(qv_bias[0]), qv_bias[1]]))
    triple = triple_of(inputs, tokens_other, full_qkv, bias)
    attended = attention_forward(item_lengths, random_blocks, triple, position)
    if staged:
        attended, mid_other, mid_far, *down_pieces = lax.optimization_barrier(
            (attended, mid_other, mid_far, *down_pieces)
        )
        mid_across = second_quad(mid_other)
        down_deep = jnp.stack([down_weight] + down_pieces)
        full_out, full_up = place(
            spot, (mid_deep, mid_other, mid_far, mid_across), [head_width, up_width]
        )
        full_out, down_deep = lax.optimization_barrier((full_out, down_deep))
        down_other, down_far = first_quad(down_deep), second_quad(down_deep)

    whole = (half, 2 * half)
    other = swap(rows_product([attended], full_out, whole, jnp.bfloat16))
    proj = rows_product([attended], full_out, (0, half), jnp.float32) + other.astype(jnp.float32)
    normed_one_out, normed_one, inverse_one = norm_forward(
        proj + out_bias + inputs.astype(jnp.float32), first_gain, first_shift
    )
    hidden_own = low(normed_one_out)
    hidden_other = swap(hidden_own)
    active_own, slope_own = up_gelu(hidden_own, full_up, up_bias)
    if staged:
        active_own, down_other, down_far = lax.optimization_barrier(
            (active_own, down_other, down_far)
        )
        down_across = second_quad(down_other)
    active_other, slope_other = up_gelu(hidden_other, full_up, up_bias)
    if staged:
        active_other, active_own, down_across = lax.optimization_barrier(
            (active_other, active_own, down_across)
        )
        (full_down,) = place(spot, (down_deep, down_other, down_far, down_across), [up_width])
    other = swap(rows_product([active_other], full_down, (0, half), jnp.bfloat16))
    layer_out, grad_res_two, grad_own, sums_two = norm_two(
        item_lengths,
        rows_product([active_own], full_down, (0, half), jnp.float32),
        other,
        normed_one_out,
        out_grad,
        down_bias,
        second_gain,
        second_shift,
        position,
    )
    grad_other = swap(grad_own)
    grad_upper_own, up_sum_own = back_slope(grad_own, full_down, slope_own)
    down_local = outer([grad_own, grad_other], [active_own, active_other])
    if staged:
        message = sum_first([down_local], spot)
        down_got = first_quad(message)
        grad_other, message = lax.optimization_barrier((grad_other, message))
    grad_upper_other, up_sum_other = back_slope(grad_other, full_down, slope_other)
    other = swap(rows_product([grad_upper_other], full_up, (0, half), jnp.bfloat16))
    up_local = outer([hidden_own, hidden_other], [grad_upper_own, grad_upper_other])
    grad_res_one, grad_proj_own, sums_one = norm_one_back(
        rows_product([grad_upper_own], full_up, (0, half), jnp.float32), other, grad_res_two, normed_one, inverse_one, first_gain
    )
    if staged:
        grad_proj_own, down_got = lax.optimization_barrier((grad_proj_own, down_got))
        down_message = sum_second([down_local], spot, down_got)
        down_two = second_quad(down_message)
        grad_proj_own, down_message = lax.optimization_barrier((grad_proj_own, down_message))
    grad_proj_other = swap(grad_proj_own)
    shared = jnp.concatenate([sums_one, sums_two], axis=0)
    shared_other = swap(shared)
    grad_attended = project_both(grad_proj_own, grad_proj_other, full_out)
    out_local = outer([grad_proj_own, grad_proj_other], [attended])

    mids = [out_local, up_local]
    split = pair_count - 1
    if staged:
        mid_message = sum_first(mids, spot)
        mid_got = first_quad(mid_message)
        grad_attended, mid_message = lax.optimization_barrier((grad_attended, mid_message))
    grads_a, sums_a = attention_backward(
        item_lengths, random_blocks, triple, grad_attended, range(split), position
    )
    if staged:
        grads_a, mid_got, down_two, grad_attended, shared_other = lax.optimization_barrier(
            (grads_a, mid_got, down_two, grad_attended, shared_other)
        )
        mid_message = sum_second(mids, spot, mid_got)
        mid_two = second_quad(mid_message)
        down_sum, *messages = sum_deep([[down_local]], spot, [down_got], [down_two])
        down_answers = [deep_step(m, deep, k + 1) for k, m in enumerate(messages)]
    local_a = outer([inputs, tokens_other], [grads_a])
    if staged:
        message_a = sum_first([local_a], spot)
        got_a = first_quad(message_a)
        grad_attended, message_a, mid_message, *messages = lax.optimization_barrier(
            (grad_attended, message_a, mid_message, *messages)
        )
    grads_b, sums_b = attention_backward(
        item_lengths, random_blocks, triple, grad_attended, range(split, pair_count), position
    )
    if staged:
        grads_b, got_a, mid_two, *down_answers = lax.optimization_barrier(
            (grads_b, got_a, mid_two, *down_answers)
        )
    local_b = outer([inputs, tokens_other], [grads_b])
    small = small_sums(shared, shared_other, up_sum_own, up_sum_other, [sums_a, sums_b])
    if staged:
        message_b = sum_first([local_b], spot, small)
        got_b = first_quad(message_b)
        message_a = sum_second([local_a], spot, after(got_a, message_b))
        two_a = second_quad(message_a)
        mid_got, message_a = lax.optimization_barrier((mid_got, message_a))
        mid_sum, *messages = sum_deep([mids], spot, [mid_got], [mid_two])
        mid_answers = [deep_step(m, deep, k + 1) for k, m in enumerate(messages)]
        grads_a, grads_b, *messages = lax.optimization_barrier((grads_a, grads_b, *messages))

    other = swap(rows_product([grads_a, grads_b], full_qkv, whole, jnp.bfloat16))
    mine = rows_product([grads_a, grads_b], full_qkv, (0, half), jnp.float32)
    if staged:
        mine, other, got_b, two_a = lax.optimization_barrier((mine, other, got_b, two_a))
        message, small = sum_second([local_b], spot, got_b, small)
        two_b = second_quad(message)
        other, message = lax.optimization_barrier((other, message))
    input_grad = low(mine + other.astype(jnp.float32) + grad_res_one)
    if staged:
        (grad_down,) = sum_last(down_sum, down_answers, [up_width])
        input_grad, grad_down, two_b = lax.optimization_barrier((input_grad, grad_down, two_b))
        small, qkv_sum, *messages = sum_deep(
            [[local_a], [local_b]], spot, [got_a, got_b], [two_a, two_b], small
        )
        answers = [deep_step(m, deep, k + 1) for k, m in enumerate(messages)]
        grad_out, grad_up = sum_last(mid_sum, mid_answers, [head_width, up_width])
        grad_out, grad_up, *answers = lax.optimization_barrier((grad_out, grad_up, *answers))
        grad_qkv, small = sum_last(qkv_sum, answers, [3 * head_width], small)
    else:
        grad_down, grad_up, grad_out = (scattered(v) for v in (down_local, up_local, out_local))
        grad_qkv = scattered(jnp.concatenate([local_a, local_b], axis=1))
        small = lax.psum(small, every)
        part = small.shape[0] // 3
        small = jnp.concatenate([small[n * part : (n + 1) * part] for n in range(3)], axis=1)

    totals = small[:, :width]
    rest = small[:, width : width + head_width]
    grad_up_bias = rest[: up_width // head_width].reshape(up_width)
    grad_qv_bias = rest[up_width // head_width :]
    return (
        layer_out,
        input_grad,
        by_kind(grad_qkv, 3),
        grad_qv_bias,
        grad_out,
        totals[0],
        totals[1],
        totals[2],
        grad_up,
        grad_up_bias,
        grad_down,
        totals[3],
        totals[4],
        totals[5],
    )


def solution(mesh):
    devices = mesh.devices.reshape(-1, QUAD, mesh.shape["head"])
    fine = Mesh(devices, ("deep", "quad", "head"))
    rows = ("deep", "quad", "head")
    dp = ("deep", "quad")
    in_specs = (
        P(rows, None),
        P(dp, None, "head"),
        P(None, "head"),
        P(dp, "head"),
        P(),
        P(),
        P(),
        P(dp, "head"),
        P("head"),
        P(dp, "head"),
        P(),
        P(),
        P(),
        P(dp, None),
        P(dp, "head", None, None),
        P(rows, None),
    )
    out_specs = (
        P(rows, None),
        P(rows, None),
        P(dp, None, "head"),
        P(None, "head"),
        P(dp, "head"),
        P(),
        P(),
        P(),
        P(dp, "head"),
        P("head"),
        P(dp, "head"),
        P(),
        P(),
        P(),
    )
    return jax.shard_map(
        on_device, mesh=fine, in_specs=in_specs, out_specs=out_specs, check_vma=False
    )
```

profile of v0, /device:TPU:0, one launch (start us, length us, event | category | flops | bytes accessed | tf_op | source)
XLA Modules:
  0.0 260.4 jit_solution(6220558183557463318)
XLA Ops:
  1.8 3.1 %collective-permute-start.1 = (bf16[48,1152]{1,0:T(8,128)(2,1)S(1)}, bf16[48,1152]{1,0:T(8,128)(2,1)S(1)}, u32[]{:S(2)}, u32[]{:S(2)}) collective-permute-start(bf16[48,1152]{1,0:T(8,128)(2,1)S(1)} %reshape.80), channel_id=1, source_target_pairs={{0,8},{1,9},{2,10},{3,11},{4,12},{5,13},{6,14},{7,15},{8,0},{9,1},... | collective-permute-start | bytes 331784 | tf_op jit(solution)/shard_map/ppermute | solution.py:973
  4.9 2.6 collective-permute-start.2
  8.4 7.9 %collective-permute-done.2 = bf16[48,1152]{1,0:T(8,128)(2,1)S(1)} collective-permute-done((bf16[48,1152]{1,0:T(8,128)(2,1)S(1)}, bf16[48,1152]{1,0:T(8,128)(2,1)S(1)}, u32[]{:S(2)}, u32[]{:S(2)}) %collective-permute-start.2) | collective-permute-done | bytes 110624 | tf_op jit(solution)/shard_map/ppermute | solution.py:973
  23.5 4.2 %collective-permute-done.6 = bf16[48,1920]{1,0:T(8,128)(2,1)S(1)} collective-permute-done((bf16[48,1920]{1,0:T(8,128)(2,1)S(1)}, bf16[48,1920]{1,0:T(8,128)(2,1)S(1)}, u32[]{:S(2)}, u32[]{:S(2)}) %collective-permute-start.6) | collective-permute-done | bytes 184352 | tf_op jit(solution)/shard_map/ppermute | solution.py:973
  29.9 7.3 %collective-permute-done.7 = bf16[48,1920]{1,0:T(8,128)(2,1)S(1)} collective-permute-done((bf16[48,1920]{1,0:T(8,128)(2,1)S(1)}, bf16[48,1920]{1,0:T(8,128)(2,1)S(1)}, u32[]{:S(2)}, u32[]{:S(2)}) %collective-permute-start.7) | collective-permute-done | bytes 184352 | tf_op jit(solution)/shard_map/ppermute | solution.py:973
  39.5 6.8 %collective-permute-done.9.refs_3_ = bf16[4,48,1152]{2,1,0:T(8,128)(2,1)S(1)} collective-permute-done((bf16[4,48,1152]{2,1,0:T(8,128)(2,1)S(1)}, bf16[4,48,1152]{2,1,0:T(8,128)(2,1)S(1)}, u32[]{:S(2)}, u32[]{:S(2)}) %collective-permute-start.9) | collective-permute-done | bytes 442400 | tf_op jit(solution)/shard_map/ppermute | solution.py:973
  46.9 2.7 %collective-permute-start.12 = (bf16[48,1536]{1,0:T(8,128)(2,1)S(1)}, bf16[48,1536]{1,0:T(8,128)(2,1)S(1)}, u32[]{:S(2)}, u32[]{:S(2)}) collective-permute-start(bf16[48,1536]{1,0:T(8,128)(2,1)S(1)} %copy-done.7), channel_id=1, source_target_pairs={{0,8},{1,9},{2,10},{3,11},{4,12},{5,13},{6,14},{7,15},{8,0},{9,1},... | collective-permute-start | bytes 442376 | tf_op jit(solution)/shard_map/ppermute | solution.py:973
  53.3 4.2 %triple.1.tri_ref = bf16[1536,1152]{1,0:T(8,128)(2,1)S(1)} custom-call(bf16[768,768]{1,0:T(8,128)(2,1)S(1)} %copy-done, bf16[768,768]{1,0:T(8,128)(2,1)S(1)} %collective-permute-done.other_ref.refs_1_, bf16[768,1152]{1,0:T(8,128)(2,1)S(1)} %place_pieces.3.weight_ref.refs_2_, f32[1,1152]{1,0:T(1,128)S(1)} %reshape_reshape.3.bias_ref), custom_call_target="tpu_custom_call" | custom-call | flops 2717908992 | bytes 7667712 | tf_op jit(solution)/shard_map/triple/pallas_call | solution.py:948
  57.5 13.7 %attend_forward.1.refs_0_.refs_2_ = bf16[1536,384]{1,0:T(8,128)(2,1)S(1)} custom-call(s32[1,2]{1,0:T(1,128)S(1)} %copy-done.2, s32[1,6,24,3]{3,2,1,0:T(8,128)S(1)} %copy.39.rb_ref, bf16[1536,1152]{1,0:T(8,128)(2,1)S(1)} %triple.1.tri_ref), custom_call_target="tpu_custom_call" | custom-call | flops 9663676416 | bytes 4718592 | tf_op jit(solution)/shard_map/attend_forward/pallas_call | solution.py:395
  72.3 10.5 %collective-permute-done.15.refs_3_ = bf16[4,48,1920]{2,1,0:T(8,128)(2,1)S(1)} collective-permute-done((bf16[4,48,1920]{2,1,0:T(8,128)(2,1)S(1)}, bf16[4,48,1920]{2,1,0:T(8,128)(2,1)S(1)}, u32[]{:S(2)}, u32[]{:S(2)}) %collective-permute-start.15) | collective-permute-done | bytes 737312 | tf_op jit(solution)/shard_map/ppermute | solution.py:973
  92.7 4.9 %up_gelu.3 = (bf16[768,1536]{1,0:T(8,128)(2,1)S(1)}, bf16[768,1536]{1,0:T(8,128)(2,1)S(1)}) custom-call(bf16[768,768]{1,0:T(8,128)(2,1)S(1)} %get-tuple-element.222.rows_ref.refs_0_, bf16[768,1536]{1,0:T(8,128)(2,1)S(1)} %get-tuple-element.136.weight_ref.refs_1_, f32[1,1536]{1,0:T(1,128)S(1)} %reshape.82.bias_ref), custom_call_target="tpu_custom_call" | custom-call | flops 1811939328 | bytes 8257536 | tf_op jit(solution)/shard_map/up_gelu/pallas_call | solution.py:477
  97.5 8.0 %collective-permute-done.18.refs_1_ = bf16[4,48,1536]{2,1,0:T(8,128)(2,1)S(1)} collective-permute-done((bf16[4,48,1536]{2,1,0:T(8,128)(2,1)S(1)}, bf16[4,48,1536]{2,1,0:T(8,128)(2,1)S(1)}, u32[]{:S(2)}, u32[]{:S(2)}) %collective-permute-start.18) | collective-permute-done | bytes 589856 | tf_op jit(solution)/shard_map/ppermute | solution.py:973
  106.7 4.9 %up_gelu.2 = (bf16[768,1536]{1,0:T(8,128)(2,1)S(1)}, bf16[768,1536]{1,0:T(8,128)(2,1)S(1)}) custom-call(bf16[768,768]{1,0:T(8,128)(2,1)S(1)} %collective-permute-done.17.rows_ref.refs_1_, bf16[768,1536]{1,0:T(8,128)(2,1)S(1)} %get-tuple-element.136.weight_ref.refs_1_, f32[1,1536]{1,0:T(1,128)S(1)} %reshape.82.bias_ref), custom_call_target="tpu_custom_call" | custom-call | flops 1811939328 | bytes 8257536 | tf_op jit(solution)/shard_map/up_gelu/pallas_call | solution.py:477
  111.6 3.8 %collective-permute-done.20.refs_3_ = bf16[4,48,1536]{2,1,0:T(8,128)(2,1)S(1)} collective-permute-done((bf16[4,48,1536]{2,1,0:T(8,128)(2,1)S(1)}, bf16[4,48,1536]{2,1,0:T(8,128)(2,1)S(1)}, u32[]{:S(2)}, u32[]{:S(2)}) %collective-permute-start.20) | collective-permute-done | bytes 589856 | tf_op jit(solution)/shard_map/ppermute | solution.py:973
  118.7 2.4 rows_product.10.down_ref
  121.5 5.4 %norm_two.1 = (bf16[768,768]{1,0:T(8,128)(2,1)}, f32[768,768]{1,0:T(8,128)S(1)}, bf16[768,768]{1,0:T(8,128)(2,1)S(1)}, f32[8,768]{1,0:T(8,128)S(1)}) custom-call(s32[1,2]{1,0:T(1,128)S(1)} %copy-done.2, f32[768,768]{1,0:T(8,128)S(1)} %rows_product.10.down_ref, bf16[768,768]{1,0:T(8,128)(2,1)S(1)} %collective-permute-done.21.other_ref, ...), custom_call_target="tpu_custom_call" | custom-call | flops 23592960 | bytes 11796480 | tf_op jit(solution)/shard_map/norm_two/pallas_call | solution.py:641
  127.1 2.6 %collective-permute-done.22.refs_1_.grad_ref = bf16[768,768]{1,0:T(8,128)(2,1)S(1)} collective-permute-done((bf16[768,768]{1,0:T(8,128)(2,1)S(1)}, bf16[768,768]{1,0:T(8,128)(2,1)S(1)}, u32[]{:S(2)}, u32[]{:S(2)}) %collective-permute-start.22) | collective-permute-done | bytes 1179680 | tf_op jit(solution)/shard_map/ppermute | solution.py:985
  129.8 4.9 %outer.5.refs_0_ = bf16[768,1536]{1,0:T(8,128)(2,1)S(1)} custom-call(bf16[768,768]{1,0:T(8,128)(2,1)S(1)} %get-tuple-element.147.grad_ref.refs_0_, bf16[768,768]{1,0:T(8,128)(2,1)S(1)} %collective-permute-done.22.refs_1_.grad_ref, bf16[768,1536]{1,0:T(8,128)(2,1)S(1)} %get-tuple-element.142.refs_0_.refs_2_, ...), custom_call_target="tpu_custom_call" | custom-call | flops 3623878656 | bytes 7077888 | tf_op jit(solution)/shard_map/outer/pallas_call | solution.py:554
  135.4 3.1 %back_slope.3 = (bf16[768,1536]{1,0:T(8,128)(2,1)S(1)}, f32[8,1536]{1,0:T(8,128)S(1)}) custom-call(bf16[768,768]{1,0:T(8,128)(2,1)S(1)} %collective-permute-done.22.refs_1_.grad_ref, bf16[768,1536]{1,0:T(8,128)(2,1)S(1)} %place_pieces.5.refs_1_.weight_ref, bf16[768,1536]{1,0:T(8,128)(2,1)S(1)} %get-tuple-element.151.slope_ref), custom_call_target="tpu_custom_call" | custom-call | flops 1811939328 | bytes 8257536 | tf_op jit(solution)/shard_map/back_slope/pallas_call | solution.py:511
  142.6 2.9 %back_slope.2 = (bf16[768,1536]{1,0:T(8,128)(2,1)S(1)}, f32[8,1536]{1,0:T(8,128)S(1)}) custom-call(bf16[768,768]{1,0:T(8,128)(2,1)S(1)} %get-tuple-element.147.grad_ref.refs_0_, bf16[768,1536]{1,0:T(8,128)(2,1)S(1)} %place_pieces.5.refs_1_.weight_ref, bf16[768,1536]{1,0:T(8,128)(2,1)S(1)} %get-tuple-element.148.slope_ref), custom_call_target="tpu_custom_call" | custom-call | flops 1811939328 | bytes 8257536 | tf_op jit(solution)/shard_map/back_slope/pallas_call | solution.py:511
  145.5 2.4 rows_product.12.own_ref
  150.2 7.2 %collective-permute-done.24.refs_1_ = bf16[384,1536]{1,0:T(8,128)(2,1)S(1)} collective-permute-done((bf16[384,1536]{1,0:T(8,128)(2,1)S(1)}, bf16[384,1536]{1,0:T(8,128)(2,1)S(1)}, u32[]{:S(2)}, u32[]{:S(2)}) %collective-permute-start.24) | collective-permute-done | bytes 1179680 | tf_op jit(solution)/shard_map/ppermute | solution.py:973
  158.2 5.0 %outer.7.refs_1_ = bf16[768,1536]{1,0:T(8,128)(2,1)S(1)} custom-call(bf16[768,768]{1,0:T(8,128)(2,1)S(1)} %get-tuple-element.222.rows_ref.refs_0_, bf16[768,768]{1,0:T(8,128)(2,1)S(1)} %collective-permute-done.17.rows_ref.refs_1_, bf16[768,1536]{1,0:T(8,128)(2,1)S(1)} %get-tuple-element.149.refs_0_.refs_2_, ...), custom_call_target="tpu_custom_call" | custom-call | flops 3623878656 | bytes 7077888 | tf_op jit(solution)/shard_map/outer/pallas_call | solution.py:554
  169.8 23.3 %attend_backward.2 = (bf16[1536,768]{1,0:T(8,128)(2,1)S(1)}, f32[8,256]{1,0:T(8,128)S(1)}) custom-call(s32[1,2]{1,0:T(1,128)S(1)} %copy-done.2, s32[1,6,24,3]{3,2,1,0:T(8,128)S(1)} %copy.39.rb_ref, bf16[1536,1152]{1,0:T(8,128)(2,1)S(1)} %triple.1.tri_ref, bf16[1536,384]{1,0:T(8,128)(2,1)S(1)} %project_both.1.grad_ref), custom_call_target="tpu_custom_call" | custom-call | flops 16106127360 | bytes 7864320 | tf_op jit(solution)/shard_map/attend_backward/pallas_call | solution.py:414
  194.6 2.5 outer.8.refs_0_
  197.7 3.0 %collective-permute-start.32 = (bf16[48,1536]{1,0:T(8,128)(2,1)S(1)}, bf16[48,1536]{1,0:T(8,128)(2,1)S(1)}, u32[]{:S(2)}, u32[]{:S(2)}) collective-permute-start(bf16[48,1536]{1,0:T(8,128)(2,1)S(1)} %get-tuple-element.167), channel_id=1, source_target_pairs={{0,16},{1,17},{2,18},{3,19},{4,20},{5,21},{6,22},{7,23},{8,24},{9,... | collective-permute-start | bytes 442376 | tf_op jit(solution)/shard_map/ppermute | solution.py:973
  204.3 15.2 %attend_backward.3 = (bf16[1536,384]{1,0:T(8,128)(2,1)S(1)}, f32[8,128]{1,0:T(8,128)S(1)}) custom-call(s32[1,2]{1,0:T(1,128)S(1)} %copy-done.2, s32[1,6,24,3]{3,2,1,0:T(8,128)S(1)} %copy.39.rb_ref, bf16[1536,1152]{1,0:T(8,128)(2,1)S(1)} %triple.1.tri_ref, bf16[1536,384]{1,0:T(8,128)(2,1)S(1)} %project_both.1.grad_ref), custom_call_target="tpu_custom_call" | custom-call | flops 8053063680 | bytes 3932160 | tf_op jit(solution)/shard_map/attend_backward/pallas_call | solution.py:414
  227.1 3.0 %collective-permute-start.39 = (bf16[48,1920]{1,0:T(8,128)(2,1)S(1)}, bf16[48,1920]{1,0:T(8,128)(2,1)S(1)}, u32[]{:S(2)}, u32[]{:S(2)}) collective-permute-start(bf16[48,1920]{1,0:T(8,128)(2,1)S(1)} %get-tuple-element.182), channel_id=1, source_target_pairs={{0,16},{1,17},{2,18},{3,19},{4,20},{5,21},{6,22},{7,23},{8,24},{9,... | collective-permute-start | bytes 552968 | tf_op jit(solution)/shard_map/ppermute | solution.py:973
  234.9 2.5 collective-permute-start.40
  239.8 3.7 %collective-permute-done.37.refs_5_ = bf16[228,384]{1,0:T(8,128)(2,1)S(1)} collective-permute-done((bf16[228,384]{1,0:T(8,128)(2,1)S(1)}, bf16[228,384]{1,0:T(8,128)(2,1)S(1)}, u32[]{:S(2)}, u32[]{:S(2)}) %collective-permute-start.37) | collective-permute-done | bytes 175136 | tf_op jit(solution)/shard_map/ppermute | solution.py:973
  246.3 2.5 collective-permute-start.43
  250.2 7.2 %collective-permute-done.42.refs_2_ = bf16[60,1152]{1,0:T(8,128)(2,1)S(1)} collective-permute-done((bf16[60,1152]{1,0:T(8,128)(2,1)S(1)}, bf16[60,1152]{1,0:T(8,128)(2,1)S(1)}, u32[]{:S(2)}, u32[]{:S(2)}) %collective-permute-start.42) | collective-permute-done | bytes 138272 | tf_op jit(solution)/shard_map/ppermute | solution.py:973
  (167 shorter events, 75.5 us)
Async XLA Ops:
  4.9 11.3 %collective-permute-start.2 = (bf16[48,1152]{1,0:T(8,128)(2,1)S(1)}, bf16[48,1152]{1,0:T(8,128)(2,1)S(1)}, u32[]{:S(2)}, u32[]{:S(2)}) collective-permute-start(bf16[48,1152]{1,0:T(8,128)(2,1)S(1)} %reshape.80), channel_id=1, source_target_pairs={{0,16},{1,17},{2,18},{3,19},{4,20},{5,21},{6,22},{7,23},{8,24},{9,... | collective-permute-start | bytes 331784 | tf_op jit(solution)/shard_map/ppermute | solution.py:973
  7.5 45.3 %collective-permute-start = (bf16[768,768]{1,0:T(8,128)(2,1)}, bf16[768,768]{1,0:T(8,128)(2,1)S(1)}, u32[]{:S(2)}, u32[]{:S(2)}) collective-permute-start(bf16[768,768]{1,0:T(8,128)(2,1)} %refs_0_.3), channel_id=1, source_target_pairs={{0,1},{1,0},{2,3},{3,2},{4,5},{5,4},{6,7},{7,6},{8,9},{9,8},{10,11... | collective-permute-start | bytes 3538952 | tf_op jit(solution)/shard_map/ppermute | solution.py:985
  16.3 20.9 %collective-permute-start.4 = (bf16[4,48,1152]{2,1,0:T(8,128)(2,1)S(1)}, bf16[4,48,1152]{2,1,0:T(8,128)(2,1)S(1)}, u32[]{:S(2)}, u32[]{:S(2)}) collective-permute-start(bf16[4,48,1152]{2,1,0:T(8,128)(2,1)S(1)} %pad_maximum_fusion.2.refs_0_), channel_id=1, source_target_pairs={{0,2},{1,5},{2,0},{3,7},{4,6},{5,1},{6,4},{7,3},{8,10},{9,13},{10,... | collective-permute-start | bytes 1327112 | tf_op jit(solution)/shard_map/ppermute | solution.py:973
  17.9 20.0 %collective-permute-start.5 = (bf16[4,48,1152]{2,1,0:T(8,128)(2,1)S(1)}, bf16[4,48,1152]{2,1,0:T(8,128)(2,1)S(1)}, u32[]{:S(2)}, u32[]{:S(2)}) collective-permute-start(bf16[4,48,1152]{2,1,0:T(8,128)(2,1)S(1)} %pad_maximum_fusion.2.refs_0_), channel_id=1, source_target_pairs={{0,4},{1,3},{2,6},{3,1},{4,0},{5,7},{6,2},{7,5},{8,12},{9,11},{10,... | collective-permute-start | bytes 1327112 | tf_op jit(solution)/shard_map/ppermute | solution.py:973
  22.2 15.0 %collective-permute-start.7 = (bf16[48,1920]{1,0:T(8,128)(2,1)S(1)}, bf16[48,1920]{1,0:T(8,128)(2,1)S(1)}, u32[]{:S(2)}, u32[]{:S(2)}) collective-permute-start(bf16[48,1920]{1,0:T(8,128)(2,1)S(1)} %constant_dynamic-update-slice_fusion), channel_id=1, source_target_pairs={{0,16},{1,17},{2,18},{3,19},{4,20},{5,21},{6,22},{7,23},{8,24},{9,... | collective-permute-start | bytes 552968 | tf_op jit(solution)/shard_map/ppermute | solution.py:973
  27.7 9.5 %collective-permute-start.8 = (bf16[48,1920]{1,0:T(8,128)(2,1)S(1)}, bf16[48,1920]{1,0:T(8,128)(2,1)S(1)}, u32[]{:S(2)}, u32[]{:S(2)}) collective-permute-start(bf16[48,1920]{1,0:T(8,128)(2,1)S(1)} %constant_dynamic-update-slice_fusion), channel_id=1, source_target_pairs={{0,24},{1,25},{2,26},{3,27},{4,28},{5,29},{6,30},{7,31},{8,16},{9,... | collective-permute-start | bytes 552968 | tf_op jit(solution)/shard_map/ppermute | solution.py:973
  46.9 24.3 %collective-permute-start.12 = (bf16[48,1536]{1,0:T(8,128)(2,1)S(1)}, bf16[48,1536]{1,0:T(8,128)(2,1)S(1)}, u32[]{:S(2)}, u32[]{:S(2)}) collective-permute-start(bf16[48,1536]{1,0:T(8,128)(2,1)S(1)} %copy-done.7), channel_id=1, source_target_pairs={{0,8},{1,9},{2,10},{3,11},{4,12},{5,13},{6,14},{7,15},{8,0},{9,1},... | collective-permute-start | bytes 442376 | tf_op jit(solution)/shard_map/ppermute | solution.py:973
  49.6 21.6 %collective-permute-start.13 = (bf16[48,1536]{1,0:T(8,128)(2,1)S(1)}, bf16[48,1536]{1,0:T(8,128)(2,1)S(1)}, u32[]{:S(2)}, u32[]{:S(2)}) collective-permute-start(bf16[48,1536]{1,0:T(8,128)(2,1)S(1)} %copy-done.7), channel_id=1, source_target_pairs={{0,16},{1,17},{2,18},{3,19},{4,20},{5,21},{6,22},{7,23},{8,24},{9,... | collective-permute-start | bytes 442376 | tf_op jit(solution)/shard_map/ppermute | solution.py:973
  50.7 20.6 %collective-permute-start.14 = (bf16[48,1536]{1,0:T(8,128)(2,1)S(1)}, bf16[48,1536]{1,0:T(8,128)(2,1)S(1)}, u32[]{:S(2)}, u32[]{:S(2)}) collective-permute-start(bf16[48,1536]{1,0:T(8,128)(2,1)S(1)} %copy-done.7), channel_id=1, source_target_pairs={{0,24},{1,25},{2,26},{3,27},{4,28},{5,29},{6,30},{7,31},{8,16},{9,... | collective-permute-start | bytes 442376 | tf_op jit(solution)/shard_map/ppermute | solution.py:973
  52.2 19.0 %collective-permute-start.10 = (bf16[4,48,1920]{2,1,0:T(8,128)(2,1)S(1)}, bf16[4,48,1920]{2,1,0:T(8,128)(2,1)S(1)}, u32[]{:S(2)}, u32[]{:S(2)}) collective-permute-start(bf16[4,48,1920]{2,1,0:T(8,128)(2,1)S(1)} %pad_maximum_fusion.refs_0_), channel_id=1, source_target_pairs={{0,2},{1,5},{2,0},{3,7},{4,6},{5,1},{6,4},{7,3},{8,10},{9,13},{10,... | collective-permute-start | bytes 2211848 | tf_op jit(solution)/shard_map/ppermute | solution.py:973
  52.8 18.4 %collective-permute-start.11 = (bf16[4,48,1920]{2,1,0:T(8,128)(2,1)S(1)}, bf16[4,48,1920]{2,1,0:T(8,128)(2,1)S(1)}, u32[]{:S(2)}, u32[]{:S(2)}) collective-permute-start(bf16[4,48,1920]{2,1,0:T(8,128)(2,1)S(1)} %pad_maximum_fusion.refs_0_), channel_id=1, source_target_pairs={{0,4},{1,3},{2,6},{3,1},{4,0},{5,7},{6,2},{7,5},{8,12},{9,11},{10,... | collective-permute-start | bytes 2211848 | tf_op jit(solution)/shard_map/ppermute | solution.py:973
  71.3 11.5 %collective-permute-start.15 = (bf16[4,48,1920]{2,1,0:T(8,128)(2,1)S(1)}, bf16[4,48,1920]{2,1,0:T(8,128)(2,1)S(1)}, u32[]{:S(2)}, u32[]{:S(2)}) collective-permute-start(bf16[4,48,1920]{2,1,0:T(8,128)(2,1)S(1)} %collective-permute-done.10.refs_1_), channel_id=1, source_target_pairs={{0,4},{1,3},{2,6},{3,1},{4,0},{5,7},{6,2},{7,5},{8,12},{9,11},{10,... | collective-permute-start | bytes 2211848 | tf_op jit(solution)/shard_map/ppermute | solution.py:973
  89.4 17.3 %collective-permute-start.17 = (bf16[768,768]{1,0:T(8,128)(2,1)S(1)}, bf16[768,768]{1,0:T(8,128)(2,1)S(1)}, u32[]{:S(2)}, u32[]{:S(2)}) collective-permute-start(bf16[768,768]{1,0:T(8,128)(2,1)S(1)} %get-tuple-element.222.rows_ref.refs_0_), channel_id=1, source_target_pairs={{0,1},{1,0},{2,3},{3,2},{4,5},{5,4},{6,7},{7,6},{8,9},{9,8},{10,11... | collective-permute-start | bytes 3538952 | tf_op jit(solution)/shard_map/ppermute | solution.py:985
  89.6 15.9 %collective-permute-start.18 = (bf16[4,48,1536]{2,1,0:T(8,128)(2,1)S(1)}, bf16[4,48,1536]{2,1,0:T(8,128)(2,1)S(1)}, u32[]{:S(2)}, u32[]{:S(2)}) collective-permute-start(bf16[4,48,1536]{2,1,0:T(8,128)(2,1)S(1)} %pad_maximum_fusion.1.refs_0_), channel_id=1, source_target_pairs={{0,2},{1,5},{2,0},{3,7},{4,6},{5,1},{6,4},{7,3},{8,10},{9,13},{10,... | collective-permute-start | bytes 1769480 | tf_op jit(solution)/shard_map/ppermute | solution.py:973
  91.1 14.4 %collective-permute-start.19 = (bf16[4,48,1536]{2,1,0:T(8,128)(2,1)S(1)}, bf16[4,48,1536]{2,1,0:T(8,128)(2,1)S(1)}, u32[]{:S(2)}, u32[]{:S(2)}) collective-permute-start(bf16[4,48,1536]{2,1,0:T(8,128)(2,1)S(1)} %pad_maximum_fusion.1.refs_0_), channel_id=1, source_target_pairs={{0,4},{1,3},{2,6},{3,1},{4,0},{5,7},{6,2},{7,5},{8,12},{9,11},{10,... | collective-permute-start | bytes 1769480 | tf_op jit(solution)/shard_map/ppermute | solution.py:973
  105.5 9.9 %collective-permute-start.20 = (bf16[4,48,1536]{2,1,0:T(8,128)(2,1)S(1)}, bf16[4,48,1536]{2,1,0:T(8,128)(2,1)S(1)}, u32[]{:S(2)}, u32[]{:S(2)}) collective-permute-start(bf16[4,48,1536]{2,1,0:T(8,128)(2,1)S(1)} %collective-permute-done.18.refs_1_), channel_id=1, source_target_pairs={{0,4},{1,3},{2,6},{3,1},{4,0},{5,7},{6,2},{7,5},{8,12},{9,11},{10,... | collective-permute-start | bytes 1769480 | tf_op jit(solution)/shard_map/ppermute | solution.py:973
  141.2 16.2 %collective-permute-start.24 = (bf16[384,1536]{1,0:T(8,128)(2,1)S(1)}, bf16[384,1536]{1,0:T(8,128)(2,1)S(1)}, u32[]{:S(2)}, u32[]{:S(2)}) collective-permute-start(bf16[384,1536]{1,0:T(8,128)(2,1)S(1)} %sum_first.4), channel_id=1, source_target_pairs={{0,2},{1,5},{2,0},{3,7},{4,6},{5,1},{6,4},{7,3},{8,10},{9,13},{10,... | collective-permute-start | bytes 3538952 | tf_op jit(solution)/shard_map/ppermute | solution.py:973
  163.1 29.9 %collective-permute-start.27 = (bf16[192,1536]{1,0:T(8,128)(2,1)S(1)}, bf16[192,1536]{1,0:T(8,128)(2,1)S(1)}, u32[]{:S(2)}, u32[]{:S(2)}) collective-permute-start(bf16[192,1536]{1,0:T(8,128)(2,1)S(1)} %sum_second.4), channel_id=1, source_target_pairs={{0,4},{1,3},{2,6},{3,1},{4,0},{5,7},{6,2},{7,5},{8,12},{9,11},{10,... | collective-permute-start | bytes 1769480 | tf_op jit(solution)/shard_map/ppermute | solution.py:973
  164.4 28.7 %collective-permute-start.28 = (f32[16,768]{1,0:T(8,128)S(1)}, f32[16,768]{1,0:T(8,128)S(1)}, u32[]{:S(2)}, u32[]{:S(2)}) collective-permute-start(f32[16,768]{1,0:T(8,128)S(1)} %constant_dynamic-update-slice_fusion.2.own_ref), channel_id=1, source_target_pairs={{0,1},{1,0},{2,3},{3,2},{4,5},{5,4},{6,7},{7,6},{8,9},{9,8},{10,11... | collective-permute-start | bytes 147464 | tf_op jit(solution)/shard_map/ppermute | solution.py:985
  166.7 26.3 %collective-permute-start.26 = (bf16[384,1920]{1,0:T(8,128)(2,1)S(1)}, bf16[384,1920]{1,0:T(8,128)(2,1)S(1)}, u32[]{:S(2)}, u32[]{:S(2)}) collective-permute-start(bf16[384,1920]{1,0:T(8,128)(2,1)S(1)} %sum_first.5), channel_id=1, source_target_pairs={{0,2},{1,5},{2,0},{3,7},{4,6},{5,1},{6,4},{7,3},{8,10},{9,13},{10,... | collective-permute-start | bytes 4423688 | tf_op jit(solution)/shard_map/ppermute | solution.py:973
  197.7 21.9 %collective-permute-start.31 = (bf16[48,1536]{1,0:T(8,128)(2,1)S(1)}, bf16[48,1536]{1,0:T(8,128)(2,1)S(1)}, u32[]{:S(2)}, u32[]{:S(2)}) collective-permute-start(bf16[48,1536]{1,0:T(8,128)(2,1)S(1)} %get-tuple-element.166), channel_id=1, source_target_pairs={{0,8},{1,9},{2,10},{3,11},{4,12},{5,13},{6,14},{7,15},{8,0},{9,1},... | collective-permute-start | bytes 442376 | tf_op jit(solution)/shard_map/ppermute | solution.py:973
  197.7 21.8 %collective-permute-start.32 = (bf16[48,1536]{1,0:T(8,128)(2,1)S(1)}, bf16[48,1536]{1,0:T(8,128)(2,1)S(1)}, u32[]{:S(2)}, u32[]{:S(2)}) collective-permute-start(bf16[48,1536]{1,0:T(8,128)(2,1)S(1)} %get-tuple-element.167), channel_id=1, source_target_pairs={{0,16},{1,17},{2,18},{3,19},{4,20},{5,21},{6,22},{7,23},{8,24},{9,... | collective-permute-start | bytes 442376 | tf_op jit(solution)/shard_map/ppermute | solution.py:973
  200.7 18.8 %collective-permute-start.33 = (bf16[48,1536]{1,0:T(8,128)(2,1)S(1)}, bf16[48,1536]{1,0:T(8,128)(2,1)S(1)}, u32[]{:S(2)}, u32[]{:S(2)}) collective-permute-start(bf16[48,1536]{1,0:T(8,128)(2,1)S(1)} %get-tuple-element.168), channel_id=1, source_target_pairs={{0,24},{1,25},{2,26},{3,27},{4,28},{5,29},{6,30},{7,31},{8,16},{9,... | collective-permute-start | bytes 442376 | tf_op jit(solution)/shard_map/ppermute | solution.py:973
  202.1 17.4 %collective-permute-start.30 = (bf16[192,1920]{1,0:T(8,128)(2,1)S(1)}, bf16[192,1920]{1,0:T(8,128)(2,1)S(1)}, u32[]{:S(2)}, u32[]{:S(2)}) collective-permute-start(bf16[192,1920]{1,0:T(8,128)(2,1)S(1)} %sum_second.5), channel_id=1, source_target_pairs={{0,4},{1,3},{2,6},{3,1},{4,0},{5,7},{6,2},{7,5},{8,12},{9,11},{10,... | collective-permute-start | bytes 2211848 | tf_op jit(solution)/shard_map/ppermute | solution.py:973
  202.1 17.4 %collective-permute-start.29 = (bf16[384,768]{1,0:T(8,128)(2,1)S(1)}, bf16[384,768]{1,0:T(8,128)(2,1)S(1)}, u32[]{:S(2)}, u32[]{:S(2)}) collective-permute-start(bf16[384,768]{1,0:T(8,128)(2,1)S(1)} %sum_first.6), channel_id=1, source_target_pairs={{0,2},{1,5},{2,0},{3,7},{4,6},{5,1},{6,4},{7,3},{8,10},{9,13},{10,... | collective-permute-start | bytes 1769480 | tf_op jit(solution)/shard_map/ppermute | solution.py:973
  225.1 12.3 %collective-permute-start.34 = (bf16[768,768]{1,0:T(8,128)(2,1)S(1)}, bf16[768,768]{1,0:T(8,128)(2,1)S(1)}, u32[]{:S(2)}, u32[]{:S(2)}) collective-permute-start(bf16[768,768]{1,0:T(8,128)(2,1)S(1)} %rows_product.15), channel_id=1, source_target_pairs={{0,1},{1,0},{2,3},{3,2},{4,5},{5,4},{6,7},{7,6},{8,9},{9,8},{10,11... | collective-permute-start | bytes 3538952 | tf_op jit(solution)/shard_map/ppermute | solution.py:985
  225.2 12.2 %collective-permute-start.35 = (bf16[420,384]{1,0:T(8,128)(2,1)S(1)}, bf16[420,384]{1,0:T(8,128)(2,1)S(1)}, u32[]{:S(2)}, u32[]{:S(2)}) collective-permute-start(bf16[420,384]{1,0:T(8,128)(2,1)S(1)} %sum_first.7), channel_id=1, source_target_pairs={{0,2},{1,5},{2,0},{3,7},{4,6},{5,1},{6,4},{7,3},{8,10},{9,13},{10,... | collective-permute-start | bytes 967688 | tf_op jit(solution)/shard_map/ppermute | solution.py:973
  227.1 19.2 %collective-permute-start.38 = (bf16[48,1920]{1,0:T(8,128)(2,1)S(1)}, bf16[48,1920]{1,0:T(8,128)(2,1)S(1)}, u32[]{:S(2)}, u32[]{:S(2)}) collective-permute-start(bf16[48,1920]{1,0:T(8,128)(2,1)S(1)} %get-tuple-element.181), channel_id=1, source_target_pairs={{0,8},{1,9},{2,10},{3,11},{4,12},{5,13},{6,14},{7,15},{8,0},{9,1},... | collective-permute-start | bytes 552968 | tf_op jit(solution)/shard_map/ppermute | solution.py:973
  227.1 21.6 %collective-permute-start.39 = (bf16[48,1920]{1,0:T(8,128)(2,1)S(1)}, bf16[48,1920]{1,0:T(8,128)(2,1)S(1)}, u32[]{:S(2)}, u32[]{:S(2)}) collective-permute-start(bf16[48,1920]{1,0:T(8,128)(2,1)S(1)} %get-tuple-element.182), channel_id=1, source_target_pairs={{0,16},{1,17},{2,18},{3,19},{4,20},{5,21},{6,22},{7,23},{8,24},{9,... | collective-permute-start | bytes 552968 | tf_op jit(solution)/shard_map/ppermute | solution.py:973
  234.9 13.8 %collective-permute-start.40 = (bf16[48,1920]{1,0:T(8,128)(2,1)S(1)}, bf16[48,1920]{1,0:T(8,128)(2,1)S(1)}, u32[]{:S(2)}, u32[]{:S(2)}) collective-permute-start(bf16[48,1920]{1,0:T(8,128)(2,1)S(1)} %get-tuple-element.183), channel_id=1, source_target_pairs={{0,24},{1,25},{2,26},{3,27},{4,28},{5,29},{6,30},{7,31},{8,16},{9,... | collective-permute-start | bytes 552968 | tf_op jit(solution)/shard_map/ppermute | solution.py:973
  244.4 13.1 %collective-permute-start.42 = (bf16[60,1152]{1,0:T(8,128)(2,1)S(1)}, bf16[60,1152]{1,0:T(8,128)(2,1)S(1)}, u32[]{:S(2)}, u32[]{:S(2)}) collective-permute-start(bf16[60,1152]{1,0:T(8,128)(2,1)S(1)} %get-tuple-element.205), channel_id=1, source_target_pairs={{0,16},{1,17},{2,18},{3,19},{4,20},{5,21},{6,22},{7,23},{8,24},{9,... | collective-permute-start | bytes 414728 | tf_op jit(solution)/shard_map/ppermute | solution.py:973
  246.3 11.2 %collective-permute-start.43 = (bf16[60,1152]{1,0:T(8,128)(2,1)S(1)}, bf16[60,1152]{1,0:T(8,128)(2,1)S(1)}, u32[]{:S(2)}, u32[]{:S(2)}) collective-permute-start(bf16[60,1152]{1,0:T(8,128)(2,1)S(1)} %get-tuple-element.206), channel_id=1, source_target_pairs={{0,24},{1,25},{2,26},{3,27},{4,28},{5,29},{6,30},{7,31},{8,16},{9,... | collective-permute-start | bytes 414728 | tf_op jit(solution)/shard_map/ppermute | solution.py:973
  (28 other events, 206.9 us)
where the time goes:
time: 260 us
  Pallas kernels  124 us (48%)
  waiting for transfers between devices  74 us (28%)
  starting transfers between devices  50 us (19%)
  local copies, waits for them, and re-layouts  7.96 us (3%)
  other arithmetic  3.25 us (1%)
    ppermute x35, waiting for transfers between devices, group_permute(): return lax.ppermute(value, ('deep', 'quad', 'head'), pairs)  69.4 us
    ppermute x35, starting transfers between devices, group_permute(): return lax.ppermute(value, ('deep', 'quad', 'head'), pairs)  48.7 us
    pallas_call x2, Pallas kernels, attention_backward(): pl.pallas_call(functools.partial(attn_bwd_kernel, pairs, position), out_s...  38.5 us
    pallas_call x8, Pallas kernels, rows_product(): pl.pallas_call(functools.partial(rows_kernel, window, columns_of(lefts)),...  16.2 us
    pallas_call x5, Pallas kernels, outer(): pl.pallas_call(functools.partial(outer_kernel, len(lefts)), out_shape=jax...  15.3 us
    pallas_call x1, Pallas kernels, attention_forward(): pl.pallas_call(functools.partial(attn_fwd_kernel, range(pairs), position)...  13.7 us
    pallas_call x18, Pallas kernels, vmem_call(): pl.pallas_call(kernel, out_shape=outs, in_specs=[smem] * scalars + [vmem]...  11.2 us
    pallas_call x2, Pallas kernels, up_gelu(): pl.pallas_call(up_kernel, out_shape=(shape, shape), in_specs=[vmem] * 3,...  9.75 us
  transfers between devices with their start and end apart: 44, of which 15 were waited for; matrix products, arithmetic and copies ran while one was open for 2% of the time, Pallas kernels for 35%

commit v1 on v0

--- a/solution.py
+++ b/solution.py
@@ -726,17 +726,20 @@
     return cuts
 
 
-def sum_first_kernel(count, deep, at_ref, *refs):
+def sum_first_kernel(count, deep, apart, at_ref, *refs):
     totals, rest = refs[:count], refs[count:]
-    out_ref = rest[-1]
     rows = totals[0].shape[0] // (deep * QUAD)
-    for part, place in enumerate((1, 3)):
+    halves = [(1, 0), (3, deep * rows)]
+    if apart:
+        halves = [(1, 0), (3, 0)]
+    for part, (place, low) in enumerate(halves):
+        out_ref = rest[part - 2] if apart else rest[-1]
         for z in range(deep):
-            row = (part * deep + z) * rows
+            row = low + z * rows
             for total, cut in zip(totals, columns_of(totals)):
                 out_ref[row : row + rows, cut] = total[slab_at(at_ref, place, z, rows), :]
-    if len(rest) > 1:
-        pack_rows(out_ref, 2 * deep * rows, rest[0][...])
+    if len(rest) > 1 and not apart:
+        pack_rows(rest[-1], 2 * deep * rows, rest[0][...])
 
 
 def sum_second_kernel(count, deep, at_ref, *refs):
@@ -752,7 +755,7 @@
     for z in range(deep):
         for total, cut in zip(totals, columns_of(totals)):
             far = total[slab_at(at_ref, 2, z, rows), :].astype(jnp.float32)
-            row = (deep + z) * rows
+            row = z * rows + (deep * rows if got_ref.shape[0] >= 2 * deep * rows else 0)
             far = far + got_ref[row : row + rows, cut].astype(jnp.float32)
             out_ref[z * rows : (z + 1) * rows, cut] = far.astype(jnp.bfloat16)
 
@@ -802,6 +805,13 @@
         for answer in answers:
             small = small + unpack_rows(answer, rows, small_rows)
         new_ref[...] = small
+    if len(outs[0].shape) == 3:
+        kinds = outs[0].shape[0]
+        for n in range(own.shape[1] // PAIR):
+            pair, kind = n // kinds, n % kinds
+            cut = slice(pair * PAIR, (pair + 1) * PAIR)
+            outs[0][kind, :, cut] = own[:, n * PAIR : (n + 1) * PAIR]
+        return
     for out_ref, cut in zip(outs, columns_of(outs)):
         out_ref[...] = own[:, cut]
 
@@ -818,12 +828,18 @@
     )(*operands)
 
 
+def sum_first_apart(total, spot):
+    shape = (total.shape[0] // QUAD, total.shape[1])
+    kernel = functools.partial(sum_first_kernel, 1, spot.deep, True)
+    return vmem_call(kernel, [(shape, jnp.bfloat16)] * 2, [spot.at, total], "sum_first")
+
+
 def sum_first(totals, spot, small=None):
     span = totals[0].shape[0] // QUAD
     extra = 0 if small is None else 2 * small.shape[0]
     shape = (2 * span + extra, sum(t.shape[1] for t in totals))
     operands = [spot.at, *totals] + ([] if small is None else [small])
-    kernel = functools.partial(sum_first_kernel, len(totals), spot.deep)
+    kernel = functools.partial(sum_first_kernel, len(totals), spot.deep, False)
     return vmem_call(kernel, [(shape, jnp.bfloat16)], operands, "sum_first")[0]
 
 
@@ -862,6 +878,8 @@
     )
     operands = [own, *answers] + ([] if small is None else [small])
     outs = [((own.shape[0], w), jnp.float32) for w in widths]
+    if small is not None:
+        outs = [((3, own.shape[0], widths[0] // 3), jnp.float32)]
     outs += [] if small is None else [(small.shape, jnp.float32)]
     return vmem_call(kernel, outs, operands, "sum_last", scalars=0)
 
@@ -1002,24 +1020,32 @@
     return [deep_step(value, spot.deep, k) for k in range(1, spot.deep)]
 
 
-def place_kernel(deep, windows, at_ref, *refs):
+def place_kernel(deep, windows, kinds, at_ref, *refs):
     pieces, outs = refs[:QUAD], refs[QUAD:]
-    rows = pieces[0].shape[1]
+    rows = pieces[0].shape[1] // kinds
     for k in range(deep):
         for j, piece in enumerate(pieces):
             row = pl.multiple_of(((at_ref[QUAD] ^ k) * QUAD + at_ref[j]) * rows, rows)
+            at = pl.ds(row, rows)
+            if kinds > 1:
+                for n in range(kinds * piece.shape[2] // PAIR):
+                    pair, kind = n // kinds, n % kinds
+                    outs[0][at, n * PAIR : (n + 1) * PAIR] = piece[
+                        k, kind * rows : (kind + 1) * rows, pair * PAIR : (pair + 1) * PAIR
+                    ]
+                continue
             for out, (low, high) in zip(outs, windows):
-                out[pl.ds(row, rows), :] = piece[k, :, low:high]
-
-
-def place(spot, pieces, widths):
+                out[at, :] = piece[k, :, low:high]
+
+
+def place(spot, pieces, widths, kinds=1):
     windows, low = [], 0
     for width in widths:
         windows.append((low, low + width))
         low += width
-    deep, rows = pieces[0].shape[:2]
+    deep, rows = pieces[0].shape[0], pieces[0].shape[1] // kinds
     outs = [((deep * QUAD * rows, width), pieces[0].dtype) for width in widths]
-    kernel = functools.partial(place_kernel, deep, windows)
+    kernel = functools.partial(place_kernel, deep, windows, kinds)
     return vmem_call(kernel, outs, [spot.at, *pieces], "place_pieces", limit=8)
 
 
@@ -1084,9 +1110,9 @@
         return quad_step(block, deep, True)
 
     tokens_other = swap(inputs)
-    qkv_block = by_pair(qkv_weight)
     mid = jnp.concatenate([out_weight, up_weight], axis=1)
     if staged:
+        qkv_block = jnp.swapaxes(qkv_weight, 0, 1).reshape(3 * shard, head_width)
         qkv_pieces = deep_pieces(qkv_block, spot)
         mid_pieces = deep_pieces(after(mid, *qkv_pieces), spot)
         qkv_deep = jnp.stack([qkv_block] + qkv_pieces)
@@ -1095,14 +1121,16 @@
             (qkv_other, qkv_far, *mid_pieces)
         )
         qkv_across = second_quad(qkv_other)
-        (full_qkv,) = place(spot, (qkv_deep, qkv_other, qkv_far, qkv_across), [3 * head_width])
+        (full_qkv,) = place(
+            spot, (qkv_deep, qkv_other, qkv_far, qkv_across), [3 * head_width], kinds=3
+        )
         full_qkv, *mid_pieces = lax.optimization_barrier((full_qkv, *mid_pieces))
         mid_deep = jnp.stack([mid] + mid_pieces)
         mid_other, mid_far = first_quad(mid_deep), second_quad(mid_deep)
         full_qkv, mid_deep = lax.optimization_barrier((full_qkv, mid_deep))
         down_pieces = deep_pieces(after(down_weight, *mid_pieces), spot)
     else:
-        full_qkv = gathered_whole(qkv_block)
+        full_qkv = gathered_whole(by_pair(qkv_weight))
         full_mid = gathered_whole(mid)
         full_out, full_up = full_mid[:, :head_width], full_mid[:, head_width:]
         full_down = gathered_whole(down_weight)
@@ -1116,11 +1144,12 @@
         )
         mid_across = second_quad(mid_other)
         down_deep = jnp.stack([down_weight] + down_pieces)
+        down_other, down_far = first_quad(down_deep), second_quad(down_deep)
+        mid_across, down_other = lax.optimization_barrier((mid_across, down_other))
+        down_across = second_quad(down_other)
         full_out, full_up = place(
             spot, (mid_deep, mid_other, mid_far, mid_across), [head_width, up_width]
         )
-        full_out, down_deep = lax.optimization_barrier((full_out, down_deep))
-        down_other, down_far = first_quad(down_deep), second_quad(down_deep)
 
     whole = (half, 2 * half)
     other = swap(rows_product([attended], full_out, whole, jnp.bfloat16))
@@ -1132,14 +1161,13 @@
     hidden_other = swap(hidden_own)
     active_own, slope_own = up_gelu(hidden_own, full_up, up_bias)
     if staged:
-        active_own, down_other, down_far = lax.optimization_barrier(
-            (active_own, down_other, down_far)
+        active_own, hidden_other, down_across = lax.optimization_barrier(
+            (active_own, hidden_other, down_across)
         )
-        down_across = second_quad(down_other)
     active_other, slope_other = up_gelu(hidden_other, full_up, up_bias)
     if staged:
-        active_other, active_own, down_across = lax.optimization_barrier(
-            (active_other, active_own, down_across)
+        active_other, active_own, down_far = lax.optimization_barrier(
+            (active_other, active_own, down_far)
         )
         (full_down,) = place(spot, (down_deep, down_other, down_far, down_across), [up_width])
     other = swap(rows_product([active_other], full_down, (0, half), jnp.bfloat16))
@@ -1158,9 +1186,10 @@
     grad_upper_own, up_sum_own = back_slope(grad_own, full_down, slope_own)
     down_local = outer([grad_own, grad_other], [active_own, active_other])
     if staged:
-        message = sum_first([down_local], spot)
-        down_got = first_quad(message)
-        grad_other, message = lax.optimization_barrier((grad_other, message))
+        near_message, far_message = sum_first_apart(down_local, spot)
+        down_far_got = first_quad(far_message)
+        grad_other, near_message = lax.optimization_barrier((grad_other, near_message))
+        down_got = first_quad(near_message)
     grad_upper_other, up_sum_other = back_slope(grad_other, full_down, slope_other)
     other = swap(rows_product([grad_upper_other], full_up, (0, half), jnp.bfloat16))
     up_local = outer([hidden_own, hidden_other], [grad_upper_own, grad_upper_other])
@@ -1168,8 +1197,8 @@
         rows_product([grad_upper_own], full_up, (0, half), jnp.float32), other, grad_res_two, normed_one, inverse_one, first_gain
     )
     if staged:
-        grad_proj_own, down_got = lax.optimization_barrier((grad_proj_own, down_got))
-        down_message = sum_second([down_local], spot, down_got)
+        grad_proj_own, down_far_got = lax.optimization_barrier((grad_proj_own, down_far_got))
+        down_message = sum_second([down_local], spot, down_far_got)
         down_two = second_quad(down_message)
         grad_proj_own, down_message = lax.optimization_barrier((grad_proj_own, down_message))
     grad_proj_other = swap(grad_proj_own)
@@ -1183,6 +1212,7 @@
     if staged:
         mid_message = sum_first(mids, spot)
         mid_got = first_quad(mid_message)
+        grad_attended, down_got = lax.optimization_barrier((grad_attended, down_got))
         grad_attended, mid_message = lax.optimization_barrier((grad_attended, mid_message))
     grads_a, sums_a = attention_backward(
         item_lengths, random_blocks, triple, grad_attended, range(split), position
@@ -1216,18 +1246,20 @@
         got_b = first_quad(message_b)
         message_a = sum_second([local_a], spot, after(got_a, message_b))
         two_a = second_quad(message_a)
-        mid_got, message_a = lax.optimization_barrier((mid_got, message_a))
+        grads_a, grads_b, message_a = lax.optimization_barrier((grads_a, grads_b, message_a))
+    product = rows_product([grads_a, grads_b], full_qkv, whole, jnp.bfloat16)
+    if staged:
+        mid_got, product = lax.optimization_barrier((mid_got, product))
         mid_sum, *messages = sum_deep([mids], spot, [mid_got], [mid_two])
         mid_answers = [deep_step(m, deep, k + 1) for k, m in enumerate(messages)]
-        grads_a, grads_b, *messages = lax.optimization_barrier((grads_a, grads_b, *messages))
-
-    other = swap(rows_product([grads_a, grads_b], full_qkv, whole, jnp.bfloat16))
-    mine = rows_product([grads_a, grads_b], full_qkv, (0, half), jnp.float32)
+        product, *messages = lax.optimization_barrier((product, *messages))
+    other = swap(product)
     if staged:
-        mine, other, got_b, two_a = lax.optimization_barrier((mine, other, got_b, two_a))
+        grads_a, other, got_b, two_a = lax.optimization_barrier((grads_a, other, got_b, two_a))
         message, small = sum_second([local_b], spot, got_b, small)
         two_b = second_quad(message)
-        other, message = lax.optimization_barrier((other, message))
+        grads_a, message = lax.optimization_barrier((grads_a, message))
+    mine = rows_product([grads_a, grads_b], full_qkv, (0, half), jnp.float32)
     input_grad = low(mine + other.astype(jnp.float32) + grad_res_one)
     if staged:
         (grad_down,) = sum_last(down_sum, down_answers, [up_width])
@@ -1239,9 +1271,10 @@
         grad_out, grad_up = sum_last(mid_sum, mid_answers, [head_width, up_width])
         grad_out, grad_up, *answers = lax.optimization_barrier((grad_out, grad_up, *answers))
         grad_qkv, small = sum_last(qkv_sum, answers, [3 * head_width], small)
+        grad_qkv = jnp.swapaxes(grad_qkv, 0, 1)
     else:
         grad_down, grad_up, grad_out = (scattered(v) for v in (down_local, up_local, out_local))
-        grad_qkv = scattered(jnp.concatenate([local_a, local_b], axis=1))
+        grad_qkv = by_kind(scattered(jnp.concatenate([local_a, local_b], axis=1)), 3)
         small = lax.psum(small, every)
         part = small.shape[0] // 3
         small = jnp.concatenate([small[n * part : (n + 1) * part] for n in range(3)], axis=1)
@@ -1253,7 +1286,7 @@
     return (
         layer_out,
         input_grad,
-        by_kind(grad_qkv, 3),
+        grad_qkv,
         grad_qv_bias,
         grad_out,
         totals[0],

time: 260 us -> 250 us (0.962)
  waiting for transfers between devices: 74 us -> 62.6 us
  starting transfers between devices: 50 us -> 53.1 us
    ppermute x35 -> x36, waiting for transfers between devices: 69.4 us -> 58 us  [group_permute(): return lax.ppermute(value, ('deep', 'quad', 'head'), pairs)]
    ppermute x35 -> x36, starting transfers between devices: 48.7 us -> 52.2 us  [group_permute(): return lax.ppermute(value, ('deep', 'quad', 'head'), pairs)]
  transfers between devices with their start and end apart: 44 -> 45, of which waited for: 15 -> 17; matrix products, arithmetic and copies ran while one was open for 2% -> 3% of each run, Pallas kernels for 35% -> 36%
where the time goes in v1:
time: 250 us
  Pallas kernels  122 us (49%)
  waiting for transfers between devices  62.6 us (25%)
  starting transfers between devices  53.1 us (21%)
  local copies, waits for them, and re-layouts  6.5 us (3%)
  other arithmetic  4.19 us (2%)
    ppermute x36, waiting for transfers between devices, group_permute(): return lax.ppermute(value, ('deep', 'quad', 'head'), pairs)  58 us
    ppermute x36, starting transfers between devices, group_permute(): return lax.ppermute(value, ('deep', 'quad', 'head'), pairs)  52.2 us
    pallas_call x2, Pallas kernels, attention_backward(): pl.pallas_call(functools.partial(attn_bwd_kernel, pairs, position), out_s...  36.5 us
    pallas_call x8, Pallas kernels, rows_product(): pl.pallas_call(functools.partial(rows_kernel, window, columns_of(lefts)),...  16.2 us
    pallas_call x5, Pallas kernels, outer(): pl.pallas_call(functools.partial(outer_kernel, len(lefts)), out_shape=jax...  15.3 us
    pallas_call x1, Pallas kernels, attention_forward(): pl.pallas_call(functools.partial(attn_fwd_kernel, range(pairs), position)...  13 us
    pallas_call x18, Pallas kernels, vmem_call(): pl.pallas_call(kernel, out_shape=outs, in_specs=[smem] * scalars + [vmem]...  12 us
    pallas_call x2, Pallas kernels, up_gelu(): pl.pallas_call(up_kernel, out_shape=(shape, shape), in_specs=[vmem] * 3,...  9.75 us
  transfers between devices with their start and end apart: 45, of which 17 were waited for; matrix products, arithmetic and copies ran while one was open for 3% of the time, Pallas kernels for 36%

profile of v1, /device:TPU:0, one launch (start us, length us, event | category | flops | bytes accessed | tf_op | source)
XLA Modules:
  0.0 249.7 jit_solution(1481501452686503105)
XLA Ops:
  0.6 3.1 %collective-permute-start.1 = (bf16[144,384]{1,0:T(8,128)(2,1)}, bf16[144,384]{1,0:T(8,128)(2,1)S(1)}, u32[]{:S(2)}, u32[]{:S(2)}) collective-permute-start(bf16[144,384]{1,0:T(8,128)(2,1)} %bitcast.35), channel_id=1, source_target_pairs={{0,8},{1,9},{2,10},{3,11},{4,12},{5,13},{6,14},{7,15},{8,0},{9,1},... | collective-permute-start | bytes 331784 | tf_op jit(solution)/shard_map/ppermute | solution.py:991
  3.7 2.6 %collective-permute-start.2 = (bf16[144,384]{1,0:T(8,128)(2,1)}, bf16[144,384]{1,0:T(8,128)(2,1)S(1)}, u32[]{:S(2)}, u32[]{:S(2)}) collective-permute-start(bf16[144,384]{1,0:T(8,128)(2,1)} %bitcast.36), channel_id=1, source_target_pairs={{0,16},{1,17},{2,18},{3,19},{4,20},{5,21},{6,22},{7,23},{8,24},{9,... | collective-permute-start | bytes 331784 | tf_op jit(solution)/shard_map/ppermute | solution.py:991
  7.1 8.2 %collective-permute-done.2 = bf16[144,384]{1,0:T(8,128)(2,1)S(1)} collective-permute-done((bf16[144,384]{1,0:T(8,128)(2,1)}, bf16[144,384]{1,0:T(8,128)(2,1)S(1)}, u32[]{:S(2)}, u32[]{:S(2)}) %collective-permute-start.2) | collective-permute-done | bytes 110624 | tf_op jit(solution)/shard_map/ppermute | solution.py:991
  23.4 4.3 %collective-permute-done.6 = bf16[48,1920]{1,0:T(8,128)(2,1)S(1)} collective-permute-done((bf16[48,1920]{1,0:T(8,128)(2,1)S(1)}, bf16[48,1920]{1,0:T(8,128)(2,1)S(1)}, u32[]{:S(2)}, u32[]{:S(2)}) %collective-permute-start.6) | collective-permute-done | bytes 184352 | tf_op jit(solution)/shard_map/ppermute | solution.py:991
  29.8 7.3 %collective-permute-done.7 = bf16[48,1920]{1,0:T(8,128)(2,1)S(1)} collective-permute-done((bf16[48,1920]{1,0:T(8,128)(2,1)S(1)}, bf16[48,1920]{1,0:T(8,128)(2,1)S(1)}, u32[]{:S(2)}, u32[]{:S(2)}) %collective-permute-start.7) | collective-permute-done | bytes 184352 | tf_op jit(solution)/shard_map/ppermute | solution.py:991
  40.2 6.0 %collective-permute-done.9.refs_3_ = bf16[4,144,384]{2,1,0:T(8,128)(2,1)S(1)} collective-permute-done((bf16[4,144,384]{2,1,0:T(8,128)(2,1)S(1)}, bf16[4,144,384]{2,1,0:T(8,128)(2,1)S(1)}, u32[]{:S(2)}, u32[]{:S(2)}) %collective-permute-start.9) | collective-permute-done | bytes 442400 | tf_op jit(solution)/shard_map/ppermute | solution.py:991
  47.1 2.7 %collective-permute-start.12 = (bf16[48,1536]{1,0:T(8,128)(2,1)S(1)}, bf16[48,1536]{1,0:T(8,128)(2,1)S(1)}, u32[]{:S(2)}, u32[]{:S(2)}) collective-permute-start(bf16[48,1536]{1,0:T(8,128)(2,1)S(1)} %copy-done.7), channel_id=1, source_target_pairs={{0,8},{1,9},{2,10},{3,11},{4,12},{5,13},{6,14},{7,15},{8,0},{9,1},... | collective-permute-start | bytes 442376 | tf_op jit(solution)/shard_map/ppermute | solution.py:991
  53.4 4.2 %triple.1.tri_ref = bf16[1536,1152]{1,0:T(8,128)(2,1)S(1)} custom-call(bf16[768,768]{1,0:T(8,128)(2,1)S(1)} %copy-done, bf16[768,768]{1,0:T(8,128)(2,1)S(1)} %collective-permute-done.other_ref.refs_1_, bf16[768,1152]{1,0:T(8,128)(2,1)S(1)} %place_pieces.3.weight_ref.refs_2_, f32[1,1152]{1,0:T(1,128)S(1)} %reshape_reshape.3.bias_ref), custom_call_target="tpu_custom_call" | custom-call | flops 2717908992 | bytes 7667712 | tf_op jit(solution)/shard_map/triple/pallas_call | solution.py:966
  57.6 13.0 %attend_forward.1.refs_0_.refs_2_ = bf16[1536,384]{1,0:T(8,128)(2,1)S(1)} custom-call(s32[1,2]{1,0:T(1,128)S(1)} %copy-done.2, s32[1,6,24,3]{3,2,1,0:T(8,128)S(1)} %copy.35.rb_ref, bf16[1536,1152]{1,0:T(8,128)(2,1)S(1)} %triple.1.tri_ref), custom_call_target="tpu_custom_call" | custom-call | flops 9663676416 | bytes 4718592 | tf_op jit(solution)/shard_map/attend_forward/pallas_call | solution.py:395
  74.0 10.3 %collective-permute-done.16.refs_1_ = bf16[4,48,1536]{2,1,0:T(8,128)(2,1)S(1)} collective-permute-done((bf16[4,48,1536]{2,1,0:T(8,128)(2,1)S(1)}, bf16[4,48,1536]{2,1,0:T(8,128)(2,1)S(1)}, u32[]{:S(2)}, u32[]{:S(2)}) %collective-permute-start.16) | collective-permute-done | bytes 589856 | tf_op jit(solution)/shard_map/ppermute | solution.py:991
  94.5 4.9 %up_gelu.2 = (bf16[768,1536]{1,0:T(8,128)(2,1)S(1)}, bf16[768,1536]{1,0:T(8,128)(2,1)S(1)}) custom-call(bf16[768,768]{1,0:T(8,128)(2,1)S(1)} %get-tuple-element.236.rows_ref.refs_0_, bf16[768,1536]{1,0:T(8,128)(2,1)S(1)} %get-tuple-element.143.weight_ref.refs_1_, f32[1,1536]{1,0:T(1,128)S(1)} %reshape.72.bias_ref), custom_call_target="tpu_custom_call" | custom-call | flops 1811939328 | bytes 8257536 | tf_op jit(solution)/shard_map/up_gelu/pallas_call | solution.py:477
  99.4 3.0 %collective-permute-done.19.refs_3_ = bf16[4,48,1536]{2,1,0:T(8,128)(2,1)S(1)} collective-permute-done((bf16[4,48,1536]{2,1,0:T(8,128)(2,1)S(1)}, bf16[4,48,1536]{2,1,0:T(8,128)(2,1)S(1)}, u32[]{:S(2)}, u32[]{:S(2)}) %collective-permute-start.19) | collective-permute-done | bytes 589856 | tf_op jit(solution)/shard_map/ppermute | solution.py:991
  102.3 4.9 %up_gelu.3 = (bf16[768,1536]{1,0:T(8,128)(2,1)S(1)}, bf16[768,1536]{1,0:T(8,128)(2,1)S(1)}) custom-call(bf16[768,768]{1,0:T(8,128)(2,1)S(1)} %collective-permute-done.18.rows_ref.refs_1_, bf16[768,1536]{1,0:T(8,128)(2,1)S(1)} %get-tuple-element.143.weight_ref.refs_1_, f32[1,1536]{1,0:T(1,128)S(1)} %reshape.72.bias_ref), custom_call_target="tpu_custom_call" | custom-call | flops 1811939328 | bytes 8257536 | tf_op jit(solution)/shard_map/up_gelu/pallas_call | solution.py:477
  112.0 2.4 rows_product.10.down_ref
  114.7 5.4 %norm_two.1 = (bf16[768,768]{1,0:T(8,128)(2,1)}, f32[768,768]{1,0:T(8,128)S(1)}, bf16[768,768]{1,0:T(8,128)(2,1)S(1)}, f32[8,768]{1,0:T(8,128)S(1)}) custom-call(s32[1,2]{1,0:T(1,128)S(1)} %copy-done.2, f32[768,768]{1,0:T(8,128)S(1)} %rows_product.10.down_ref, bf16[768,768]{1,0:T(8,128)(2,1)S(1)} %collective-permute-done.21.other_ref, ...), custom_call_target="tpu_custom_call" | custom-call | flops 23592960 | bytes 11796480 | tf_op jit(solution)/shard_map/norm_two/pallas_call | solution.py:641
  120.4 2.6 %collective-permute-done.22.refs_1_.grad_ref = bf16[768,768]{1,0:T(8,128)(2,1)S(1)} collective-permute-done((bf16[768,768]{1,0:T(8,128)(2,1)S(1)}, bf16[768,768]{1,0:T(8,128)(2,1)S(1)}, u32[]{:S(2)}, u32[]{:S(2)}) %collective-permute-start.22) | collective-permute-done | bytes 1179680 | tf_op jit(solution)/shard_map/ppermute | solution.py:1003
  123.0 4.9 %outer.5.refs_0_ = bf16[768,1536]{1,0:T(8,128)(2,1)S(1)} custom-call(bf16[768,768]{1,0:T(8,128)(2,1)S(1)} %get-tuple-element.154.grad_ref.refs_0_, bf16[768,768]{1,0:T(8,128)(2,1)S(1)} %collective-permute-done.22.refs_1_.grad_ref, bf16[768,1536]{1,0:T(8,128)(2,1)S(1)} %get-tuple-element.149.refs_0_.refs_2_, ...), custom_call_target="tpu_custom_call" | custom-call | flops 3623878656 | bytes 7077888 | tf_op jit(solution)/shard_map/outer/pallas_call | solution.py:554
  128.6 3.1 %back_slope.3 = (bf16[768,1536]{1,0:T(8,128)(2,1)S(1)}, f32[8,1536]{1,0:T(8,128)S(1)}) custom-call(bf16[768,768]{1,0:T(8,128)(2,1)S(1)} %collective-permute-done.22.refs_1_.grad_ref, bf16[768,1536]{1,0:T(8,128)(2,1)S(1)} %place_pieces.5.refs_1_.weight_ref, bf16[768,1536]{1,0:T(8,128)(2,1)S(1)} %get-tuple-element.159.slope_ref), custom_call_target="tpu_custom_call" | custom-call | flops 1811939328 | bytes 8257536 | tf_op jit(solution)/shard_map/back_slope/pallas_call | solution.py:511
  131.8 2.4 rows_product.13
  135.6 2.9 %back_slope.2 = (bf16[768,1536]{1,0:T(8,128)(2,1)S(1)}, f32[8,1536]{1,0:T(8,128)S(1)}) custom-call(bf16[768,768]{1,0:T(8,128)(2,1)S(1)} %get-tuple-element.154.grad_ref.refs_0_, bf16[768,1536]{1,0:T(8,128)(2,1)S(1)} %place_pieces.5.refs_1_.weight_ref, bf16[768,1536]{1,0:T(8,128)(2,1)S(1)} %get-tuple-element.155.slope_ref), custom_call_target="tpu_custom_call" | custom-call | flops 1811939328 | bytes 8257536 | tf_op jit(solution)/shard_map/back_slope/pallas_call | solution.py:511
  138.6 2.4 rows_product.12.own_ref
  146.2 5.0 %outer.7.refs_1_ = bf16[768,1536]{1,0:T(8,128)(2,1)S(1)} custom-call(bf16[768,768]{1,0:T(8,128)(2,1)S(1)} %get-tuple-element.236.rows_ref.refs_0_, bf16[768,768]{1,0:T(8,128)(2,1)S(1)} %collective-permute-done.18.rows_ref.refs_1_, bf16[768,1536]{1,0:T(8,128)(2,1)S(1)} %get-tuple-element.156.refs_0_.refs_2_, ...), custom_call_target="tpu_custom_call" | custom-call | flops 3623878656 | bytes 7077888 | tf_op jit(solution)/shard_map/outer/pallas_call | solution.py:554
  158.5 22.0 %attend_backward.2 = (bf16[1536,768]{1,0:T(8,128)(2,1)S(1)}, f32[8,256]{1,0:T(8,128)S(1)}) custom-call(s32[1,2]{1,0:T(1,128)S(1)} %copy-done.2, s32[1,6,24,3]{3,2,1,0:T(8,128)S(1)} %copy.35.rb_ref, bf16[1536,1152]{1,0:T(8,128)(2,1)S(1)} %triple.1.tri_ref, bf16[1536,384]{1,0:T(8,128)(2,1)S(1)} %project_both.1.grad_ref), custom_call_target="tpu_custom_call" | custom-call | flops 16106127360 | bytes 7864320 | tf_op jit(solution)/shard_map/attend_backward/pallas_call | solution.py:414
  181.3 2.5 %outer.8.refs_0_ = bf16[768,768]{1,0:T(8,128)(2,1)S(1)} custom-call(bf16[768,768]{1,0:T(8,128)(2,1)S(1)} %copy-done, bf16[768,768]{1,0:T(8,128)(2,1)S(1)} %collective-permute-done.other_ref.refs_1_, bf16[1536,768]{1,0:T(8,128)(2,1)S(1)} %get-tuple-element.203.refs_2_.refs_0_), custom_call_target="tpu_custom_call" | custom-call | flops 1811939328 | bytes 4718592 | tf_op jit(solution)/shard_map/outer/pallas_call | solution.py:554
  185.1 2.6 %collective-permute-start.32 = (bf16[48,1536]{1,0:T(8,128)(2,1)S(1)}, bf16[48,1536]{1,0:T(8,128)(2,1)S(1)}, u32[]{:S(2)}, u32[]{:S(2)}) collective-permute-start(bf16[48,1536]{1,0:T(8,128)(2,1)S(1)} %get-tuple-element.178), channel_id=1, source_target_pairs={{0,8},{1,9},{2,10},{3,11},{4,12},{5,13},{6,14},{7,15},{8,0},{9,1},... | collective-permute-start | bytes 442376 | tf_op jit(solution)/shard_map/ppermute | solution.py:991
  190.5 3.5 %collective-permute-start.31 = (bf16[192,1920]{1,0:T(8,128)(2,1)S(1)}, bf16[192,1920]{1,0:T(8,128)(2,1)S(1)}, u32[]{:S(2)}, u32[]{:S(2)}) collective-permute-start(bf16[192,1920]{1,0:T(8,128)(2,1)S(1)} %sum_second.5), channel_id=1, source_target_pairs={{0,4},{1,3},{2,6},{3,1},{4,0},{5,7},{6,2},{7,5},{8,12},{9,11},{10,... | collective-permute-start | bytes 2211848 | tf_op jit(solution)/shard_map/ppermute | solution.py:991
  194.3 14.5 %attend_backward.3 = (bf16[1536,384]{1,0:T(8,128)(2,1)S(1)}, f32[8,128]{1,0:T(8,128)S(1)}) custom-call(s32[1,2]{1,0:T(1,128)S(1)} %copy-done.2, s32[1,6,24,3]{3,2,1,0:T(8,128)S(1)} %copy.35.rb_ref, bf16[1536,1152]{1,0:T(8,128)(2,1)S(1)} %triple.1.tri_ref, bf16[1536,384]{1,0:T(8,128)(2,1)S(1)} %project_both.1.grad_ref), custom_call_target="tpu_custom_call" | custom-call | flops 8053063680 | bytes 3932160 | tf_op jit(solution)/shard_map/attend_backward/pallas_call | solution.py:414
  216.2 2.8 %collective-permute-start.40 = (bf16[48,1920]{1,0:T(8,128)(2,1)S(1)}, bf16[48,1920]{1,0:T(8,128)(2,1)S(1)}, u32[]{:S(2)}, u32[]{:S(2)}) collective-permute-start(bf16[48,1920]{1,0:T(8,128)(2,1)S(1)} %get-tuple-element.197), channel_id=1, source_target_pairs={{0,16},{1,17},{2,18},{3,19},{4,20},{5,21},{6,22},{7,23},{8,24},{9,... | collective-permute-start | bytes 552968 | tf_op jit(solution)/shard_map/ppermute | solution.py:991
  219.8 4.4 %collective-permute-done.37.refs_4_ = bf16[192,768]{1,0:T(8,128)(2,1)S(1)} collective-permute-done((bf16[192,768]{1,0:T(8,128)(2,1)S(1)}, bf16[192,768]{1,0:T(8,128)(2,1)S(1)}, u32[]{:S(2)}, u32[]{:S(2)}) %collective-permute-start.37) | collective-permute-done | bytes 294944 | tf_op jit(solution)/shard_map/ppermute | solution.py:991
  224.2 3.1 %collective-permute-start.41 = (bf16[48,1920]{1,0:T(8,128)(2,1)S(1)}, bf16[48,1920]{1,0:T(8,128)(2,1)S(1)}, u32[]{:S(2)}, u32[]{:S(2)}) collective-permute-start(bf16[48,1920]{1,0:T(8,128)(2,1)S(1)} %get-tuple-element.198), channel_id=1, source_target_pairs={{0,24},{1,25},{2,26},{3,27},{4,28},{5,29},{6,30},{7,31},{8,16},{9,... | collective-permute-start | bytes 552968 | tf_op jit(solution)/shard_map/ppermute | solution.py:991
  235.6 3.1 %collective-permute-start.44 = (bf16[60,1152]{1,0:T(8,128)(2,1)S(1)}, bf16[60,1152]{1,0:T(8,128)(2,1)S(1)}, u32[]{:S(2)}, u32[]{:S(2)}) collective-permute-start(bf16[60,1152]{1,0:T(8,128)(2,1)S(1)} %get-tuple-element.220), channel_id=1, source_target_pairs={{0,24},{1,25},{2,26},{3,27},{4,28},{5,29},{6,30},{7,31},{8,16},{9,... | collective-permute-start | bytes 414728 | tf_op jit(solution)/shard_map/ppermute | solution.py:991
  240.1 7.1 %collective-permute-done.43.refs_2_ = bf16[60,1152]{1,0:T(8,128)(2,1)S(1)} collective-permute-done((bf16[60,1152]{1,0:T(8,128)(2,1)S(1)}, bf16[60,1152]{1,0:T(8,128)(2,1)S(1)}, u32[]{:S(2)}, u32[]{:S(2)}) %collective-permute-start.43) | collective-permute-done | bytes 138272 | tf_op jit(solution)/shard_map/ppermute | solution.py:991
  (160 shorter events, 77.1 us)
Async XLA Ops:
  3.7 11.6 %collective-permute-start.2 = (bf16[144,384]{1,0:T(8,128)(2,1)}, bf16[144,384]{1,0:T(8,128)(2,1)S(1)}, u32[]{:S(2)}, u32[]{:S(2)}) collective-permute-start(bf16[144,384]{1,0:T(8,128)(2,1)} %bitcast.36), channel_id=1, source_target_pairs={{0,16},{1,17},{2,18},{3,19},{4,20},{5,21},{6,22},{7,23},{8,24},{9,... | collective-permute-start | bytes 331784 | tf_op jit(solution)/shard_map/ppermute | solution.py:991
  6.3 46.6 %collective-permute-start = (bf16[768,768]{1,0:T(8,128)(2,1)}, bf16[768,768]{1,0:T(8,128)(2,1)S(1)}, u32[]{:S(2)}, u32[]{:S(2)}) collective-permute-start(bf16[768,768]{1,0:T(8,128)(2,1)} %refs_0_.3), channel_id=1, source_target_pairs={{0,1},{1,0},{2,3},{3,2},{4,5},{5,4},{6,7},{7,6},{8,9},{9,8},{10,11... | collective-permute-start | bytes 3538952 | tf_op jit(solution)/shard_map/ppermute | solution.py:1003
  16.3 20.9 %collective-permute-start.4 = (bf16[4,144,384]{2,1,0:T(8,128)(2,1)S(1)}, bf16[4,144,384]{2,1,0:T(8,128)(2,1)S(1)}, u32[]{:S(2)}, u32[]{:S(2)}) collective-permute-start(bf16[4,144,384]{2,1,0:T(8,128)(2,1)S(1)} %pad_maximum_fusion.2.refs_0_), channel_id=1, source_target_pairs={{0,2},{1,5},{2,0},{3,7},{4,6},{5,1},{6,4},{7,3},{8,10},{9,13},{10,... | collective-permute-start | bytes 1327112 | tf_op jit(solution)/shard_map/ppermute | solution.py:991
  17.9 20.0 %collective-permute-start.5 = (bf16[4,144,384]{2,1,0:T(8,128)(2,1)S(1)}, bf16[4,144,384]{2,1,0:T(8,128)(2,1)S(1)}, u32[]{:S(2)}, u32[]{:S(2)}) collective-permute-start(bf16[4,144,384]{2,1,0:T(8,128)(2,1)S(1)} %pad_maximum_fusion.2.refs_0_), channel_id=1, source_target_pairs={{0,4},{1,3},{2,6},{3,1},{4,0},{5,7},{6,2},{7,5},{8,12},{9,11},{10,... | collective-permute-start | bytes 1327112 | tf_op jit(solution)/shard_map/ppermute | solution.py:991
  22.2 15.0 %collective-permute-start.7 = (bf16[48,1920]{1,0:T(8,128)(2,1)S(1)}, bf16[48,1920]{1,0:T(8,128)(2,1)S(1)}, u32[]{:S(2)}, u32[]{:S(2)}) collective-permute-start(bf16[48,1920]{1,0:T(8,128)(2,1)S(1)} %constant_dynamic-update-slice_fusion), channel_id=1, source_target_pairs={{0,16},{1,17},{2,18},{3,19},{4,20},{5,21},{6,22},{7,23},{8,24},{9,... | collective-permute-start | bytes 552968 | tf_op jit(solution)/shard_map/ppermute | solution.py:991
  47.1 23.6 %collective-permute-start.12 = (bf16[48,1536]{1,0:T(8,128)(2,1)S(1)}, bf16[48,1536]{1,0:T(8,128)(2,1)S(1)}, u32[]{:S(2)}, u32[]{:S(2)}) collective-permute-start(bf16[48,1536]{1,0:T(8,128)(2,1)S(1)} %copy-done.7), channel_id=1, source_target_pairs={{0,8},{1,9},{2,10},{3,11},{4,12},{5,13},{6,14},{7,15},{8,0},{9,1},... | collective-permute-start | bytes 442376 | tf_op jit(solution)/shard_map/ppermute | solution.py:991
  49.8 20.9 %collective-permute-start.13 = (bf16[48,1536]{1,0:T(8,128)(2,1)S(1)}, bf16[48,1536]{1,0:T(8,128)(2,1)S(1)}, u32[]{:S(2)}, u32[]{:S(2)}) collective-permute-start(bf16[48,1536]{1,0:T(8,128)(2,1)S(1)} %copy-done.7), channel_id=1, source_target_pairs={{0,16},{1,17},{2,18},{3,19},{4,20},{5,21},{6,22},{7,23},{8,24},{9,... | collective-permute-start | bytes 442376 | tf_op jit(solution)/shard_map/ppermute | solution.py:991
  50.8 19.9 %collective-permute-start.14 = (bf16[48,1536]{1,0:T(8,128)(2,1)S(1)}, bf16[48,1536]{1,0:T(8,128)(2,1)S(1)}, u32[]{:S(2)}, u32[]{:S(2)}) collective-permute-start(bf16[48,1536]{1,0:T(8,128)(2,1)S(1)} %copy-done.7), channel_id=1, source_target_pairs={{0,24},{1,25},{2,26},{3,27},{4,28},{5,29},{6,30},{7,31},{8,16},{9,... | collective-permute-start | bytes 442376 | tf_op jit(solution)/shard_map/ppermute | solution.py:991
  52.4 18.4 %collective-permute-start.10 = (bf16[4,48,1920]{2,1,0:T(8,128)(2,1)S(1)}, bf16[4,48,1920]{2,1,0:T(8,128)(2,1)S(1)}, u32[]{:S(2)}, u32[]{:S(2)}) collective-permute-start(bf16[4,48,1920]{2,1,0:T(8,128)(2,1)S(1)} %pad_maximum_fusion.refs_0_), channel_id=1, source_target_pairs={{0,2},{1,5},{2,0},{3,7},{4,6},{5,1},{6,4},{7,3},{8,10},{9,13},{10,... | collective-permute-start | bytes 2211848 | tf_op jit(solution)/shard_map/ppermute | solution.py:991
  53.0 17.8 %collective-permute-start.11 = (bf16[4,48,1920]{2,1,0:T(8,128)(2,1)S(1)}, bf16[4,48,1920]{2,1,0:T(8,128)(2,1)S(1)}, u32[]{:S(2)}, u32[]{:S(2)}) collective-permute-start(bf16[4,48,1920]{2,1,0:T(8,128)(2,1)S(1)} %pad_maximum_fusion.refs_0_), channel_id=1, source_target_pairs={{0,4},{1,3},{2,6},{3,1},{4,0},{5,7},{6,2},{7,5},{8,12},{9,11},{10,... | collective-permute-start | bytes 2211848 | tf_op jit(solution)/shard_map/ppermute | solution.py:991
  70.7 14.9 %collective-permute-start.15 = (bf16[4,48,1920]{2,1,0:T(8,128)(2,1)S(1)}, bf16[4,48,1920]{2,1,0:T(8,128)(2,1)S(1)}, u32[]{:S(2)}, u32[]{:S(2)}) collective-permute-start(bf16[4,48,1920]{2,1,0:T(8,128)(2,1)S(1)} %collective-permute-done.10.refs_1_), channel_id=1, source_target_pairs={{0,4},{1,3},{2,6},{3,1},{4,0},{5,7},{6,2},{7,5},{8,12},{9,11},{10,... | collective-permute-start | bytes 2211848 | tf_op jit(solution)/shard_map/ppermute | solution.py:991
  73.1 11.2 %collective-permute-start.16 = (bf16[4,48,1536]{2,1,0:T(8,128)(2,1)S(1)}, bf16[4,48,1536]{2,1,0:T(8,128)(2,1)S(1)}, u32[]{:S(2)}, u32[]{:S(2)}) collective-permute-start(bf16[4,48,1536]{2,1,0:T(8,128)(2,1)S(1)} %pad_maximum_fusion.1.refs_0_), channel_id=1, source_target_pairs={{0,2},{1,5},{2,0},{3,7},{4,6},{5,1},{6,4},{7,3},{8,10},{9,13},{10,... | collective-permute-start | bytes 1769480 | tf_op jit(solution)/shard_map/ppermute | solution.py:991
  92.3 10.1 %collective-permute-start.18 = (bf16[768,768]{1,0:T(8,128)(2,1)S(1)}, bf16[768,768]{1,0:T(8,128)(2,1)S(1)}, u32[]{:S(2)}, u32[]{:S(2)}) collective-permute-start(bf16[768,768]{1,0:T(8,128)(2,1)S(1)} %get-tuple-element.236.rows_ref.refs_0_), channel_id=1, source_target_pairs={{0,1},{1,0},{2,3},{3,2},{4,5},{5,4},{6,7},{7,6},{8,9},{9,8},{10,11... | collective-permute-start | bytes 3538952 | tf_op jit(solution)/shard_map/ppermute | solution.py:1003
  92.5 9.9 %collective-permute-start.19 = (bf16[4,48,1536]{2,1,0:T(8,128)(2,1)S(1)}, bf16[4,48,1536]{2,1,0:T(8,128)(2,1)S(1)}, u32[]{:S(2)}, u32[]{:S(2)}) collective-permute-start(bf16[4,48,1536]{2,1,0:T(8,128)(2,1)S(1)} %collective-permute-done.16.refs_1_), channel_id=1, source_target_pairs={{0,4},{1,3},{2,6},{3,1},{4,0},{5,7},{6,2},{7,5},{8,12},{9,11},{10,... | collective-permute-start | bytes 1769480 | tf_op jit(solution)/shard_map/ppermute | solution.py:991
  94.0 14.7 %collective-permute-start.20 = (bf16[4,48,1536]{2,1,0:T(8,128)(2,1)S(1)}, bf16[4,48,1536]{2,1,0:T(8,128)(2,1)S(1)}, u32[]{:S(2)}, u32[]{:S(2)}) collective-permute-start(bf16[4,48,1536]{2,1,0:T(8,128)(2,1)S(1)} %pad_maximum_fusion.1.refs_0_), channel_id=1, source_target_pairs={{0,4},{1,3},{2,6},{3,1},{4,0},{5,7},{6,2},{7,5},{8,12},{9,11},{10,... | collective-permute-start | bytes 1769480 | tf_op jit(solution)/shard_map/ppermute | solution.py:991
  134.4 9.9 %collective-permute-start.24 = (bf16[192,1536]{1,0:T(8,128)(2,1)S(1)}, bf16[192,1536]{1,0:T(8,128)(2,1)S(1)}, u32[]{:S(2)}, u32[]{:S(2)}) collective-permute-start(bf16[192,1536]{1,0:T(8,128)(2,1)S(1)} %get-tuple-element.163), channel_id=1, source_target_pairs={{0,2},{1,5},{2,0},{3,7},{4,6},{5,1},{6,4},{7,3},{8,10},{9,13},{10,... | collective-permute-start | bytes 1769480 | tf_op jit(solution)/shard_map/ppermute | solution.py:991
  145.1 10.5 %collective-permute-start.26 = (bf16[192,1536]{1,0:T(8,128)(2,1)S(1)}, bf16[192,1536]{1,0:T(8,128)(2,1)S(1)}, u32[]{:S(2)}, u32[]{:S(2)}) collective-permute-start(bf16[192,1536]{1,0:T(8,128)(2,1)S(1)} %get-tuple-element.167), channel_id=1, source_target_pairs={{0,2},{1,5},{2,0},{3,7},{4,6},{5,1},{6,4},{7,3},{8,10},{9,13},{10,... | collective-permute-start | bytes 1769480 | tf_op jit(solution)/shard_map/ppermute | solution.py:991
  151.1 29.4 %collective-permute-start.28 = (bf16[192,1536]{1,0:T(8,128)(2,1)S(1)}, bf16[192,1536]{1,0:T(8,128)(2,1)S(1)}, u32[]{:S(2)}, u32[]{:S(2)}) collective-permute-start(bf16[192,1536]{1,0:T(8,128)(2,1)S(1)} %sum_second.4), channel_id=1, source_target_pairs={{0,4},{1,3},{2,6},{3,1},{4,0},{5,7},{6,2},{7,5},{8,12},{9,11},{10,... | collective-permute-start | bytes 1769480 | tf_op jit(solution)/shard_map/ppermute | solution.py:991
  152.9 27.6 %collective-permute-start.29 = (f32[16,768]{1,0:T(8,128)S(1)}, f32[16,768]{1,0:T(8,128)S(1)}, u32[]{:S(2)}, u32[]{:S(2)}) collective-permute-start(f32[16,768]{1,0:T(8,128)S(1)} %constant_dynamic-update-slice_fusion.2.own_ref), channel_id=1, source_target_pairs={{0,1},{1,0},{2,3},{3,2},{4,5},{5,4},{6,7},{7,6},{8,9},{9,8},{10,11... | collective-permute-start | bytes 147464 | tf_op jit(solution)/shard_map/ppermute | solution.py:1003
  157.6 22.9 %collective-permute-start.27 = (bf16[384,1920]{1,0:T(8,128)(2,1)S(1)}, bf16[384,1920]{1,0:T(8,128)(2,1)S(1)}, u32[]{:S(2)}, u32[]{:S(2)}) collective-permute-start(bf16[384,1920]{1,0:T(8,128)(2,1)S(1)} %sum_first.5), channel_id=1, source_target_pairs={{0,2},{1,5},{2,0},{3,7},{4,6},{5,1},{6,4},{7,3},{8,10},{9,13},{10,... | collective-permute-start | bytes 4423688 | tf_op jit(solution)/shard_map/ppermute | solution.py:991
  185.1 23.7 %collective-permute-start.32 = (bf16[48,1536]{1,0:T(8,128)(2,1)S(1)}, bf16[48,1536]{1,0:T(8,128)(2,1)S(1)}, u32[]{:S(2)}, u32[]{:S(2)}) collective-permute-start(bf16[48,1536]{1,0:T(8,128)(2,1)S(1)} %get-tuple-element.178), channel_id=1, source_target_pairs={{0,8},{1,9},{2,10},{3,11},{4,12},{5,13},{6,14},{7,15},{8,0},{9,1},... | collective-permute-start | bytes 442376 | tf_op jit(solution)/shard_map/ppermute | solution.py:991
  187.7 21.1 %collective-permute-start.33 = (bf16[48,1536]{1,0:T(8,128)(2,1)S(1)}, bf16[48,1536]{1,0:T(8,128)(2,1)S(1)}, u32[]{:S(2)}, u32[]{:S(2)}) collective-permute-start(bf16[48,1536]{1,0:T(8,128)(2,1)S(1)} %get-tuple-element.179), channel_id=1, source_target_pairs={{0,16},{1,17},{2,18},{3,19},{4,20},{5,21},{6,22},{7,23},{8,24},{9,... | collective-permute-start | bytes 442376 | tf_op jit(solution)/shard_map/ppermute | solution.py:991
  189.9 18.9 %collective-permute-start.34 = (bf16[48,1536]{1,0:T(8,128)(2,1)S(1)}, bf16[48,1536]{1,0:T(8,128)(2,1)S(1)}, u32[]{:S(2)}, u32[]{:S(2)}) collective-permute-start(bf16[48,1536]{1,0:T(8,128)(2,1)S(1)} %get-tuple-element.180), channel_id=1, source_target_pairs={{0,24},{1,25},{2,26},{3,27},{4,28},{5,29},{6,30},{7,31},{8,16},{9,... | collective-permute-start | bytes 442376 | tf_op jit(solution)/shard_map/ppermute | solution.py:991
  190.5 18.4 %collective-permute-start.31 = (bf16[192,1920]{1,0:T(8,128)(2,1)S(1)}, bf16[192,1920]{1,0:T(8,128)(2,1)S(1)}, u32[]{:S(2)}, u32[]{:S(2)}) collective-permute-start(bf16[192,1920]{1,0:T(8,128)(2,1)S(1)} %sum_second.5), channel_id=1, source_target_pairs={{0,4},{1,3},{2,6},{3,1},{4,0},{5,7},{6,2},{7,5},{8,12},{9,11},{10,... | collective-permute-start | bytes 2211848 | tf_op jit(solution)/shard_map/ppermute | solution.py:991
  194.0 14.9 %collective-permute-start.30 = (bf16[384,768]{1,0:T(8,128)(2,1)S(1)}, bf16[384,768]{1,0:T(8,128)(2,1)S(1)}, u32[]{:S(2)}, u32[]{:S(2)}) collective-permute-start(bf16[384,768]{1,0:T(8,128)(2,1)S(1)} %sum_first.6), channel_id=1, source_target_pairs={{0,2},{1,5},{2,0},{3,7},{4,6},{5,1},{6,4},{7,3},{8,10},{9,13},{10,... | collective-permute-start | bytes 1769480 | tf_op jit(solution)/shard_map/ppermute | solution.py:991
  214.4 12.9 %collective-permute-start.35 = (bf16[768,768]{1,0:T(8,128)(2,1)S(1)}, bf16[768,768]{1,0:T(8,128)(2,1)S(1)}, u32[]{:S(2)}, u32[]{:S(2)}) collective-permute-start(bf16[768,768]{1,0:T(8,128)(2,1)S(1)} %rows_product.14), channel_id=1, source_target_pairs={{0,1},{1,0},{2,3},{3,2},{4,5},{5,4},{6,7},{7,6},{8,9},{9,8},{10,11... | collective-permute-start | bytes 3538952 | tf_op jit(solution)/shard_map/ppermute | solution.py:1003
  214.5 12.8 %collective-permute-start.36 = (bf16[420,384]{1,0:T(8,128)(2,1)S(1)}, bf16[420,384]{1,0:T(8,128)(2,1)S(1)}, u32[]{:S(2)}, u32[]{:S(2)}) collective-permute-start(bf16[420,384]{1,0:T(8,128)(2,1)S(1)} %sum_first.7), channel_id=1, source_target_pairs={{0,2},{1,5},{2,0},{3,7},{4,6},{5,1},{6,4},{7,3},{8,10},{9,13},{10,... | collective-permute-start | bytes 967688 | tf_op jit(solution)/shard_map/ppermute | solution.py:991
  216.2 19.3 %collective-permute-start.39 = (bf16[48,1920]{1,0:T(8,128)(2,1)S(1)}, bf16[48,1920]{1,0:T(8,128)(2,1)S(1)}, u32[]{:S(2)}, u32[]{:S(2)}) collective-permute-start(bf16[48,1920]{1,0:T(8,128)(2,1)S(1)} %get-tuple-element.196), channel_id=1, source_target_pairs={{0,8},{1,9},{2,10},{3,11},{4,12},{5,13},{6,14},{7,15},{8,0},{9,1},... | collective-permute-start | bytes 552968 | tf_op jit(solution)/shard_map/ppermute | solution.py:991
  216.2 22.4 %collective-permute-start.40 = (bf16[48,1920]{1,0:T(8,128)(2,1)S(1)}, bf16[48,1920]{1,0:T(8,128)(2,1)S(1)}, u32[]{:S(2)}, u32[]{:S(2)}) collective-permute-start(bf16[48,1920]{1,0:T(8,128)(2,1)S(1)} %get-tuple-element.197), channel_id=1, source_target_pairs={{0,16},{1,17},{2,18},{3,19},{4,20},{5,21},{6,22},{7,23},{8,24},{9,... | collective-permute-start | bytes 552968 | tf_op jit(solution)/shard_map/ppermute | solution.py:991
  224.2 14.4 %collective-permute-start.41 = (bf16[48,1920]{1,0:T(8,128)(2,1)S(1)}, bf16[48,1920]{1,0:T(8,128)(2,1)S(1)}, u32[]{:S(2)}, u32[]{:S(2)}) collective-permute-start(bf16[48,1920]{1,0:T(8,128)(2,1)S(1)} %get-tuple-element.198), channel_id=1, source_target_pairs={{0,24},{1,25},{2,26},{3,27},{4,28},{5,29},{6,30},{7,31},{8,16},{9,... | collective-permute-start | bytes 552968 | tf_op jit(solution)/shard_map/ppermute | solution.py:991
  234.3 12.8 %collective-permute-start.43 = (bf16[60,1152]{1,0:T(8,128)(2,1)S(1)}, bf16[60,1152]{1,0:T(8,128)(2,1)S(1)}, u32[]{:S(2)}, u32[]{:S(2)}) collective-permute-start(bf16[60,1152]{1,0:T(8,128)(2,1)S(1)} %get-tuple-element.219), channel_id=1, source_target_pairs={{0,16},{1,17},{2,18},{3,19},{4,20},{5,21},{6,22},{7,23},{8,24},{9,... | collective-permute-start | bytes 414728 | tf_op jit(solution)/shard_map/ppermute | solution.py:991
  235.6 11.6 %collective-permute-start.44 = (bf16[60,1152]{1,0:T(8,128)(2,1)S(1)}, bf16[60,1152]{1,0:T(8,128)(2,1)S(1)}, u32[]{:S(2)}, u32[]{:S(2)}) collective-permute-start(bf16[60,1152]{1,0:T(8,128)(2,1)S(1)} %get-tuple-element.220), channel_id=1, source_target_pairs={{0,24},{1,25},{2,26},{3,27},{4,28},{5,29},{6,30},{7,31},{8,16},{9,... | collective-permute-start | bytes 414728 | tf_op jit(solution)/shard_map/ppermute | solution.py:991
  (28 other events, 176.6 us)

commit v2 on v1

--- a/solution.py
+++ b/solution.py
@@ -585,7 +585,7 @@
 
 
 GROUP = 16
-SPLIT = 4
+SPLIT = 12
 
 
 def groups_at(r):
@@ -811,6 +811,13 @@
             pair, kind = n // kinds, n % kinds
             cut = slice(pair * PAIR, (pair + 1) * PAIR)
             outs[0][kind, :, cut] = own[:, n * PAIR : (n + 1) * PAIR]
+        up_ref, qv_ref = outs[1:]
+        wide = qv_ref.shape[1]
+        rest = small[:, -wide:]
+        ups = up_ref.shape[1] // wide
+        for n in range(ups):
+            up_ref[:, n * wide : (n + 1) * wide] = rest[n : n + 1]
+        qv_ref[...] = rest[ups : ups + 2]
         return
     for out_ref, cut in zip(outs, columns_of(outs)):
         out_ref[...] = own[:, cut]
@@ -872,14 +879,16 @@
     return vmem_call(kernel, outs, operands, "sum_deep")
 
 
-def sum_last(own, answers, widths, small=None):
+def sum_last(own, answers, widths, small=None, up_width=0):
     kernel = functools.partial(
         sum_last_kernel, len(answers), 0 if small is None else small.shape[0]
     )
     operands = [own, *answers] + ([] if small is None else [small])
     outs = [((own.shape[0], w), jnp.float32) for w in widths]
     if small is not None:
-        outs = [((3, own.shape[0], widths[0] // 3), jnp.float32)]
+        width = widths[0] // 3
+        outs = [((3, own.shape[0], width), jnp.float32)]
+        outs += [((1, up_width), jnp.float32), ((2, width), jnp.float32)]
     outs += [] if small is None else [(small.shape, jnp.float32)]
     return vmem_call(kernel, outs, operands, "sum_last", scalars=0)
 
@@ -1270,19 +1279,21 @@
         answers = [deep_step(m, deep, k + 1) for k, m in enumerate(messages)]
         grad_out, grad_up = sum_last(mid_sum, mid_answers, [head_width, up_width])
         grad_out, grad_up, *answers = lax.optimization_barrier((grad_out, grad_up, *answers))
-        grad_qkv, small = sum_last(qkv_sum, answers, [3 * head_width], small)
+        grad_qkv, grad_up_bias, grad_qv_bias, small = sum_last(
+            qkv_sum, answers, [3 * head_width], small, up_width
+        )
         grad_qkv = jnp.swapaxes(grad_qkv, 0, 1)
+        grad_up_bias = grad_up_bias.reshape(up_width)
     else:
         grad_down, grad_up, grad_out = (scattered(v) for v in (down_local, up_local, out_local))
         grad_qkv = by_kind(scattered(jnp.concatenate([local_a, local_b], axis=1)), 3)
         small = lax.psum(small, every)
         part = small.shape[0] // 3
         small = jnp.concatenate([small[n * part : (n + 1) * part] for n in range(3)], axis=1)
-
+        rest = small[:, width : width + head_width]
+        grad_up_bias = rest[: up_width // head_width].reshape(up_width)
+        grad_qv_bias = rest[up_width // head_width :]
     totals = small[:, :width]
-    rest = small[:, width : width + head_width]
-    grad_up_bias = rest[: up_width // head_width].reshape(up_width)
-    grad_qv_bias = rest[up_width // head_width :]
     return (
         layer_out,
         input_grad,

time: 250 us -> 249 us (level)
  waiting for transfers between devices: 62.6 us -> 66.3 us
  starting transfers between devices: 53.1 us -> 50.4 us
    ppermute x36, waiting for transfers between devices: 58 us -> 61.7 us  [group_permute(): return lax.ppermute(value, ('deep', 'quad', 'head'), pairs)]
    ppermute x36, starting transfers between devices: 52.2 us -> 49.5 us  [group_permute(): return lax.ppermute(value, ('deep', 'quad', 'head'), pairs)]
where the time goes in v2:
time: 249 us; the launch traced here: 248 us
  Pallas kernels  120 us (48%)
  waiting for transfers between devices  66.3 us (27%)
  starting transfers between devices  50.4 us (20%)
  local copies, waits for them, and re-layouts  5.31 us (2%)
  other arithmetic  4.81 us (2%)
    ppermute x36, waiting for transfers between devices, group_permute(): return lax.ppermute(value, ('deep', 'quad', 'head'), pairs)  61.7 us
    ppermute x36, starting transfers between devices, group_permute(): return lax.ppermute(value, ('deep', 'quad', 'head'), pairs)  49.5 us
    pallas_call x2, Pallas kernels, attention_backward(): pl.pallas_call(functools.partial(attn_bwd_kernel, pairs, position), out_s...  36.5 us
    pallas_call x8, Pallas kernels, rows_product(): pl.pallas_call(functools.partial(rows_kernel, window, columns_of(lefts)),...  16.2 us
    pallas_call x5, Pallas kernels, outer(): pl.pallas_call(functools.partial(outer_kernel, len(lefts)), out_shape=jax...  15.3 us
    pallas_call x1, Pallas kernels, attention_forward(): pl.pallas_call(functools.partial(attn_fwd_kernel, range(pairs), position)...  13 us
    pallas_call x18, Pallas kernels, vmem_call(): pl.pallas_call(kernel, out_shape=outs, in_specs=[smem] * scalars + [vmem]...  12 us
    pallas_call x2, Pallas kernels, up_gelu(): pl.pallas_call(up_kernel, out_shape=(shape, shape), in_specs=[vmem] * 3,...  9.75 us
  transfers between devices with their start and end apart: 45, of which 17 were waited for; matrix products, arithmetic and copies ran while one was open for 3% of the time, Pallas kernels for 36%

profile of v2, /device:TPU:0, one launch (start us, length us, event | category | flops | bytes accessed | tf_op | source)
XLA Modules:
  0.0 248.0 jit_solution(13894058094320159503)
XLA Ops:
  0.6 3.1 %collective-permute-start.1 = (bf16[144,384]{1,0:T(8,128)(2,1)}, bf16[144,384]{1,0:T(8,128)(2,1)S(1)}, u32[]{:S(2)}, u32[]{:S(2)}) collective-permute-start(bf16[144,384]{1,0:T(8,128)(2,1)} %bitcast.35), channel_id=1, source_target_pairs={{0,8},{1,9},{2,10},{3,11},{4,12},{5,13},{6,14},{7,15},{8,0},{9,1},... | collective-permute-start | bytes 331784 | tf_op jit(solution)/shard_map/ppermute | solution.py:1000
  3.7 2.6 %collective-permute-start.2 = (bf16[144,384]{1,0:T(8,128)(2,1)}, bf16[144,384]{1,0:T(8,128)(2,1)S(1)}, u32[]{:S(2)}, u32[]{:S(2)}) collective-permute-start(bf16[144,384]{1,0:T(8,128)(2,1)} %bitcast.36), channel_id=1, source_target_pairs={{0,16},{1,17},{2,18},{3,19},{4,20},{5,21},{6,22},{7,23},{8,24},{9,... | collective-permute-start | bytes 331784 | tf_op jit(solution)/shard_map/ppermute | solution.py:1000
  7.1 8.2 %collective-permute-done.2 = bf16[144,384]{1,0:T(8,128)(2,1)S(1)} collective-permute-done((bf16[144,384]{1,0:T(8,128)(2,1)}, bf16[144,384]{1,0:T(8,128)(2,1)S(1)}, u32[]{:S(2)}, u32[]{:S(2)}) %collective-permute-start.2) | collective-permute-done | bytes 110624 | tf_op jit(solution)/shard_map/ppermute | solution.py:1000
  23.4 4.3 %collective-permute-done.6 = bf16[48,1920]{1,0:T(8,128)(2,1)S(1)} collective-permute-done((bf16[48,1920]{1,0:T(8,128)(2,1)S(1)}, bf16[48,1920]{1,0:T(8,128)(2,1)S(1)}, u32[]{:S(2)}, u32[]{:S(2)}) %collective-permute-start.6) | collective-permute-done | bytes 184352 | tf_op jit(solution)/shard_map/ppermute | solution.py:1000
  29.8 7.3 %collective-permute-done.7 = bf16[48,1920]{1,0:T(8,128)(2,1)S(1)} collective-permute-done((bf16[48,1920]{1,0:T(8,128)(2,1)S(1)}, bf16[48,1920]{1,0:T(8,128)(2,1)S(1)}, u32[]{:S(2)}, u32[]{:S(2)}) %collective-permute-start.7) | collective-permute-done | bytes 184352 | tf_op jit(solution)/shard_map/ppermute | solution.py:1000
  40.2 6.0 %collective-permute-done.9.refs_3_ = bf16[4,144,384]{2,1,0:T(8,128)(2,1)S(1)} collective-permute-done((bf16[4,144,384]{2,1,0:T(8,128)(2,1)S(1)}, bf16[4,144,384]{2,1,0:T(8,128)(2,1)S(1)}, u32[]{:S(2)}, u32[]{:S(2)}) %collective-permute-start.9) | collective-permute-done | bytes 442400 | tf_op jit(solution)/shard_map/ppermute | solution.py:1000
  47.1 2.7 %collective-permute-start.12 = (bf16[48,1536]{1,0:T(8,128)(2,1)S(1)}, bf16[48,1536]{1,0:T(8,128)(2,1)S(1)}, u32[]{:S(2)}, u32[]{:S(2)}) collective-permute-start(bf16[48,1536]{1,0:T(8,128)(2,1)S(1)} %copy-done.7), channel_id=1, source_target_pairs={{0,8},{1,9},{2,10},{3,11},{4,12},{5,13},{6,14},{7,15},{8,0},{9,1},... | collective-permute-start | bytes 442376 | tf_op jit(solution)/shard_map/ppermute | solution.py:1000
  53.4 4.2 %triple.1.tri_ref = bf16[1536,1152]{1,0:T(8,128)(2,1)S(1)} custom-call(bf16[768,768]{1,0:T(8,128)(2,1)S(1)} %copy-done, bf16[768,768]{1,0:T(8,128)(2,1)S(1)} %collective-permute-done.other_ref.refs_1_, bf16[768,1152]{1,0:T(8,128)(2,1)S(1)} %place_pieces.3.weight_ref.refs_2_, f32[1,1152]{1,0:T(1,128)S(1)} %reshape_reshape.3.bias_ref), custom_call_target="tpu_custom_call" | custom-call | flops 2717908992 | bytes 7667712 | tf_op jit(solution)/shard_map/triple/pallas_call | solution.py:975
  57.6 13.0 %attend_forward.1.refs_0_.refs_2_ = bf16[1536,384]{1,0:T(8,128)(2,1)S(1)} custom-call(s32[1,2]{1,0:T(1,128)S(1)} %copy-done.2, s32[1,6,24,3]{3,2,1,0:T(8,128)S(1)} %copy.35.rb_ref, bf16[1536,1152]{1,0:T(8,128)(2,1)S(1)} %triple.1.tri_ref), custom_call_target="tpu_custom_call" | custom-call | flops 9663676416 | bytes 4718592 | tf_op jit(solution)/shard_map/attend_forward/pallas_call | solution.py:395
  74.0 10.7 %collective-permute-done.16.refs_1_ = bf16[4,48,1536]{2,1,0:T(8,128)(2,1)S(1)} collective-permute-done((bf16[4,48,1536]{2,1,0:T(8,128)(2,1)S(1)}, bf16[4,48,1536]{2,1,0:T(8,128)(2,1)S(1)}, u32[]{:S(2)}, u32[]{:S(2)}) %collective-permute-start.16) | collective-permute-done | bytes 589856 | tf_op jit(solution)/shard_map/ppermute | solution.py:1000
  95.2 4.9 %up_gelu.2 = (bf16[768,1536]{1,0:T(8,128)(2,1)S(1)}, bf16[768,1536]{1,0:T(8,128)(2,1)S(1)}) custom-call(bf16[768,768]{1,0:T(8,128)(2,1)S(1)} %get-tuple-element.240.rows_ref.refs_0_, bf16[768,1536]{1,0:T(8,128)(2,1)S(1)} %get-tuple-element.145.weight_ref.refs_1_, f32[1,1536]{1,0:T(1,128)S(1)} %reshape.72.bias_ref), custom_call_target="tpu_custom_call" | custom-call | flops 1811939328 | bytes 8257536 | tf_op jit(solution)/shard_map/up_gelu/pallas_call | solution.py:477
  100.1 3.0 %collective-permute-done.19.refs_3_ = bf16[4,48,1536]{2,1,0:T(8,128)(2,1)S(1)} collective-permute-done((bf16[4,48,1536]{2,1,0:T(8,128)(2,1)S(1)}, bf16[4,48,1536]{2,1,0:T(8,128)(2,1)S(1)}, u32[]{:S(2)}, u32[]{:S(2)}) %collective-permute-start.19) | collective-permute-done | bytes 589856 | tf_op jit(solution)/shard_map/ppermute | solution.py:1000
  103.0 4.9 %up_gelu.3 = (bf16[768,1536]{1,0:T(8,128)(2,1)S(1)}, bf16[768,1536]{1,0:T(8,128)(2,1)S(1)}) custom-call(bf16[768,768]{1,0:T(8,128)(2,1)S(1)} %collective-permute-done.18.rows_ref.refs_1_, bf16[768,1536]{1,0:T(8,128)(2,1)S(1)} %get-tuple-element.145.weight_ref.refs_1_, f32[1,1536]{1,0:T(1,128)S(1)} %reshape.72.bias_ref), custom_call_target="tpu_custom_call" | custom-call | flops 1811939328 | bytes 8257536 | tf_op jit(solution)/shard_map/up_gelu/pallas_call | solution.py:477
  110.1 2.4 rows_product.11
  112.7 2.4 rows_product.10.down_ref
  115.4 3.9 %norm_two.1 = (bf16[768,768]{1,0:T(8,128)(2,1)}, f32[768,768]{1,0:T(8,128)S(1)}, bf16[768,768]{1,0:T(8,128)(2,1)S(1)}, f32[8,768]{1,0:T(8,128)S(1)}) custom-call(s32[1,2]{1,0:T(1,128)S(1)} %copy-done.2, f32[768,768]{1,0:T(8,128)S(1)} %rows_product.10.down_ref, bf16[768,768]{1,0:T(8,128)(2,1)S(1)} %collective-permute-done.21.other_ref, ...), custom_call_target="tpu_custom_call" | custom-call | flops 23592960 | bytes 11796480 | tf_op jit(solution)/shard_map/norm_two/pallas_call | solution.py:641
  119.6 2.6 %collective-permute-done.22.refs_1_.grad_ref = bf16[768,768]{1,0:T(8,128)(2,1)S(1)} collective-permute-done((bf16[768,768]{1,0:T(8,128)(2,1)S(1)}, bf16[768,768]{1,0:T(8,128)(2,1)S(1)}, u32[]{:S(2)}, u32[]{:S(2)}) %collective-permute-start.22) | collective-permute-done | bytes 1179680 | tf_op jit(solution)/shard_map/ppermute | solution.py:1012
  122.2 4.9 %outer.5.refs_0_ = bf16[768,1536]{1,0:T(8,128)(2,1)S(1)} custom-call(bf16[768,768]{1,0:T(8,128)(2,1)S(1)} %get-tuple-element.156.grad_ref.refs_0_, bf16[768,768]{1,0:T(8,128)(2,1)S(1)} %collective-permute-done.22.refs_1_.grad_ref, bf16[768,1536]{1,0:T(8,128)(2,1)S(1)} %get-tuple-element.151.refs_0_.refs_2_, ...), custom_call_target="tpu_custom_call" | custom-call | flops 3623878656 | bytes 7077888 | tf_op jit(solution)/shard_map/outer/pallas_call | solution.py:554
  127.8 2.9 %back_slope.3 = (bf16[768,1536]{1,0:T(8,128)(2,1)S(1)}, f32[8,1536]{1,0:T(8,128)S(1)}) custom-call(bf16[768,768]{1,0:T(8,128)(2,1)S(1)} %collective-permute-done.22.refs_1_.grad_ref, bf16[768,1536]{1,0:T(8,128)(2,1)S(1)} %place_pieces.5.refs_1_.weight_ref, bf16[768,1536]{1,0:T(8,128)(2,1)S(1)} %get-tuple-element.161.slope_ref), custom_call_target="tpu_custom_call" | custom-call | flops 1811939328 | bytes 8257536 | tf_op jit(solution)/shard_map/back_slope/pallas_call | solution.py:511
  133.9 2.9 %back_slope.2 = (bf16[768,1536]{1,0:T(8,128)(2,1)S(1)}, f32[8,1536]{1,0:T(8,128)S(1)}) custom-call(bf16[768,768]{1,0:T(8,128)(2,1)S(1)} %get-tuple-element.156.grad_ref.refs_0_, bf16[768,1536]{1,0:T(8,128)(2,1)S(1)} %place_pieces.5.refs_1_.weight_ref, bf16[768,1536]{1,0:T(8,128)(2,1)S(1)} %get-tuple-element.157.slope_ref), custom_call_target="tpu_custom_call" | custom-call | flops 1811939328 | bytes 8257536 | tf_op jit(solution)/shard_map/back_slope/pallas_call | solution.py:511
  136.8 2.4 rows_product.12.own_ref
  144.4 5.0 %outer.7.refs_1_ = bf16[768,1536]{1,0:T(8,128)(2,1)S(1)} custom-call(bf16[768,768]{1,0:T(8,128)(2,1)S(1)} %get-tuple-element.240.rows_ref.refs_0_, bf16[768,768]{1,0:T(8,128)(2,1)S(1)} %collective-permute-done.18.rows_ref.refs_1_, bf16[768,1536]{1,0:T(8,128)(2,1)S(1)} %get-tuple-element.158.refs_0_.refs_2_, ...), custom_call_target="tpu_custom_call" | custom-call | flops 3623878656 | bytes 7077888 | tf_op jit(solution)/shard_map/outer/pallas_call | solution.py:554
  152.0 3.2 %collective-permute-done.26.refs_1_ = bf16[192,1536]{1,0:T(8,128)(2,1)S(1)} collective-permute-done((bf16[192,1536]{1,0:T(8,128)(2,1)S(1)}, bf16[192,1536]{1,0:T(8,128)(2,1)S(1)}, u32[]{:S(2)}, u32[]{:S(2)}) %collective-permute-start.26) | collective-permute-done | bytes 589856 | tf_op jit(solution)/shard_map/ppermute | solution.py:1000
  157.4 22.2 %attend_backward.2 = (bf16[1536,768]{1,0:T(8,128)(2,1)S(1)}, f32[8,256]{1,0:T(8,128)S(1)}) custom-call(s32[1,2]{1,0:T(1,128)S(1)} %copy-done.2, s32[1,6,24,3]{3,2,1,0:T(8,128)S(1)} %copy.35.rb_ref, bf16[1536,1152]{1,0:T(8,128)(2,1)S(1)} %triple.1.tri_ref, bf16[1536,384]{1,0:T(8,128)(2,1)S(1)} %project_both.1.grad_ref), custom_call_target="tpu_custom_call" | custom-call | flops 16106127360 | bytes 7864320 | tf_op jit(solution)/shard_map/attend_backward/pallas_call | solution.py:414
  180.4 2.5 %outer.8.refs_0_ = bf16[768,768]{1,0:T(8,128)(2,1)S(1)} custom-call(bf16[768,768]{1,0:T(8,128)(2,1)S(1)} %copy-done, bf16[768,768]{1,0:T(8,128)(2,1)S(1)} %collective-permute-done.other_ref.refs_1_, bf16[1536,768]{1,0:T(8,128)(2,1)S(1)} %get-tuple-element.205.refs_2_.refs_0_), custom_call_target="tpu_custom_call" | custom-call | flops 1811939328 | bytes 4718592 | tf_op jit(solution)/shard_map/outer/pallas_call | solution.py:554
  184.9 4.3 %collective-permute-start.33 = (bf16[48,1536]{1,0:T(8,128)(2,1)S(1)}, bf16[48,1536]{1,0:T(8,128)(2,1)S(1)}, u32[]{:S(2)}, u32[]{:S(2)}) collective-permute-start(bf16[48,1536]{1,0:T(8,128)(2,1)S(1)} %get-tuple-element.181), channel_id=1, source_target_pairs={{0,16},{1,17},{2,18},{3,19},{4,20},{5,21},{6,22},{7,23},{8,24},{9,... | collective-permute-start | bytes 442376 | tf_op jit(solution)/shard_map/ppermute | solution.py:1000
  192.6 14.2 %attend_backward.3 = (bf16[1536,384]{1,0:T(8,128)(2,1)S(1)}, f32[8,128]{1,0:T(8,128)S(1)}) custom-call(s32[1,2]{1,0:T(1,128)S(1)} %copy-done.2, s32[1,6,24,3]{3,2,1,0:T(8,128)S(1)} %copy.35.rb_ref, bf16[1536,1152]{1,0:T(8,128)(2,1)S(1)} %triple.1.tri_ref, bf16[1536,384]{1,0:T(8,128)(2,1)S(1)} %project_both.1.grad_ref), custom_call_target="tpu_custom_call" | custom-call | flops 8053063680 | bytes 3932160 | tf_op jit(solution)/shard_map/attend_backward/pallas_call | solution.py:414
  214.3 3.3 %collective-permute-start.40 = (bf16[48,1920]{1,0:T(8,128)(2,1)S(1)}, bf16[48,1920]{1,0:T(8,128)(2,1)S(1)}, u32[]{:S(2)}, u32[]{:S(2)}) collective-permute-start(bf16[48,1920]{1,0:T(8,128)(2,1)S(1)} %get-tuple-element.199), channel_id=1, source_target_pairs={{0,16},{1,17},{2,18},{3,19},{4,20},{5,21},{6,22},{7,23},{8,24},{9,... | collective-permute-start | bytes 552968 | tf_op jit(solution)/shard_map/ppermute | solution.py:1000
  218.4 3.9 %collective-permute-done.37.refs_4_ = bf16[192,768]{1,0:T(8,128)(2,1)S(1)} collective-permute-done((bf16[192,768]{1,0:T(8,128)(2,1)S(1)}, bf16[192,768]{1,0:T(8,128)(2,1)S(1)}, u32[]{:S(2)}, u32[]{:S(2)}) %collective-permute-start.37) | collective-permute-done | bytes 294944 | tf_op jit(solution)/shard_map/ppermute | solution.py:1000
  222.3 3.1 %collective-permute-start.41 = (bf16[48,1920]{1,0:T(8,128)(2,1)S(1)}, bf16[48,1920]{1,0:T(8,128)(2,1)S(1)}, u32[]{:S(2)}, u32[]{:S(2)}) collective-permute-start(bf16[48,1920]{1,0:T(8,128)(2,1)S(1)} %get-tuple-element.200), channel_id=1, source_target_pairs={{0,24},{1,25},{2,26},{3,27},{4,28},{5,29},{6,30},{7,31},{8,16},{9,... | collective-permute-start | bytes 552968 | tf_op jit(solution)/shard_map/ppermute | solution.py:1000
  233.6 3.1 %collective-permute-start.44 = (bf16[60,1152]{1,0:T(8,128)(2,1)S(1)}, bf16[60,1152]{1,0:T(8,128)(2,1)S(1)}, u32[]{:S(2)}, u32[]{:S(2)}) collective-permute-start(bf16[60,1152]{1,0:T(8,128)(2,1)S(1)} %get-tuple-element.222), channel_id=1, source_target_pairs={{0,24},{1,25},{2,26},{3,27},{4,28},{5,29},{6,30},{7,31},{8,16},{9,... | collective-permute-start | bytes 414728 | tf_op jit(solution)/shard_map/ppermute | solution.py:1000
  239.2 6.7 %collective-permute-done.43.refs_2_ = bf16[60,1152]{1,0:T(8,128)(2,1)S(1)} collective-permute-done((bf16[60,1152]{1,0:T(8,128)(2,1)S(1)}, bf16[60,1152]{1,0:T(8,128)(2,1)S(1)}, u32[]{:S(2)}, u32[]{:S(2)}) %collective-permute-start.43) | collective-permute-done | bytes 138272 | tf_op jit(solution)/shard_map/ppermute | solution.py:1000
  (158 shorter events, 75.6 us)
Async XLA Ops:
  3.7 11.6 %collective-permute-start.2 = (bf16[144,384]{1,0:T(8,128)(2,1)}, bf16[144,384]{1,0:T(8,128)(2,1)S(1)}, u32[]{:S(2)}, u32[]{:S(2)}) collective-permute-start(bf16[144,384]{1,0:T(8,128)(2,1)} %bitcast.36), channel_id=1, source_target_pairs={{0,16},{1,17},{2,18},{3,19},{4,20},{5,21},{6,22},{7,23},{8,24},{9,... | collective-permute-start | bytes 331784 | tf_op jit(solution)/shard_map/ppermute | solution.py:1000
  6.3 46.6 %collective-permute-start = (bf16[768,768]{1,0:T(8,128)(2,1)}, bf16[768,768]{1,0:T(8,128)(2,1)S(1)}, u32[]{:S(2)}, u32[]{:S(2)}) collective-permute-start(bf16[768,768]{1,0:T(8,128)(2,1)} %refs_0_.3), channel_id=1, source_target_pairs={{0,1},{1,0},{2,3},{3,2},{4,5},{5,4},{6,7},{7,6},{8,9},{9,8},{10,11... | collective-permute-start | bytes 3538952 | tf_op jit(solution)/shard_map/ppermute | solution.py:1012
  16.3 20.9 %collective-permute-start.4 = (bf16[4,144,384]{2,1,0:T(8,128)(2,1)S(1)}, bf16[4,144,384]{2,1,0:T(8,128)(2,1)S(1)}, u32[]{:S(2)}, u32[]{:S(2)}) collective-permute-start(bf16[4,144,384]{2,1,0:T(8,128)(2,1)S(1)} %pad_maximum_fusion.2.refs_0_), channel_id=1, source_target_pairs={{0,2},{1,5},{2,0},{3,7},{4,6},{5,1},{6,4},{7,3},{8,10},{9,13},{10,... | collective-permute-start | bytes 1327112 | tf_op jit(solution)/shard_map/ppermute | solution.py:1000
  17.9 20.0 %collective-permute-start.5 = (bf16[4,144,384]{2,1,0:T(8,128)(2,1)S(1)}, bf16[4,144,384]{2,1,0:T(8,128)(2,1)S(1)}, u32[]{:S(2)}, u32[]{:S(2)}) collective-permute-start(bf16[4,144,384]{2,1,0:T(8,128)(2,1)S(1)} %pad_maximum_fusion.2.refs_0_), channel_id=1, source_target_pairs={{0,4},{1,3},{2,6},{3,1},{4,0},{5,7},{6,2},{7,5},{8,12},{9,11},{10,... | collective-permute-start | bytes 1327112 | tf_op jit(solution)/shard_map/ppermute | solution.py:1000
  22.2 15.0 %collective-permute-start.7 = (bf16[48,1920]{1,0:T(8,128)(2,1)S(1)}, bf16[48,1920]{1,0:T(8,128)(2,1)S(1)}, u32[]{:S(2)}, u32[]{:S(2)}) collective-permute-start(bf16[48,1920]{1,0:T(8,128)(2,1)S(1)} %constant_dynamic-update-slice_fusion), channel_id=1, source_target_pairs={{0,16},{1,17},{2,18},{3,19},{4,20},{5,21},{6,22},{7,23},{8,24},{9,... | collective-permute-start | bytes 552968 | tf_op jit(solution)/shard_map/ppermute | solution.py:1000
  47.1 23.6 %collective-permute-start.12 = (bf16[48,1536]{1,0:T(8,128)(2,1)S(1)}, bf16[48,1536]{1,0:T(8,128)(2,1)S(1)}, u32[]{:S(2)}, u32[]{:S(2)}) collective-permute-start(bf16[48,1536]{1,0:T(8,128)(2,1)S(1)} %copy-done.7), channel_id=1, source_target_pairs={{0,8},{1,9},{2,10},{3,11},{4,12},{5,13},{6,14},{7,15},{8,0},{9,1},... | collective-permute-start | bytes 442376 | tf_op jit(solution)/shard_map/ppermute | solution.py:1000
  49.8 20.9 %collective-permute-start.13 = (bf16[48,1536]{1,0:T(8,128)(2,1)S(1)}, bf16[48,1536]{1,0:T(8,128)(2,1)S(1)}, u32[]{:S(2)}, u32[]{:S(2)}) collective-permute-start(bf16[48,1536]{1,0:T(8,128)(2,1)S(1)} %copy-done.7), channel_id=1, source_target_pairs={{0,16},{1,17},{2,18},{3,19},{4,20},{5,21},{6,22},{7,23},{8,24},{9,... | collective-permute-start | bytes 442376 | tf_op jit(solution)/shard_map/ppermute | solution.py:1000
  50.8 19.9 %collective-permute-start.14 = (bf16[48,1536]{1,0:T(8,128)(2,1)S(1)}, bf16[48,1536]{1,0:T(8,128)(2,1)S(1)}, u32[]{:S(2)}, u32[]{:S(2)}) collective-permute-start(bf16[48,1536]{1,0:T(8,128)(2,1)S(1)} %copy-done.7), channel_id=1, source_target_pairs={{0,24},{1,25},{2,26},{3,27},{4,28},{5,29},{6,30},{7,31},{8,16},{9,... | collective-permute-start | bytes 442376 | tf_op jit(solution)/shard_map/ppermute | solution.py:1000
  52.4 18.4 %collective-permute-start.10 = (bf16[4,48,1920]{2,1,0:T(8,128)(2,1)S(1)}, bf16[4,48,1920]{2,1,0:T(8,128)(2,1)S(1)}, u32[]{:S(2)}, u32[]{:S(2)}) collective-permute-start(bf16[4,48,1920]{2,1,0:T(8,128)(2,1)S(1)} %pad_maximum_fusion.refs_0_), channel_id=1, source_target_pairs={{0,2},{1,5},{2,0},{3,7},{4,6},{5,1},{6,4},{7,3},{8,10},{9,13},{10,... | collective-permute-start | bytes 2211848 | tf_op jit(solution)/shard_map/ppermute | solution.py:1000
  53.0 17.8 %collective-permute-start.11 = (bf16[4,48,1920]{2,1,0:T(8,128)(2,1)S(1)}, bf16[4,48,1920]{2,1,0:T(8,128)(2,1)S(1)}, u32[]{:S(2)}, u32[]{:S(2)}) collective-permute-start(bf16[4,48,1920]{2,1,0:T(8,128)(2,1)S(1)} %pad_maximum_fusion.refs_0_), channel_id=1, source_target_pairs={{0,4},{1,3},{2,6},{3,1},{4,0},{5,7},{6,2},{7,5},{8,12},{9,11},{10,... | collective-permute-start | bytes 2211848 | tf_op jit(solution)/shard_map/ppermute | solution.py:1000
  70.7 15.6 %collective-permute-start.15 = (bf16[4,48,1920]{2,1,0:T(8,128)(2,1)S(1)}, bf16[4,48,1920]{2,1,0:T(8,128)(2,1)S(1)}, u32[]{:S(2)}, u32[]{:S(2)}) collective-permute-start(bf16[4,48,1920]{2,1,0:T(8,128)(2,1)S(1)} %collective-permute-done.10.refs_1_), channel_id=1, source_target_pairs={{0,4},{1,3},{2,6},{3,1},{4,0},{5,7},{6,2},{7,5},{8,12},{9,11},{10,... | collective-permute-start | bytes 2211848 | tf_op jit(solution)/shard_map/ppermute | solution.py:1000
  72.4 12.3 %collective-permute-start.16 = (bf16[4,48,1536]{2,1,0:T(8,128)(2,1)S(1)}, bf16[4,48,1536]{2,1,0:T(8,128)(2,1)S(1)}, u32[]{:S(2)}, u32[]{:S(2)}) collective-permute-start(bf16[4,48,1536]{2,1,0:T(8,128)(2,1)S(1)} %pad_maximum_fusion.1.refs_0_), channel_id=1, source_target_pairs={{0,2},{1,5},{2,0},{3,7},{4,6},{5,1},{6,4},{7,3},{8,10},{9,13},{10,... | collective-permute-start | bytes 1769480 | tf_op jit(solution)/shard_map/ppermute | solution.py:1000
  92.9 10.1 %collective-permute-start.18 = (bf16[768,768]{1,0:T(8,128)(2,1)S(1)}, bf16[768,768]{1,0:T(8,128)(2,1)S(1)}, u32[]{:S(2)}, u32[]{:S(2)}) collective-permute-start(bf16[768,768]{1,0:T(8,128)(2,1)S(1)} %get-tuple-element.240.rows_ref.refs_0_), channel_id=1, source_target_pairs={{0,1},{1,0},{2,3},{3,2},{4,5},{5,4},{6,7},{7,6},{8,9},{9,8},{10,11... | collective-permute-start | bytes 3538952 | tf_op jit(solution)/shard_map/ppermute | solution.py:1012
  93.1 9.9 %collective-permute-start.19 = (bf16[4,48,1536]{2,1,0:T(8,128)(2,1)S(1)}, bf16[4,48,1536]{2,1,0:T(8,128)(2,1)S(1)}, u32[]{:S(2)}, u32[]{:S(2)}) collective-permute-start(bf16[4,48,1536]{2,1,0:T(8,128)(2,1)S(1)} %collective-permute-done.16.refs_1_), channel_id=1, source_target_pairs={{0,4},{1,3},{2,6},{3,1},{4,0},{5,7},{6,2},{7,5},{8,12},{9,11},{10,... | collective-permute-start | bytes 1769480 | tf_op jit(solution)/shard_map/ppermute | solution.py:1000
  94.0 15.4 %collective-permute-start.20 = (bf16[4,48,1536]{2,1,0:T(8,128)(2,1)S(1)}, bf16[4,48,1536]{2,1,0:T(8,128)(2,1)S(1)}, u32[]{:S(2)}, u32[]{:S(2)}) collective-permute-start(bf16[4,48,1536]{2,1,0:T(8,128)(2,1)S(1)} %pad_maximum_fusion.1.refs_0_), channel_id=1, source_target_pairs={{0,4},{1,3},{2,6},{3,1},{4,0},{5,7},{6,2},{7,5},{8,12},{9,11},{10,... | collective-permute-start | bytes 1769480 | tf_op jit(solution)/shard_map/ppermute | solution.py:1000
  133.4 9.9 %collective-permute-start.24 = (bf16[192,1536]{1,0:T(8,128)(2,1)S(1)}, bf16[192,1536]{1,0:T(8,128)(2,1)S(1)}, u32[]{:S(2)}, u32[]{:S(2)}) collective-permute-start(bf16[192,1536]{1,0:T(8,128)(2,1)S(1)} %get-tuple-element.165), channel_id=1, source_target_pairs={{0,2},{1,5},{2,0},{3,7},{4,6},{5,1},{6,4},{7,3},{8,10},{9,13},{10,... | collective-permute-start | bytes 1769480 | tf_op jit(solution)/shard_map/ppermute | solution.py:1000
  144.1 11.1 %collective-permute-start.26 = (bf16[192,1536]{1,0:T(8,128)(2,1)S(1)}, bf16[192,1536]{1,0:T(8,128)(2,1)S(1)}, u32[]{:S(2)}, u32[]{:S(2)}) collective-permute-start(bf16[192,1536]{1,0:T(8,128)(2,1)S(1)} %get-tuple-element.169), channel_id=1, source_target_pairs={{0,2},{1,5},{2,0},{3,7},{4,6},{5,1},{6,4},{7,3},{8,10},{9,13},{10,... | collective-permute-start | bytes 1769480 | tf_op jit(solution)/shard_map/ppermute | solution.py:1000
  149.4 30.3 %collective-permute-start.28 = (bf16[192,1536]{1,0:T(8,128)(2,1)S(1)}, bf16[192,1536]{1,0:T(8,128)(2,1)S(1)}, u32[]{:S(2)}, u32[]{:S(2)}) collective-permute-start(bf16[192,1536]{1,0:T(8,128)(2,1)S(1)} %sum_second.4), channel_id=1, source_target_pairs={{0,4},{1,3},{2,6},{3,1},{4,0},{5,7},{6,2},{7,5},{8,12},{9,11},{10,... | collective-permute-start | bytes 1769480 | tf_op jit(solution)/shard_map/ppermute | solution.py:1000
  150.5 29.1 %collective-permute-start.29 = (f32[16,768]{1,0:T(8,128)S(1)}, f32[16,768]{1,0:T(8,128)S(1)}, u32[]{:S(2)}, u32[]{:S(2)}) collective-permute-start(f32[16,768]{1,0:T(8,128)S(1)} %constant_dynamic-update-slice_fusion.2.own_ref), channel_id=1, source_target_pairs={{0,1},{1,0},{2,3},{3,2},{4,5},{5,4},{6,7},{7,6},{8,9},{9,8},{10,11... | collective-permute-start | bytes 147464 | tf_op jit(solution)/shard_map/ppermute | solution.py:1012
  157.3 22.4 %collective-permute-start.27 = (bf16[384,1920]{1,0:T(8,128)(2,1)S(1)}, bf16[384,1920]{1,0:T(8,128)(2,1)S(1)}, u32[]{:S(2)}, u32[]{:S(2)}) collective-permute-start(bf16[384,1920]{1,0:T(8,128)(2,1)S(1)} %sum_first.5), channel_id=1, source_target_pairs={{0,2},{1,5},{2,0},{3,7},{4,6},{5,1},{6,4},{7,3},{8,10},{9,13},{10,... | collective-permute-start | bytes 4423688 | tf_op jit(solution)/shard_map/ppermute | solution.py:1000
  184.3 22.6 %collective-permute-start.32 = (bf16[48,1536]{1,0:T(8,128)(2,1)S(1)}, bf16[48,1536]{1,0:T(8,128)(2,1)S(1)}, u32[]{:S(2)}, u32[]{:S(2)}) collective-permute-start(bf16[48,1536]{1,0:T(8,128)(2,1)S(1)} %get-tuple-element.180), channel_id=1, source_target_pairs={{0,8},{1,9},{2,10},{3,11},{4,12},{5,13},{6,14},{7,15},{8,0},{9,1},... | collective-permute-start | bytes 442376 | tf_op jit(solution)/shard_map/ppermute | solution.py:1000
  184.9 22.0 %collective-permute-start.33 = (bf16[48,1536]{1,0:T(8,128)(2,1)S(1)}, bf16[48,1536]{1,0:T(8,128)(2,1)S(1)}, u32[]{:S(2)}, u32[]{:S(2)}) collective-permute-start(bf16[48,1536]{1,0:T(8,128)(2,1)S(1)} %get-tuple-element.181), channel_id=1, source_target_pairs={{0,16},{1,17},{2,18},{3,19},{4,20},{5,21},{6,22},{7,23},{8,24},{9,... | collective-permute-start | bytes 442376 | tf_op jit(solution)/shard_map/ppermute | solution.py:1000
  189.1 17.8 %collective-permute-start.34 = (bf16[48,1536]{1,0:T(8,128)(2,1)S(1)}, bf16[48,1536]{1,0:T(8,128)(2,1)S(1)}, u32[]{:S(2)}, u32[]{:S(2)}) collective-permute-start(bf16[48,1536]{1,0:T(8,128)(2,1)S(1)} %get-tuple-element.182), channel_id=1, source_target_pairs={{0,24},{1,25},{2,26},{3,27},{4,28},{5,29},{6,30},{7,31},{8,16},{9,... | collective-permute-start | bytes 442376 | tf_op jit(solution)/shard_map/ppermute | solution.py:1000
  189.1 17.8 %collective-permute-start.31 = (bf16[192,1920]{1,0:T(8,128)(2,1)S(1)}, bf16[192,1920]{1,0:T(8,128)(2,1)S(1)}, u32[]{:S(2)}, u32[]{:S(2)}) collective-permute-start(bf16[192,1920]{1,0:T(8,128)(2,1)S(1)} %sum_second.5), channel_id=1, source_target_pairs={{0,4},{1,3},{2,6},{3,1},{4,0},{5,7},{6,2},{7,5},{8,12},{9,11},{10,... | collective-permute-start | bytes 2211848 | tf_op jit(solution)/shard_map/ppermute | solution.py:1000
  191.0 15.9 %collective-permute-start.30 = (bf16[384,768]{1,0:T(8,128)(2,1)S(1)}, bf16[384,768]{1,0:T(8,128)(2,1)S(1)}, u32[]{:S(2)}, u32[]{:S(2)}) collective-permute-start(bf16[384,768]{1,0:T(8,128)(2,1)S(1)} %sum_first.6), channel_id=1, source_target_pairs={{0,2},{1,5},{2,0},{3,7},{4,6},{5,1},{6,4},{7,3},{8,10},{9,13},{10,... | collective-permute-start | bytes 1769480 | tf_op jit(solution)/shard_map/ppermute | solution.py:1000
  212.5 12.9 %collective-permute-start.35 = (bf16[768,768]{1,0:T(8,128)(2,1)S(1)}, bf16[768,768]{1,0:T(8,128)(2,1)S(1)}, u32[]{:S(2)}, u32[]{:S(2)}) collective-permute-start(bf16[768,768]{1,0:T(8,128)(2,1)S(1)} %rows_product.14), channel_id=1, source_target_pairs={{0,1},{1,0},{2,3},{3,2},{4,5},{5,4},{6,7},{7,6},{8,9},{9,8},{10,11... | collective-permute-start | bytes 3538952 | tf_op jit(solution)/shard_map/ppermute | solution.py:1012
  212.6 12.8 %collective-permute-start.36 = (bf16[420,384]{1,0:T(8,128)(2,1)S(1)}, bf16[420,384]{1,0:T(8,128)(2,1)S(1)}, u32[]{:S(2)}, u32[]{:S(2)}) collective-permute-start(bf16[420,384]{1,0:T(8,128)(2,1)S(1)} %sum_first.7), channel_id=1, source_target_pairs={{0,2},{1,5},{2,0},{3,7},{4,6},{5,1},{6,4},{7,3},{8,10},{9,13},{10,... | collective-permute-start | bytes 967688 | tf_op jit(solution)/shard_map/ppermute | solution.py:1000
  214.0 19.6 %collective-permute-start.39 = (bf16[48,1920]{1,0:T(8,128)(2,1)S(1)}, bf16[48,1920]{1,0:T(8,128)(2,1)S(1)}, u32[]{:S(2)}, u32[]{:S(2)}) collective-permute-start(bf16[48,1920]{1,0:T(8,128)(2,1)S(1)} %get-tuple-element.198), channel_id=1, source_target_pairs={{0,8},{1,9},{2,10},{3,11},{4,12},{5,13},{6,14},{7,15},{8,0},{9,1},... | collective-permute-start | bytes 552968 | tf_op jit(solution)/shard_map/ppermute | solution.py:1000
  214.3 22.5 %collective-permute-start.40 = (bf16[48,1920]{1,0:T(8,128)(2,1)S(1)}, bf16[48,1920]{1,0:T(8,128)(2,1)S(1)}, u32[]{:S(2)}, u32[]{:S(2)}) collective-permute-start(bf16[48,1920]{1,0:T(8,128)(2,1)S(1)} %get-tuple-element.199), channel_id=1, source_target_pairs={{0,16},{1,17},{2,18},{3,19},{4,20},{5,21},{6,22},{7,23},{8,24},{9,... | collective-permute-start | bytes 552968 | tf_op jit(solution)/shard_map/ppermute | solution.py:1000
  222.3 14.4 %collective-permute-start.41 = (bf16[48,1920]{1,0:T(8,128)(2,1)S(1)}, bf16[48,1920]{1,0:T(8,128)(2,1)S(1)}, u32[]{:S(2)}, u32[]{:S(2)}) collective-permute-start(bf16[48,1920]{1,0:T(8,128)(2,1)S(1)} %get-tuple-element.200), channel_id=1, source_target_pairs={{0,24},{1,25},{2,26},{3,27},{4,28},{5,29},{6,30},{7,31},{8,16},{9,... | collective-permute-start | bytes 552968 | tf_op jit(solution)/shard_map/ppermute | solution.py:1000
  232.4 13.6 %collective-permute-start.43 = (bf16[60,1152]{1,0:T(8,128)(2,1)S(1)}, bf16[60,1152]{1,0:T(8,128)(2,1)S(1)}, u32[]{:S(2)}, u32[]{:S(2)}) collective-permute-start(bf16[60,1152]{1,0:T(8,128)(2,1)S(1)} %get-tuple-element.221), channel_id=1, source_target_pairs={{0,16},{1,17},{2,18},{3,19},{4,20},{5,21},{6,22},{7,23},{8,24},{9,... | collective-permute-start | bytes 414728 | tf_op jit(solution)/shard_map/ppermute | solution.py:1000
  233.6 12.3 %collective-permute-start.44 = (bf16[60,1152]{1,0:T(8,128)(2,1)S(1)}, bf16[60,1152]{1,0:T(8,128)(2,1)S(1)}, u32[]{:S(2)}, u32[]{:S(2)}) collective-permute-start(bf16[60,1152]{1,0:T(8,128)(2,1)S(1)} %get-tuple-element.222), channel_id=1, source_target_pairs={{0,24},{1,25},{2,26},{3,27},{4,28},{5,29},{6,30},{7,31},{8,16},{9,... | collective-permute-start | bytes 414728 | tf_op jit(solution)/shard_map/ppermute | solution.py:1000
  (28 other events, 176.3 us)

commit v3 on v2

--- a/solution.py
+++ b/solution.py
@@ -1260,14 +1260,16 @@
     if staged:
         mid_got, product = lax.optimization_barrier((mid_got, product))
         mid_sum, *messages = sum_deep([mids], spot, [mid_got], [mid_two])
-        mid_answers = [deep_step(m, deep, k + 1) for k, m in enumerate(messages)]
+        mid_answers = [deep_step(m, deep, k + 1) for k, m in enumerate(messages[:-1])]
+        mid_last = messages[-1]
         product, *messages = lax.optimization_barrier((product, *messages))
     other = swap(product)
     if staged:
         grads_a, other, got_b, two_a = lax.optimization_barrier((grads_a, other, got_b, two_a))
         message, small = sum_second([local_b], spot, got_b, small)
         two_b = second_quad(message)
-        grads_a, message = lax.optimization_barrier((grads_a, message))
+        grads_a, message, mid_last = lax.optimization_barrier((grads_a, message, mid_last))
+        mid_answers.append(deep_step(mid_last, deep, deep - 1))
     mine = rows_product([grads_a, grads_b], full_qkv, (0, half), jnp.float32)
     input_grad = low(mine + other.astype(jnp.float32) + grad_res_one)
     if staged:

time: 249 us -> 248 us (level)
  transfers between devices with their start and end apart: 45 -> 45, of which waited for: 17 -> 17; matrix products, arithmetic and copies ran while one was open for 3% -> 3% of each run, Pallas kernels for 36% -> 37%
where the time goes in v3:
time: 248 us
  Pallas kernels  122 us (49%)
  waiting for transfers between devices  65.2 us (26%)
  starting transfers between devices  48.7 us (20%)
  local copies, waits for them, and re-layouts  5.31 us (2%)
  other arithmetic  4.81 us (2%)
    ppermute x36, waiting for transfers between devices, group_permute(): return lax.ppermute(value, ('deep', 'quad', 'head'), pairs)  60.6 us
    ppermute x36, starting transfers between devices, group_permute(): return lax.ppermute(value, ('deep', 'quad', 'head'), pairs)  47.8 us
    pallas_call x2, Pallas kernels, attention_backward(): pl.pallas_call(functools.partial(attn_bwd_kernel, pairs, position), out_s...  38.4 us
    pallas_call x8, Pallas kernels, rows_product(): pl.pallas_call(functools.partial(rows_kernel, window, columns_of(lefts)),...  16.2 us
    pallas_call x5, Pallas kernels, outer(): pl.pallas_call(functools.partial(outer_kernel, len(lefts)), out_shape=jax...  15.3 us
    pallas_call x1, Pallas kernels, attention_forward(): pl.pallas_call(functools.partial(attn_fwd_kernel, range(pairs), position)...  13.7 us
    pallas_call x18, Pallas kernels, vmem_call(): pl.pallas_call(kernel, out_shape=outs, in_specs=[smem] * scalars + [vmem]...  12 us
    pallas_call x2, Pallas kernels, up_gelu(): pl.pallas_call(up_kernel, out_shape=(shape, shape), in_specs=[vmem] * 3,...  9.75 us
  transfers between devices with their start and end apart: 45, of which 17 were waited for; matrix products, arithmetic and copies ran while one was open for 3% of the time, Pallas kernels for 37%

profile of v3, /device:TPU:0, one launch (start us, length us, event | category | flops | bytes accessed | tf_op | source)
XLA Modules:
  0.0 247.8 jit_solution(10380256924547842516)
XLA Ops:
  0.6 3.1 %collective-permute-start.1 = (bf16[144,384]{1,0:T(8,128)(2,1)}, bf16[144,384]{1,0:T(8,128)(2,1)S(1)}, u32[]{:S(2)}, u32[]{:S(2)}) collective-permute-start(bf16[144,384]{1,0:T(8,128)(2,1)} %bitcast.35), channel_id=1, source_target_pairs={{0,8},{1,9},{2,10},{3,11},{4,12},{5,13},{6,14},{7,15},{8,0},{9,1},... | collective-permute-start | bytes 331784 | tf_op jit(solution)/shard_map/ppermute | solution.py:1000
  3.7 2.6 %collective-permute-start.2 = (bf16[144,384]{1,0:T(8,128)(2,1)}, bf16[144,384]{1,0:T(8,128)(2,1)S(1)}, u32[]{:S(2)}, u32[]{:S(2)}) collective-permute-start(bf16[144,384]{1,0:T(8,128)(2,1)} %bitcast.36), channel_id=1, source_target_pairs={{0,16},{1,17},{2,18},{3,19},{4,20},{5,21},{6,22},{7,23},{8,24},{9,... | collective-permute-start | bytes 331784 | tf_op jit(solution)/shard_map/ppermute | solution.py:1000
  7.1 8.2 %collective-permute-done.2 = bf16[144,384]{1,0:T(8,128)(2,1)S(1)} collective-permute-done((bf16[144,384]{1,0:T(8,128)(2,1)}, bf16[144,384]{1,0:T(8,128)(2,1)S(1)}, u32[]{:S(2)}, u32[]{:S(2)}) %collective-permute-start.2) | collective-permute-done | bytes 110624 | tf_op jit(solution)/shard_map/ppermute | solution.py:1000
  23.4 4.3 %collective-permute-done.6 = bf16[48,1920]{1,0:T(8,128)(2,1)S(1)} collective-permute-done((bf16[48,1920]{1,0:T(8,128)(2,1)S(1)}, bf16[48,1920]{1,0:T(8,128)(2,1)S(1)}, u32[]{:S(2)}, u32[]{:S(2)}) %collective-permute-start.6) | collective-permute-done | bytes 184352 | tf_op jit(solution)/shard_map/ppermute | solution.py:1000
  29.8 7.3 %collective-permute-done.7 = bf16[48,1920]{1,0:T(8,128)(2,1)S(1)} collective-permute-done((bf16[48,1920]{1,0:T(8,128)(2,1)S(1)}, bf16[48,1920]{1,0:T(8,128)(2,1)S(1)}, u32[]{:S(2)}, u32[]{:S(2)}) %collective-permute-start.7) | collective-permute-done | bytes 184352 | tf_op jit(solution)/shard_map/ppermute | solution.py:1000
  40.2 6.0 %collective-permute-done.9.refs_3_ = bf16[4,144,384]{2,1,0:T(8,128)(2,1)S(1)} collective-permute-done((bf16[4,144,384]{2,1,0:T(8,128)(2,1)S(1)}, bf16[4,144,384]{2,1,0:T(8,128)(2,1)S(1)}, u32[]{:S(2)}, u32[]{:S(2)}) %collective-permute-start.9) | collective-permute-done | bytes 442400 | tf_op jit(solution)/shard_map/ppermute | solution.py:1000
  47.1 2.7 %collective-permute-start.12 = (bf16[48,1536]{1,0:T(8,128)(2,1)S(1)}, bf16[48,1536]{1,0:T(8,128)(2,1)S(1)}, u32[]{:S(2)}, u32[]{:S(2)}) collective-permute-start(bf16[48,1536]{1,0:T(8,128)(2,1)S(1)} %copy-done.7), channel_id=1, source_target_pairs={{0,8},{1,9},{2,10},{3,11},{4,12},{5,13},{6,14},{7,15},{8,0},{9,1},... | collective-permute-start | bytes 442376 | tf_op jit(solution)/shard_map/ppermute | solution.py:1000
  53.4 4.2 %triple.1.tri_ref = bf16[1536,1152]{1,0:T(8,128)(2,1)S(1)} custom-call(bf16[768,768]{1,0:T(8,128)(2,1)S(1)} %copy-done, bf16[768,768]{1,0:T(8,128)(2,1)S(1)} %collective-permute-done.other_ref.refs_1_, bf16[768,1152]{1,0:T(8,128)(2,1)S(1)} %place_pieces.3.weight_ref.refs_2_, f32[1,1152]{1,0:T(1,128)S(1)} %reshape_reshape.3.bias_ref), custom_call_target="tpu_custom_call" | custom-call | flops 2717908992 | bytes 7667712 | tf_op jit(solution)/shard_map/triple/pallas_call | solution.py:975
  57.6 13.7 %attend_forward.1.refs_0_.refs_2_ = bf16[1536,384]{1,0:T(8,128)(2,1)S(1)} custom-call(s32[1,2]{1,0:T(1,128)S(1)} %copy-done.2, s32[1,6,24,3]{3,2,1,0:T(8,128)S(1)} %copy.35.rb_ref, bf16[1536,1152]{1,0:T(8,128)(2,1)S(1)} %triple.1.tri_ref), custom_call_target="tpu_custom_call" | custom-call | flops 9663676416 | bytes 4718592 | tf_op jit(solution)/shard_map/attend_forward/pallas_call | solution.py:395
  74.0 11.0 %collective-permute-done.16.refs_1_ = bf16[4,48,1536]{2,1,0:T(8,128)(2,1)S(1)} collective-permute-done((bf16[4,48,1536]{2,1,0:T(8,128)(2,1)S(1)}, bf16[4,48,1536]{2,1,0:T(8,128)(2,1)S(1)}, u32[]{:S(2)}, u32[]{:S(2)}) %collective-permute-start.16) | collective-permute-done | bytes 589856 | tf_op jit(solution)/shard_map/ppermute | solution.py:1000
  95.2 4.9 %up_gelu.2 = (bf16[768,1536]{1,0:T(8,128)(2,1)S(1)}, bf16[768,1536]{1,0:T(8,128)(2,1)S(1)}) custom-call(bf16[768,768]{1,0:T(8,128)(2,1)S(1)} %get-tuple-element.242.rows_ref.refs_0_, bf16[768,1536]{1,0:T(8,128)(2,1)S(1)} %get-tuple-element.146.weight_ref.refs_1_, f32[1,1536]{1,0:T(1,128)S(1)} %reshape.72.bias_ref), custom_call_target="tpu_custom_call" | custom-call | flops 1811939328 | bytes 8257536 | tf_op jit(solution)/shard_map/up_gelu/pallas_call | solution.py:477
  100.1 3.0 %collective-permute-done.19.refs_3_ = bf16[4,48,1536]{2,1,0:T(8,128)(2,1)S(1)} collective-permute-done((bf16[4,48,1536]{2,1,0:T(8,128)(2,1)S(1)}, bf16[4,48,1536]{2,1,0:T(8,128)(2,1)S(1)}, u32[]{:S(2)}, u32[]{:S(2)}) %collective-permute-start.19) | collective-permute-done | bytes 589856 | tf_op jit(solution)/shard_map/ppermute | solution.py:1000
  103.0 4.9 %up_gelu.3 = (bf16[768,1536]{1,0:T(8,128)(2,1)S(1)}, bf16[768,1536]{1,0:T(8,128)(2,1)S(1)}) custom-call(bf16[768,768]{1,0:T(8,128)(2,1)S(1)} %collective-permute-done.18.rows_ref.refs_1_, bf16[768,1536]{1,0:T(8,128)(2,1)S(1)} %get-tuple-element.146.weight_ref.refs_1_, f32[1,1536]{1,0:T(1,128)S(1)} %reshape.72.bias_ref), custom_call_target="tpu_custom_call" | custom-call | flops 1811939328 | bytes 8257536 | tf_op jit(solution)/shard_map/up_gelu/pallas_call | solution.py:477
  110.1 2.4 rows_product.11
  112.7 2.4 rows_product.10.down_ref
  115.4 3.9 %norm_two.1 = (bf16[768,768]{1,0:T(8,128)(2,1)}, f32[768,768]{1,0:T(8,128)S(1)}, bf16[768,768]{1,0:T(8,128)(2,1)S(1)}, f32[8,768]{1,0:T(8,128)S(1)}) custom-call(s32[1,2]{1,0:T(1,128)S(1)} %copy-done.2, f32[768,768]{1,0:T(8,128)S(1)} %rows_product.10.down_ref, bf16[768,768]{1,0:T(8,128)(2,1)S(1)} %collective-permute-done.21.other_ref, ...), custom_call_target="tpu_custom_call" | custom-call | flops 23592960 | bytes 11796480 | tf_op jit(solution)/shard_map/norm_two/pallas_call | solution.py:641
  119.6 2.6 %collective-permute-done.22.refs_1_.grad_ref = bf16[768,768]{1,0:T(8,128)(2,1)S(1)} collective-permute-done((bf16[768,768]{1,0:T(8,128)(2,1)S(1)}, bf16[768,768]{1,0:T(8,128)(2,1)S(1)}, u32[]{:S(2)}, u32[]{:S(2)}) %collective-permute-start.22) | collective-permute-done | bytes 1179680 | tf_op jit(solution)/shard_map/ppermute | solution.py:1012
  122.2 4.9 %outer.5.refs_0_ = bf16[768,1536]{1,0:T(8,128)(2,1)S(1)} custom-call(bf16[768,768]{1,0:T(8,128)(2,1)S(1)} %get-tuple-element.157.grad_ref.refs_0_, bf16[768,768]{1,0:T(8,128)(2,1)S(1)} %collective-permute-done.22.refs_1_.grad_ref, bf16[768,1536]{1,0:T(8,128)(2,1)S(1)} %get-tuple-element.152.refs_0_.refs_2_, ...), custom_call_target="tpu_custom_call" | custom-call | flops 3623878656 | bytes 7077888 | tf_op jit(solution)/shard_map/outer/pallas_call | solution.py:554
  127.8 2.9 %back_slope.3 = (bf16[768,1536]{1,0:T(8,128)(2,1)S(1)}, f32[8,1536]{1,0:T(8,128)S(1)}) custom-call(bf16[768,768]{1,0:T(8,128)(2,1)S(1)} %collective-permute-done.22.refs_1_.grad_ref, bf16[768,1536]{1,0:T(8,128)(2,1)S(1)} %place_pieces.5.refs_1_.weight_ref, bf16[768,1536]{1,0:T(8,128)(2,1)S(1)} %get-tuple-element.162.slope_ref), custom_call_target="tpu_custom_call" | custom-call | flops 1811939328 | bytes 8257536 | tf_op jit(solution)/shard_map/back_slope/pallas_call | solution.py:511
  134.1 2.9 %back_slope.2 = (bf16[768,1536]{1,0:T(8,128)(2,1)S(1)}, f32[8,1536]{1,0:T(8,128)S(1)}) custom-call(bf16[768,768]{1,0:T(8,128)(2,1)S(1)} %get-tuple-element.157.grad_ref.refs_0_, bf16[768,1536]{1,0:T(8,128)(2,1)S(1)} %place_pieces.5.refs_1_.weight_ref, bf16[768,1536]{1,0:T(8,128)(2,1)S(1)} %get-tuple-element.158.slope_ref), custom_call_target="tpu_custom_call" | custom-call | flops 1811939328 | bytes 8257536 | tf_op jit(solution)/shard_map/back_slope/pallas_call | solution.py:511
  137.1 2.4 rows_product.12.own_ref
  144.7 5.0 %outer.7.refs_1_ = bf16[768,1536]{1,0:T(8,128)(2,1)S(1)} custom-call(bf16[768,768]{1,0:T(8,128)(2,1)S(1)} %get-tuple-element.242.rows_ref.refs_0_, bf16[768,768]{1,0:T(8,128)(2,1)S(1)} %collective-permute-done.18.rows_ref.refs_1_, bf16[768,1536]{1,0:T(8,128)(2,1)S(1)} %get-tuple-element.159.refs_0_.refs_2_, ...), custom_call_target="tpu_custom_call" | custom-call | flops 3623878656 | bytes 7077888 | tf_op jit(solution)/shard_map/outer/pallas_call | solution.py:554
  152.0 3.2 %collective-permute-done.26.refs_1_ = bf16[192,1536]{1,0:T(8,128)(2,1)S(1)} collective-permute-done((bf16[192,1536]{1,0:T(8,128)(2,1)S(1)}, bf16[192,1536]{1,0:T(8,128)(2,1)S(1)}, u32[]{:S(2)}, u32[]{:S(2)}) %collective-permute-start.26) | collective-permute-done | bytes 589856 | tf_op jit(solution)/shard_map/ppermute | solution.py:1000
  157.9 23.5 %attend_backward.2 = (bf16[1536,768]{1,0:T(8,128)(2,1)S(1)}, f32[8,256]{1,0:T(8,128)S(1)}) custom-call(s32[1,2]{1,0:T(1,128)S(1)} %copy-done.2, s32[1,6,24,3]{3,2,1,0:T(8,128)S(1)} %copy.35.rb_ref, bf16[1536,1152]{1,0:T(8,128)(2,1)S(1)} %triple.1.tri_ref, bf16[1536,384]{1,0:T(8,128)(2,1)S(1)} %project_both.1.grad_ref), custom_call_target="tpu_custom_call" | custom-call | flops 16106127360 | bytes 7864320 | tf_op jit(solution)/shard_map/attend_backward/pallas_call | solution.py:414
  182.2 2.5 %outer.8.refs_0_ = bf16[768,768]{1,0:T(8,128)(2,1)S(1)} custom-call(bf16[768,768]{1,0:T(8,128)(2,1)S(1)} %copy-done, bf16[768,768]{1,0:T(8,128)(2,1)S(1)} %collective-permute-done.other_ref.refs_1_, bf16[1536,768]{1,0:T(8,128)(2,1)S(1)} %get-tuple-element.206.refs_2_.refs_0_), custom_call_target="tpu_custom_call" | custom-call | flops 1811939328 | bytes 4718592 | tf_op jit(solution)/shard_map/outer/pallas_call | solution.py:554
  187.3 3.2 %collective-permute-start.34 = (bf16[48,1536]{1,0:T(8,128)(2,1)S(1)}, bf16[48,1536]{1,0:T(8,128)(2,1)S(1)}, u32[]{:S(2)}, u32[]{:S(2)}) collective-permute-start(bf16[48,1536]{1,0:T(8,128)(2,1)S(1)} %get-tuple-element.183), channel_id=1, source_target_pairs={{0,24},{1,25},{2,26},{3,27},{4,28},{5,29},{6,30},{7,31},{8,16},{9,... | collective-permute-start | bytes 442376 | tf_op jit(solution)/shard_map/ppermute | solution.py:1000
  192.6 14.9 %attend_backward.3 = (bf16[1536,384]{1,0:T(8,128)(2,1)S(1)}, f32[8,128]{1,0:T(8,128)S(1)}) custom-call(s32[1,2]{1,0:T(1,128)S(1)} %copy-done.2, s32[1,6,24,3]{3,2,1,0:T(8,128)S(1)} %copy.35.rb_ref, bf16[1536,1152]{1,0:T(8,128)(2,1)S(1)} %triple.1.tri_ref, bf16[1536,384]{1,0:T(8,128)(2,1)S(1)} %project_both.1.grad_ref), custom_call_target="tpu_custom_call" | custom-call | flops 8053063680 | bytes 3932160 | tf_op jit(solution)/shard_map/attend_backward/pallas_call | solution.py:414
  214.6 3.6 %collective-permute-start.40 = (bf16[48,1920]{1,0:T(8,128)(2,1)S(1)}, bf16[48,1920]{1,0:T(8,128)(2,1)S(1)}, u32[]{:S(2)}, u32[]{:S(2)}) collective-permute-start(bf16[48,1920]{1,0:T(8,128)(2,1)S(1)} %get-tuple-element.200), channel_id=1, source_target_pairs={{0,16},{1,17},{2,18},{3,19},{4,20},{5,21},{6,22},{7,23},{8,24},{9,... | collective-permute-start | bytes 552968 | tf_op jit(solution)/shard_map/ppermute | solution.py:1000
  219.0 4.0 %collective-permute-done.37.refs_4_ = bf16[192,768]{1,0:T(8,128)(2,1)S(1)} collective-permute-done((bf16[192,768]{1,0:T(8,128)(2,1)S(1)}, bf16[192,768]{1,0:T(8,128)(2,1)S(1)}, u32[]{:S(2)}, u32[]{:S(2)}) %collective-permute-start.37) | collective-permute-done | bytes 294944 | tf_op jit(solution)/shard_map/ppermute | solution.py:1000
  224.8 3.1 %collective-permute-start.41 = (bf16[48,1920]{1,0:T(8,128)(2,1)S(1)}, bf16[48,1920]{1,0:T(8,128)(2,1)S(1)}, u32[]{:S(2)}, u32[]{:S(2)}) collective-permute-start(bf16[48,1920]{1,0:T(8,128)(2,1)S(1)} %get-tuple-element.219), channel_id=1, source_target_pairs={{0,24},{1,25},{2,26},{3,27},{4,28},{5,29},{6,30},{7,31},{8,16},{9,... | collective-permute-start | bytes 552968 | tf_op jit(solution)/shard_map/ppermute | solution.py:1000
  234.0 2.5 %collective-permute-start.44 = (bf16[60,1152]{1,0:T(8,128)(2,1)S(1)}, bf16[60,1152]{1,0:T(8,128)(2,1)S(1)}, u32[]{:S(2)}, u32[]{:S(2)}) collective-permute-start(bf16[60,1152]{1,0:T(8,128)(2,1)S(1)} %get-tuple-element.224), channel_id=1, source_target_pairs={{0,24},{1,25},{2,26},{3,27},{4,28},{5,29},{6,30},{7,31},{8,16},{9,... | collective-permute-start | bytes 414728 | tf_op jit(solution)/shard_map/ppermute | solution.py:1000
  239.1 6.7 %collective-permute-done.43.refs_2_ = bf16[60,1152]{1,0:T(8,128)(2,1)S(1)} collective-permute-done((bf16[60,1152]{1,0:T(8,128)(2,1)S(1)}, bf16[60,1152]{1,0:T(8,128)(2,1)S(1)}, u32[]{:S(2)}, u32[]{:S(2)}) %collective-permute-start.43) | collective-permute-done | bytes 138272 | tf_op jit(solution)/shard_map/ppermute | solution.py:1000
  (158 shorter events, 73.8 us)
Async XLA Ops:
  3.7 11.6 %collective-permute-start.2 = (bf16[144,384]{1,0:T(8,128)(2,1)}, bf16[144,384]{1,0:T(8,128)(2,1)S(1)}, u32[]{:S(2)}, u32[]{:S(2)}) collective-permute-start(bf16[144,384]{1,0:T(8,128)(2,1)} %bitcast.36), channel_id=1, source_target_pairs={{0,16},{1,17},{2,18},{3,19},{4,20},{5,21},{6,22},{7,23},{8,24},{9,... | collective-permute-start | bytes 331784 | tf_op jit(solution)/shard_map/ppermute | solution.py:1000
  6.3 46.6 %collective-permute-start = (bf16[768,768]{1,0:T(8,128)(2,1)}, bf16[768,768]{1,0:T(8,128)(2,1)S(1)}, u32[]{:S(2)}, u32[]{:S(2)}) collective-permute-start(bf16[768,768]{1,0:T(8,128)(2,1)} %refs_0_.3), channel_id=1, source_target_pairs={{0,1},{1,0},{2,3},{3,2},{4,5},{5,4},{6,7},{7,6},{8,9},{9,8},{10,11... | collective-permute-start | bytes 3538952 | tf_op jit(solution)/shard_map/ppermute | solution.py:1012
  16.3 20.9 %collective-permute-start.4 = (bf16[4,144,384]{2,1,0:T(8,128)(2,1)S(1)}, bf16[4,144,384]{2,1,0:T(8,128)(2,1)S(1)}, u32[]{:S(2)}, u32[]{:S(2)}) collective-permute-start(bf16[4,144,384]{2,1,0:T(8,128)(2,1)S(1)} %pad_maximum_fusion.2.refs_0_), channel_id=1, source_target_pairs={{0,2},{1,5},{2,0},{3,7},{4,6},{5,1},{6,4},{7,3},{8,10},{9,13},{10,... | collective-permute-start | bytes 1327112 | tf_op jit(solution)/shard_map/ppermute | solution.py:1000
  17.9 20.0 %collective-permute-start.5 = (bf16[4,144,384]{2,1,0:T(8,128)(2,1)S(1)}, bf16[4,144,384]{2,1,0:T(8,128)(2,1)S(1)}, u32[]{:S(2)}, u32[]{:S(2)}) collective-permute-start(bf16[4,144,384]{2,1,0:T(8,128)(2,1)S(1)} %pad_maximum_fusion.2.refs_0_), channel_id=1, source_target_pairs={{0,4},{1,3},{2,6},{3,1},{4,0},{5,7},{6,2},{7,5},{8,12},{9,11},{10,... | collective-permute-start | bytes 1327112 | tf_op jit(solution)/shard_map/ppermute | solution.py:1000
  22.2 15.0 %collective-permute-start.7 = (bf16[48,1920]{1,0:T(8,128)(2,1)S(1)}, bf16[48,1920]{1,0:T(8,128)(2,1)S(1)}, u32[]{:S(2)}, u32[]{:S(2)}) collective-permute-start(bf16[48,1920]{1,0:T(8,128)(2,1)S(1)} %constant_dynamic-update-slice_fusion), channel_id=1, source_target_pairs={{0,16},{1,17},{2,18},{3,19},{4,20},{5,21},{6,22},{7,23},{8,24},{9,... | collective-permute-start | bytes 552968 | tf_op jit(solution)/shard_map/ppermute | solution.py:1000
  47.1 24.3 %collective-permute-start.12 = (bf16[48,1536]{1,0:T(8,128)(2,1)S(1)}, bf16[48,1536]{1,0:T(8,128)(2,1)S(1)}, u32[]{:S(2)}, u32[]{:S(2)}) collective-permute-start(bf16[48,1536]{1,0:T(8,128)(2,1)S(1)} %copy-done.7), channel_id=1, source_target_pairs={{0,8},{1,9},{2,10},{3,11},{4,12},{5,13},{6,14},{7,15},{8,0},{9,1},... | collective-permute-start | bytes 442376 | tf_op jit(solution)/shard_map/ppermute | solution.py:1000
  49.8 21.6 %collective-permute-start.13 = (bf16[48,1536]{1,0:T(8,128)(2,1)S(1)}, bf16[48,1536]{1,0:T(8,128)(2,1)S(1)}, u32[]{:S(2)}, u32[]{:S(2)}) collective-permute-start(bf16[48,1536]{1,0:T(8,128)(2,1)S(1)} %copy-done.7), channel_id=1, source_target_pairs={{0,16},{1,17},{2,18},{3,19},{4,20},{5,21},{6,22},{7,23},{8,24},{9,... | collective-permute-start | bytes 442376 | tf_op jit(solution)/shard_map/ppermute | solution.py:1000
  50.8 20.6 %collective-permute-start.14 = (bf16[48,1536]{1,0:T(8,128)(2,1)S(1)}, bf16[48,1536]{1,0:T(8,128)(2,1)S(1)}, u32[]{:S(2)}, u32[]{:S(2)}) collective-permute-start(bf16[48,1536]{1,0:T(8,128)(2,1)S(1)} %copy-done.7), channel_id=1, source_target_pairs={{0,24},{1,25},{2,26},{3,27},{4,28},{5,29},{6,30},{7,31},{8,16},{9,... | collective-permute-start | bytes 442376 | tf_op jit(solution)/shard_map/ppermute | solution.py:1000
  52.4 19.0 %collective-permute-start.10 = (bf16[4,48,1920]{2,1,0:T(8,128)(2,1)S(1)}, bf16[4,48,1920]{2,1,0:T(8,128)(2,1)S(1)}, u32[]{:S(2)}, u32[]{:S(2)}) collective-permute-start(bf16[4,48,1920]{2,1,0:T(8,128)(2,1)S(1)} %pad_maximum_fusion.refs_0_), channel_id=1, source_target_pairs={{0,2},{1,5},{2,0},{3,7},{4,6},{5,1},{6,4},{7,3},{8,10},{9,13},{10,... | collective-permute-start | bytes 2211848 | tf_op jit(solution)/shard_map/ppermute | solution.py:1000
  53.0 18.4 %collective-permute-start.11 = (bf16[4,48,1920]{2,1,0:T(8,128)(2,1)S(1)}, bf16[4,48,1920]{2,1,0:T(8,128)(2,1)S(1)}, u32[]{:S(2)}, u32[]{:S(2)}) collective-permute-start(bf16[4,48,1920]{2,1,0:T(8,128)(2,1)S(1)} %pad_maximum_fusion.refs_0_), channel_id=1, source_target_pairs={{0,4},{1,3},{2,6},{3,1},{4,0},{5,7},{6,2},{7,5},{8,12},{9,11},{10,... | collective-permute-start | bytes 2211848 | tf_op jit(solution)/shard_map/ppermute | solution.py:1000
  71.4 14.9 %collective-permute-start.15 = (bf16[4,48,1920]{2,1,0:T(8,128)(2,1)S(1)}, bf16[4,48,1920]{2,1,0:T(8,128)(2,1)S(1)}, u32[]{:S(2)}, u32[]{:S(2)}) collective-permute-start(bf16[4,48,1920]{2,1,0:T(8,128)(2,1)S(1)} %collective-permute-done.10.refs_1_), channel_id=1, source_target_pairs={{0,4},{1,3},{2,6},{3,1},{4,0},{5,7},{6,2},{7,5},{8,12},{9,11},{10,... | collective-permute-start | bytes 2211848 | tf_op jit(solution)/shard_map/ppermute | solution.py:1000
  72.4 12.6 %collective-permute-start.16 = (bf16[4,48,1536]{2,1,0:T(8,128)(2,1)S(1)}, bf16[4,48,1536]{2,1,0:T(8,128)(2,1)S(1)}, u32[]{:S(2)}, u32[]{:S(2)}) collective-permute-start(bf16[4,48,1536]{2,1,0:T(8,128)(2,1)S(1)} %pad_maximum_fusion.1.refs_0_), channel_id=1, source_target_pairs={{0,2},{1,5},{2,0},{3,7},{4,6},{5,1},{6,4},{7,3},{8,10},{9,13},{10,... | collective-permute-start | bytes 1769480 | tf_op jit(solution)/shard_map/ppermute | solution.py:1000
  92.9 10.1 %collective-permute-start.18 = (bf16[768,768]{1,0:T(8,128)(2,1)S(1)}, bf16[768,768]{1,0:T(8,128)(2,1)S(1)}, u32[]{:S(2)}, u32[]{:S(2)}) collective-permute-start(bf16[768,768]{1,0:T(8,128)(2,1)S(1)} %get-tuple-element.242.rows_ref.refs_0_), channel_id=1, source_target_pairs={{0,1},{1,0},{2,3},{3,2},{4,5},{5,4},{6,7},{7,6},{8,9},{9,8},{10,11... | collective-permute-start | bytes 3538952 | tf_op jit(solution)/shard_map/ppermute | solution.py:1012
  93.1 9.9 %collective-permute-start.19 = (bf16[4,48,1536]{2,1,0:T(8,128)(2,1)S(1)}, bf16[4,48,1536]{2,1,0:T(8,128)(2,1)S(1)}, u32[]{:S(2)}, u32[]{:S(2)}) collective-permute-start(bf16[4,48,1536]{2,1,0:T(8,128)(2,1)S(1)} %collective-permute-done.16.refs_1_), channel_id=1, source_target_pairs={{0,4},{1,3},{2,6},{3,1},{4,0},{5,7},{6,2},{7,5},{8,12},{9,11},{10,... | collective-permute-start | bytes 1769480 | tf_op jit(solution)/shard_map/ppermute | solution.py:1000
  94.0 15.4 %collective-permute-start.20 = (bf16[4,48,1536]{2,1,0:T(8,128)(2,1)S(1)}, bf16[4,48,1536]{2,1,0:T(8,128)(2,1)S(1)}, u32[]{:S(2)}, u32[]{:S(2)}) collective-permute-start(bf16[4,48,1536]{2,1,0:T(8,128)(2,1)S(1)} %pad_maximum_fusion.1.refs_0_), channel_id=1, source_target_pairs={{0,4},{1,3},{2,6},{3,1},{4,0},{5,7},{6,2},{7,5},{8,12},{9,11},{10,... | collective-permute-start | bytes 1769480 | tf_op jit(solution)/shard_map/ppermute | solution.py:1000
  133.4 9.9 %collective-permute-start.24 = (bf16[192,1536]{1,0:T(8,128)(2,1)S(1)}, bf16[192,1536]{1,0:T(8,128)(2,1)S(1)}, u32[]{:S(2)}, u32[]{:S(2)}) collective-permute-start(bf16[192,1536]{1,0:T(8,128)(2,1)S(1)} %get-tuple-element.166), channel_id=1, source_target_pairs={{0,2},{1,5},{2,0},{3,7},{4,6},{5,1},{6,4},{7,3},{8,10},{9,13},{10,... | collective-permute-start | bytes 1769480 | tf_op jit(solution)/shard_map/ppermute | solution.py:1000
  144.1 11.1 %collective-permute-start.26 = (bf16[192,1536]{1,0:T(8,128)(2,1)S(1)}, bf16[192,1536]{1,0:T(8,128)(2,1)S(1)}, u32[]{:S(2)}, u32[]{:S(2)}) collective-permute-start(bf16[192,1536]{1,0:T(8,128)(2,1)S(1)} %get-tuple-element.170), channel_id=1, source_target_pairs={{0,2},{1,5},{2,0},{3,7},{4,6},{5,1},{6,4},{7,3},{8,10},{9,13},{10,... | collective-permute-start | bytes 1769480 | tf_op jit(solution)/shard_map/ppermute | solution.py:1000
  149.7 31.8 %collective-permute-start.28 = (bf16[192,1536]{1,0:T(8,128)(2,1)S(1)}, bf16[192,1536]{1,0:T(8,128)(2,1)S(1)}, u32[]{:S(2)}, u32[]{:S(2)}) collective-permute-start(bf16[192,1536]{1,0:T(8,128)(2,1)S(1)} %sum_second.4), channel_id=1, source_target_pairs={{0,4},{1,3},{2,6},{3,1},{4,0},{5,7},{6,2},{7,5},{8,12},{9,11},{10,... | collective-permute-start | bytes 1769480 | tf_op jit(solution)/shard_map/ppermute | solution.py:1000
  150.5 30.9 %collective-permute-start.29 = (f32[16,768]{1,0:T(8,128)S(1)}, f32[16,768]{1,0:T(8,128)S(1)}, u32[]{:S(2)}, u32[]{:S(2)}) collective-permute-start(f32[16,768]{1,0:T(8,128)S(1)} %constant_dynamic-update-slice_fusion.2.own_ref), channel_id=1, source_target_pairs={{0,1},{1,0},{2,3},{3,2},{4,5},{5,4},{6,7},{7,6},{8,9},{9,8},{10,11... | collective-permute-start | bytes 147464 | tf_op jit(solution)/shard_map/ppermute | solution.py:1012
  157.3 24.2 %collective-permute-start.27 = (bf16[384,1920]{1,0:T(8,128)(2,1)S(1)}, bf16[384,1920]{1,0:T(8,128)(2,1)S(1)}, u32[]{:S(2)}, u32[]{:S(2)}) collective-permute-start(bf16[384,1920]{1,0:T(8,128)(2,1)S(1)} %sum_first.5), channel_id=1, source_target_pairs={{0,2},{1,5},{2,0},{3,7},{4,6},{5,1},{6,4},{7,3},{8,10},{9,13},{10,... | collective-permute-start | bytes 4423688 | tf_op jit(solution)/shard_map/ppermute | solution.py:1000
  186.1 21.5 %collective-permute-start.32 = (bf16[48,1536]{1,0:T(8,128)(2,1)S(1)}, bf16[48,1536]{1,0:T(8,128)(2,1)S(1)}, u32[]{:S(2)}, u32[]{:S(2)}) collective-permute-start(bf16[48,1536]{1,0:T(8,128)(2,1)S(1)} %get-tuple-element.181), channel_id=1, source_target_pairs={{0,8},{1,9},{2,10},{3,11},{4,12},{5,13},{6,14},{7,15},{8,0},{9,1},... | collective-permute-start | bytes 442376 | tf_op jit(solution)/shard_map/ppermute | solution.py:1000
  186.2 21.4 %collective-permute-start.33 = (bf16[48,1536]{1,0:T(8,128)(2,1)S(1)}, bf16[48,1536]{1,0:T(8,128)(2,1)S(1)}, u32[]{:S(2)}, u32[]{:S(2)}) collective-permute-start(bf16[48,1536]{1,0:T(8,128)(2,1)S(1)} %get-tuple-element.182), channel_id=1, source_target_pairs={{0,16},{1,17},{2,18},{3,19},{4,20},{5,21},{6,22},{7,23},{8,24},{9,... | collective-permute-start | bytes 442376 | tf_op jit(solution)/shard_map/ppermute | solution.py:1000
  187.3 20.3 %collective-permute-start.34 = (bf16[48,1536]{1,0:T(8,128)(2,1)S(1)}, bf16[48,1536]{1,0:T(8,128)(2,1)S(1)}, u32[]{:S(2)}, u32[]{:S(2)}) collective-permute-start(bf16[48,1536]{1,0:T(8,128)(2,1)S(1)} %get-tuple-element.183), channel_id=1, source_target_pairs={{0,24},{1,25},{2,26},{3,27},{4,28},{5,29},{6,30},{7,31},{8,16},{9,... | collective-permute-start | bytes 442376 | tf_op jit(solution)/shard_map/ppermute | solution.py:1000
  190.5 17.1 %collective-permute-start.31 = (bf16[192,1920]{1,0:T(8,128)(2,1)S(1)}, bf16[192,1920]{1,0:T(8,128)(2,1)S(1)}, u32[]{:S(2)}, u32[]{:S(2)}) collective-permute-start(bf16[192,1920]{1,0:T(8,128)(2,1)S(1)} %sum_second.5), channel_id=1, source_target_pairs={{0,4},{1,3},{2,6},{3,1},{4,0},{5,7},{6,2},{7,5},{8,12},{9,11},{10,... | collective-permute-start | bytes 2211848 | tf_op jit(solution)/shard_map/ppermute | solution.py:1000
  191.1 16.5 %collective-permute-start.30 = (bf16[384,768]{1,0:T(8,128)(2,1)S(1)}, bf16[384,768]{1,0:T(8,128)(2,1)S(1)}, u32[]{:S(2)}, u32[]{:S(2)}) collective-permute-start(bf16[384,768]{1,0:T(8,128)(2,1)S(1)} %sum_first.6), channel_id=1, source_target_pairs={{0,2},{1,5},{2,0},{3,7},{4,6},{5,1},{6,4},{7,3},{8,10},{9,13},{10,... | collective-permute-start | bytes 1769480 | tf_op jit(solution)/shard_map/ppermute | solution.py:1000
  213.2 10.2 %collective-permute-start.35 = (bf16[768,768]{1,0:T(8,128)(2,1)S(1)}, bf16[768,768]{1,0:T(8,128)(2,1)S(1)}, u32[]{:S(2)}, u32[]{:S(2)}) collective-permute-start(bf16[768,768]{1,0:T(8,128)(2,1)S(1)} %rows_product.14), channel_id=1, source_target_pairs={{0,1},{1,0},{2,3},{3,2},{4,5},{5,4},{6,7},{7,6},{8,9},{9,8},{10,11... | collective-permute-start | bytes 3538952 | tf_op jit(solution)/shard_map/ppermute | solution.py:1012
  213.2 10.2 %collective-permute-start.36 = (bf16[420,384]{1,0:T(8,128)(2,1)S(1)}, bf16[420,384]{1,0:T(8,128)(2,1)S(1)}, u32[]{:S(2)}, u32[]{:S(2)}) collective-permute-start(bf16[420,384]{1,0:T(8,128)(2,1)S(1)} %sum_first.7), channel_id=1, source_target_pairs={{0,2},{1,5},{2,0},{3,7},{4,6},{5,1},{6,4},{7,3},{8,10},{9,13},{10,... | collective-permute-start | bytes 967688 | tf_op jit(solution)/shard_map/ppermute | solution.py:1000
  214.6 19.4 %collective-permute-start.39 = (bf16[48,1920]{1,0:T(8,128)(2,1)S(1)}, bf16[48,1920]{1,0:T(8,128)(2,1)S(1)}, u32[]{:S(2)}, u32[]{:S(2)}) collective-permute-start(bf16[48,1920]{1,0:T(8,128)(2,1)S(1)} %get-tuple-element.199), channel_id=1, source_target_pairs={{0,8},{1,9},{2,10},{3,11},{4,12},{5,13},{6,14},{7,15},{8,0},{9,1},... | collective-permute-start | bytes 552968 | tf_op jit(solution)/shard_map/ppermute | solution.py:1000
  214.6 21.9 %collective-permute-start.40 = (bf16[48,1920]{1,0:T(8,128)(2,1)S(1)}, bf16[48,1920]{1,0:T(8,128)(2,1)S(1)}, u32[]{:S(2)}, u32[]{:S(2)}) collective-permute-start(bf16[48,1920]{1,0:T(8,128)(2,1)S(1)} %get-tuple-element.200), channel_id=1, source_target_pairs={{0,16},{1,17},{2,18},{3,19},{4,20},{5,21},{6,22},{7,23},{8,24},{9,... | collective-permute-start | bytes 552968 | tf_op jit(solution)/shard_map/ppermute | solution.py:1000
  224.8 11.8 %collective-permute-start.41 = (bf16[48,1920]{1,0:T(8,128)(2,1)S(1)}, bf16[48,1920]{1,0:T(8,128)(2,1)S(1)}, u32[]{:S(2)}, u32[]{:S(2)}) collective-permute-start(bf16[48,1920]{1,0:T(8,128)(2,1)S(1)} %get-tuple-element.219), channel_id=1, source_target_pairs={{0,24},{1,25},{2,26},{3,27},{4,28},{5,29},{6,30},{7,31},{8,16},{9,... | collective-permute-start | bytes 552968 | tf_op jit(solution)/shard_map/ppermute | solution.py:1000
  232.2 13.6 %collective-permute-start.43 = (bf16[60,1152]{1,0:T(8,128)(2,1)S(1)}, bf16[60,1152]{1,0:T(8,128)(2,1)S(1)}, u32[]{:S(2)}, u32[]{:S(2)}) collective-permute-start(bf16[60,1152]{1,0:T(8,128)(2,1)S(1)} %get-tuple-element.223), channel_id=1, source_target_pairs={{0,16},{1,17},{2,18},{3,19},{4,20},{5,21},{6,22},{7,23},{8,24},{9,... | collective-permute-start | bytes 414728 | tf_op jit(solution)/shard_map/ppermute | solution.py:1000
  234.0 11.8 %collective-permute-start.44 = (bf16[60,1152]{1,0:T(8,128)(2,1)S(1)}, bf16[60,1152]{1,0:T(8,128)(2,1)S(1)}, u32[]{:S(2)}, u32[]{:S(2)}) collective-permute-start(bf16[60,1152]{1,0:T(8,128)(2,1)S(1)} %get-tuple-element.224), channel_id=1, source_target_pairs={{0,24},{1,25},{2,26},{3,27},{4,28},{5,29},{6,30},{7,31},{8,16},{9,... | collective-permute-start | bytes 414728 | tf_op jit(solution)/shard_map/ppermute | solution.py:1000
  (28 other events, 179.0 us)
